TPU v7x, 32 devices: a whole 2x2x4 slice. The times are simulated.
32 devices in a mesh: run: 8 (over z, core), mz: 4 (over y, x).
Axes of the slice: x: 2, y: 2, z: 4, core: 2. Of those that a mesh axis runs over, the one named last changes fastest.
Arguments:
- lcms: bfloat16 [512, 256, 4096], P('run', None, 'mz'), may hold values from -600 to 600
- spectra: float32 [512, 65536], P('run', 'mz'), may hold values from -200 to 200
- scan_factor: float32 [64, 256], replicated, may hold values from 0.05 to 0.9
- mz_factor: float32 [64, 4096], P(None, 'mz'), may hold values from 0 to 1.7
- ppm_factor: float32 [64, 65536], P(None, 'mz'), may hold values from 0 to 1.7
Outputs:
- sample_factor: float32 [512, 64], P('run')
- ppm_new: float32 [64, 65536], P(None, ('mz', 'run'))
All inputs are finite; a program needn't handle non-finite values.
Results may differ from a plain program's by a relative error of at most 0.0048.
Values sent between devices are 32-bit elements; how exact they have to be, the bound alone decides.
No kernel may reach another device: no remote copies, remote signals or barrier semaphores. Data moves between devices by JAX's collectives and lax.ppermute only.
A program may use at most 128 MiB of HBM per device.

v0:
```python
import jax
import jax.numpy as jnp
from jax import lax
from jax.sharding import PartitionSpec as P


def solve_rows(gram_matrix, right_rows):
    lower_factor = jnp.linalg.cholesky(gram_matrix)
    return jax.scipy.linalg.cho_solve((lower_factor, True), right_rows.T).T


def per_device(lcms, spectra, scan_factor, mz_factor, ppm_factor):
    highest = lax.Precision.HIGHEST
    shared_spectra = lax.all_to_all(spectra, "run", split_axis=1, concat_axis=0, tiled=True)
    scan_bf = scan_factor.astype(jnp.bfloat16)
    tensor = jnp.einsum("ijk,rj->irk", lcms, scan_bf, preferred_element_type=jnp.float32)
    lcms_local = jnp.sum(tensor * mz_factor[None], axis=2)
    nmr_local = lax.dot_general(spectra, ppm_factor, (((1,), (1,)), ((), ())), precision=highest)
    mz_local = jnp.dot(mz_factor, mz_factor.T, precision=highest)
    ppm_local = jnp.dot(ppm_factor, ppm_factor.T, precision=highest)
    mz_gram, ppm_gram = lax.psum((mz_local, ppm_local), "mz")
    lcms_part, nmr_part = lax.psum((lcms_local, nmr_local), "mz")
    lcms_gram = jnp.dot(scan_factor, scan_factor.T, precision=highest) * mz_gram
    sample_first = solve_rows(lcms_gram + ppm_gram, lcms_part + nmr_part)
    whole_rows = lax.all_gather(sample_first, "run", axis=0, tiled=True)
    sample_gram = lax.psum(jnp.dot(sample_first.T, sample_first, precision=highest), "run")
    projected = jnp.dot(whole_rows.T, shared_spectra, precision=highest)
    ppm_new = jax.scipy.linalg.cho_solve((jnp.linalg.cholesky(sample_gram), True), projected)
    gram_local = jnp.dot(ppm_new, ppm_new.T, precision=highest)
    new_gram = lax.psum(gram_local, ("run", "mz"))
    fit_local = lax.dot_general(
        shared_spectra, ppm_new, (((1,), (1,)), ((), ())), precision=highest
    )
    fit_owned = lax.psum_scatter(fit_local, "run", scatter_dimension=0, tiled=True)
    nmr_fit = lax.psum(fit_owned, "mz")
    sample_factor = solve_rows(lcms_gram + new_gram, lcms_part + nmr_fit)
    return (sample_factor, ppm_new)


def solution(mesh):
    return jax.shard_map(
        per_device,
        mesh=mesh,
        in_specs=(P("run", None, "mz"), P("run", "mz"), P(), P(None, "mz"), P(None, "mz")),
        out_specs=(P("run", None), P(None, ("mz", "run"))),
        check_vma=False,
    )
```

profile of v0, /device:TPU:0, one launch (start us, length us, event | category | flops | bytes accessed | tf_op | source)
XLA Modules:
  0.0 250.2 jit_solution(10968291417373203832)
XLA Ops:
  7.2 4.7 %copy.56 = f32[8,8,8,2048]{3,2,0,1:T(8,128)} copy(f32[8,8,8,2048]{3,2,1,0:T(8,128)} %bitcast.76) | data formatting | bytes 8388608 | tf_op jit(solution)/shard_map/all_to_all | solution.py:14
  11.8 0.0 copy-start.2
  11.8 6.5 %all-to-all-start = ((f32[64,8,2048]{2,0,1:T(8,128)}), f32[64,8,2048]{2,0,1:T(8,128)}, u32[]{:S(2)}, u32[]{:S(2)}) async-start(f32[64,8,2048]{2,0,1:T(8,128)} %bitcast.77), calls=%async_computation | async-start | bytes 8388608 | tf_op jit(solution)/shard_map/all_to_all | solution.py:14
  18.3 0.0 all-reduce.3.cloned.1.call-start
  18.4 0.0 copy-done.2
  18.4 1.0 fusion.28
  19.3 0.0 copy-start
  19.3 7.7 %fusion.30 = f32[64,64]{1,0:T(8,128)} fusion(f32[64,16384]{1,0:T(8,128)} %param.9, f32[64,16384]{1,0:T(8,128)} %param.12), kind=kOutput, calls=%fused_computation.47 | convolution fusion | flops 805306368 | bytes 8404992 | tf_op jit(solution)/shard_map/dot_general | solution.py:18
  27.0 0.0 copy-done
  27.0 0.0 copy-start.3
  27.0 4.0 %fusion.29 = f32[64,64]{0,1:T(8,128)} fusion(f32[64,16384]{1,0:T(8,128)S(1)} %copy-done), kind=kOutput, calls=%fused_computation.46 | convolution fusion | flops 805306368 | bytes 4210688 | tf_op jit(solution)/shard_map/dot_general | solution.py:20
  31.0 0.0 copy-done.3
  31.0 17.2 %multiply_reduce_fusion = f32[64,64]{0,1:T(8,128)} fusion(bf16[64,256,1024]{2,1,0:T(8,128)(2,1)} %param.8, f32[64,1024]{1,0:T(8,128)S(1)} %copy-done.2, f32[64,256]{1,0:T(8,128)S(1)} %copy-done.3), kind=kOutput, calls=%fused_computation | convolution fusion | flops 2155884544 | bytes 33898496 | tf_op jit(solution)/shard_map/ijk,rj->irk/dot_general | solution.py:16
  48.2 0.0 all-reduce.3.cloned.1.call-update
  48.2 0.2 reduce-scatter.2.cloned.1.call-start
  48.4 44.0 %all-reduce.3.cloned.1.call-done = (f32[64,64]{0,1:T(8,128)}, f32[64,64]{0,1:T(8,128)}, f32[64,64]{1,0:T(8,128)}, f32[64,64]{1,0:T(8,128)}) async-done(((f32[64,64]{0,1:T(8,128)}, f32[64,64]{0,1:T(8,128)}, f32[64,64]{1,0:T(8,128)}, f32[64,64]{1,0:T(8,128)}), (f32[64,64]{0,1:T(8,128)}, f32[64,64]{0,1:T(8,128)}, f32[64,64]{1,0:T(8,128)}, f32[64,64]{1,0:T(8,128)})) %all-reduce.3.cloned.1.call-update) | async-done | bytes 65552 | tf_op jit(solution)/shard_map/psum | solution.py:21
  92.4 1.0 fusion.27
  93.4 0.1 copy.39
  93.5 5.8 %cholesky.59 = f32[64,64]{1,0:T(8,128)S(1)} custom-call(f32[64,64]{1,0:T(8,128)S(1)} %fusion.19), custom_call_target="Cholesky" | custom-call | tf_op jit(solution)/shard_map/jit(cholesky)/cholesky | solution.py:8
  99.4 0.6 compare_reduce_fusion.2
  100.0 0.7 fusion
  100.7 4.9 %custom-call.16 = f32[1,64,64]{1,2,0:T(8,128)S(1)} custom-call(f32[1,64,64]{2,1,0:T(8,128)S(1)} %fusion), custom_call_target="InvertDiagBlocksLowerTriangular" | custom-call | tf_op jit(solution)/shard_map/jit(_cho_solve)/triangular_solve | solution.py:9
  105.6 1.0 fusion.13
  106.6 0.2 fusion.16
  106.8 0.1 copy.42
  106.9 0.2 fusion.31
  107.1 28.0 %psum.53 = f32[64,64]{0,1:T(8,128)S(1)} all-reduce(f32[64,64]{0,1:T(8,128)S(1)} %fusion.31), channel_id=1, replica_groups=mesh['run'=8,'mz'=4] {'run'}, use_global_device_ids=true, to_apply=%region_7.10 | all-reduce | flops 4096 | bytes 32768 | tf_op jit(solution)/shard_map/psum | solution.py:26
  135.1 0.1 copy.41
  135.2 5.8 %cholesky.70 = f32[64,64]{1,0:T(8,128)S(1)} custom-call(f32[64,64]{1,0:T(8,128)S(1)} %fusion.12), custom_call_target="Cholesky" | custom-call | tf_op jit(solution)/shard_map/jit(cholesky)/cholesky | solution.py:28
  141.1 0.6 compare_reduce_fusion.1
  141.7 0.7 fusion.1
  142.4 4.9 %custom-call.14 = f32[1,64,64]{1,2,0:T(8,128)S(1)} custom-call(f32[1,64,64]{2,1,0:T(8,128)S(1)} %fusion.1), custom_call_target="InvertDiagBlocksLowerTriangular" | custom-call | tf_op jit(solution)/shard_map/jit(_cho_solve)/triangular_solve | solution.py:28
  147.3 14.2 %all_gather.3 = f32[512,64]{1,0:T(8,128)S(1)} all-gather(f32[64,64]{1,0:T(8,128)S(1)} %copy.42), channel_id=1, replica_groups=mesh['run'=8,'mz'=4] {'run'}, dimensions={0}, use_global_device_ids=true | all-gather | bytes 147456 | tf_op jit(solution)/shard_map/all_gather | solution.py:25
  161.5 0.0 all-to-all-done
  161.5 4.8 %fusion.32 = f32[64,2048]{1,0:T(8,128)S(1)} fusion(f32[512,64]{1,0:T(8,128)S(1)} %all_gather.3, f32[512,2048]{1,0:T(8,128)} %bitcast.11), kind=kOutput, calls=%fused_computation.49 | convolution fusion | flops 805306368 | bytes 4849664 | tf_op jit(solution)/shard_map/dot_general | solution.py:27
  166.3 0.6 fusion.10
  166.9 0.0 copy-start.4
  166.9 0.6 fusion.8
  167.5 0.0 copy-start.1
  167.5 6.5 %convolution_bitcast_fusion = f32[512,64]{1,0:T(8,128)} fusion(f32[64,2048]{1,0:T(8,128)S(1)} %fusion.8, f32[512,2048]{1,0:T(8,128)} %bitcast.11), kind=kOutput, calls=%fused_computation.2 | convolution fusion | flops 805306368 | bytes 4849664 | tf_op jit(solution)/shard_map/dot_general | solution.py:31
  174.0 0.6 fusion.33
  174.6 0.0 reduce-scatter.2.cloned.1.call-update
  174.6 37.8 %psum.54 = f32[64,64]{0,1:T(8,128)S(1)} all-reduce(f32[64,64]{0,1:T(8,128)S(1)} %fusion.33), channel_id=1, replica_groups=mesh['run'=8,'mz'=4] {'run','mz'}, use_global_device_ids=true, to_apply=%region_8.11 | all-reduce | flops 4096 | bytes 32768 | tf_op jit(solution)/shard_map/psum | solution.py:30
  212.4 0.1 copy.45
  212.5 5.8 %cholesky.81 = f32[64,64]{1,0:T(8,128)S(1)} custom-call(f32[64,64]{1,0:T(8,128)S(1)} %fusion.7), custom_call_target="Cholesky" | custom-call | tf_op jit(solution)/shard_map/jit(cholesky)/cholesky | solution.py:8
  218.4 0.6 compare_reduce_fusion
  219.0 0.7 fusion.2
  219.7 4.9 %custom-call.17 = f32[1,64,64]{1,2,0:T(8,128)S(1)} custom-call(f32[1,64,64]{2,1,0:T(8,128)S(1)} %fusion.2), custom_call_target="InvertDiagBlocksLowerTriangular" | custom-call | tf_op jit(solution)/shard_map/jit(_cho_solve)/triangular_solve | solution.py:9
  224.6 0.0 reduce-scatter.2.cloned.1.call-done
  224.6 17.7 %psum.55 = f32[64,64]{1,0:T(8,128)S(1)} all-reduce(f32[64,64]{1,0:T(8,128)} %reduce-scatter.2.cloned.1.call-done), channel_id=1, replica_groups=mesh['run'=8,'mz'=4] {'mz'}, use_global_device_ids=true, to_apply=%region_10.13 | all-reduce | flops 4096 | bytes 32768 | tf_op jit(solution)/shard_map/psum | solution.py:35
  242.3 0.0 copy-done.4
  242.3 0.2 fusion.3
  242.5 0.2 convolution_bitcast_fusion.1
  242.7 0.7 copy.47
  243.4 0.0 copy-done.1
  (7 shorter events, 0.1 us)
Async XLA Ops:
  11.8 6.5 %copy-start.2 = (f32[64,1024]{1,0:T(8,128)S(1)}, f32[64,1024]{1,0:T(8,128)}, u32[]{:S(2)}) copy-start(f32[64,1024]{1,0:T(8,128)} %param.11) | copy-start | bytes 786436
  11.8 149.6 %all-to-all-start = ((f32[64,8,2048]{2,0,1:T(8,128)}), f32[64,8,2048]{2,0,1:T(8,128)}, u32[]{:S(2)}, u32[]{:S(2)}) async-start(f32[64,8,2048]{2,0,1:T(8,128)} %bitcast.77), calls=%async_computation | async-start | bytes 8388608 | tf_op jit(solution)/shard_map/all_to_all | solution.py:14
  18.3 74.1 %all-reduce.3.cloned.1.call-start = ((), (), s32[]{:S(2)}) async-start(), calls=%async_computation.3 | async-start | bytes 262144 | tf_op jit(solution)/shard_map/psum | solution.py:21
  19.3 7.7 %copy-start = (f32[64,16384]{1,0:T(8,128)S(1)}, f32[64,16384]{1,0:T(8,128)}, u32[]{:S(2)}) copy-start(f32[64,16384]{1,0:T(8,128)} %param.12) | copy-start | bytes 12582916
  27.0 4.0 %copy-start.3 = (f32[64,256]{1,0:T(8,128)S(1)}, f32[64,256]{1,0:T(8,128)}, u32[]{:S(2)}) copy-start(f32[64,256]{1,0:T(8,128)} %param.10) | copy-start | bytes 196612
  48.2 176.4 %reduce-scatter.2.cloned.1.call-start = ((), (), s32[]{:S(2)}) async-start(), calls=%async_computation.2 | async-start | bytes 294912 | tf_op jit(solution)/shard_map/reduce_scatter | solution.py:34
  166.9 75.4 %copy-start.4 = (f32[64,64]{1,0:T(8,128)S(1)}, f32[64,64]{1,0:T(8,128)}, u32[]{:S(2)}) copy-start(f32[64,64]{1,0:T(8,128)} %get-tuple-element.14) | copy-start | bytes 49156
  167.5 75.9 %copy-start.1 = (f32[64,2048]{1,0:T(8,128)}, f32[64,2048]{1,0:T(8,128)S(1)}, u32[]{:S(2)}) copy-start(f32[64,2048]{1,0:T(8,128)S(1)} %fusion.8) | copy-start | bytes 1572868
Sparse Core Ops, SparseCore 0:
  48.3 44.0 all-reduce.2
  174.7 28.0 reduce-scatter.1
where the time goes:
time: 251 us; the launch traced here: 250 us
  blocking collectives  97.7 us (39%)
  matrix products  45.6 us (18%)
  waiting for transfers between devices  44.1 us (18%)
  other arithmetic  36.2 us (14%)
  between operations  14.2 us (6%)
  starting transfers between devices  6.74 us (3%)
  local copies, waits for them, and re-layouts  5.68 us (2%)
    psum x1, waiting for transfers between devices, per_device(): mz_gram, ppm_gram = lax.psum((mz_local, ppm_local), 'mz')  44 us
    psum x1, blocking collectives, per_device(): new_gram = lax.psum(gram_local, ('run', 'mz'))  37.8 us
    psum x1, blocking collectives, per_device(): lax.psum(jnp.dot(sample_first.T, sample_first, precision=highest), 'run')  28 us
    psum x1, blocking collectives, per_device(): nmr_fit = lax.psum(fit_owned, 'mz')  17.7 us
    dot_general x1, matrix products, per_device(): jnp.einsum('ijk,rj->irk', lcms, scan_bf, preferred_element_type=jnp.float32)  17.2 us
    all_gather x1, blocking collectives, per_device(): whole_rows = lax.all_gather(sample_first, 'run', axis=0, tiled=True)  14.2 us
    another operation x6, other arithmetic, solve_rows(): lower_factor = jnp.linalg.cholesky(gram_matrix)  13 us
    another operation x4, other arithmetic, solve_rows(): return jax.scipy.linalg.cho_solve((lower_factor, True), right_rows.T).T  11.1 us
  transfers between devices with their start and end apart: 3, of which 1 were waited for; matrix products, arithmetic and copies ran while one was open for 27% of the time, Pallas kernels for 0%

commit v1 on v0

v1 whole, which is shorter than its diff:
```python
import functools

import jax
import jax.numpy as jnp
from jax import lax
from jax.experimental import pallas as pl
from jax.experimental.pallas import tpu as pltpu
from jax.sharding import PartitionSpec as P


F32, BF16 = jnp.float32, jnp.bfloat16
HIGHEST = lax.Precision.HIGHEST
NT = (((1,), (1,)), ((), ()))


def split(values):
    high = values.astype(BF16)
    return high, (values - high.astype(F32)).astype(BF16)


def stack_split(blocks):
    pairs = [split(block) for block in blocks]
    return jnp.concatenate([pair[0] for pair in pairs] + [pair[1] for pair in pairs], axis=0)


def cost(flops, transferred):
    return pl.CostEstimate(flops=int(flops), bytes_accessed=int(transferred), transcendentals=0)


def whole(shape):
    return pl.BlockSpec(shape, lambda *_: (0,) * len(shape))


def nmr_body(blocks, core_ref, *refs):
    spectra_refs, ppm_refs = refs[: 2 * blocks], refs[2 * blocks : 4 * blocks]
    mz_ref, part_ref, keep_ref, send_ref, total = refs[4 * blocks :]
    piece = pl.program_id(0)
    rank = mz_ref.shape[0]

    @pl.when(piece == 0)
    def _():
        total[...] = jnp.zeros_like(total)
        channels = stack_split([mz_ref[...]])
        products = lax.dot_general(channels, channels, NT, preferred_element_type=F32)
        rows = products[:rank] + products[rank:]
        gram = rows[:, :rank] + rows[:, rank:]
        part_ref[rank:, :] = jnp.concatenate([gram, gram], axis=1)

    for core in (0, 1):
        even = jnp.concatenate([spectra_refs[2 * b + core][...] for b in range(blocks)], axis=1)
        positions = stack_split(
            [jnp.concatenate([ppm_refs[2 * b + core][...] for b in range(blocks)], axis=1)]
        )
        left = jnp.concatenate([stack_split([even]), positions], axis=0)
        total[...] += lax.dot_general(left, positions, NT, preferred_element_type=F32)

        @pl.when(core_ref[0] == core)
        def _():
            keep_ref[0] = even

        @pl.when(core_ref[0] != core)
        def _():
            send_ref[0] = even

    @pl.when(piece == pl.num_programs(0) - 1)
    def _():
        samples = spectra_refs[0].shape[0]
        products = total[...]
        fit = products[:samples] + products[samples : 2 * samples]
        gram = products[2 * samples : 2 * samples + rank] + products[2 * samples + rank :]
        part_ref[:rank, :] = jnp.concatenate(
            [fit[:, :rank] + fit[:, rank:], gram[:, :rank] + gram[:, rank:]], axis=1
        )


def nmr_pass(core, spectra, ppm_factor, mz_factor, blocks, pieces):
    samples, positions = spectra.shape
    rank, channels = mz_factor.shape
    width = positions // (2 * blocks * pieces)

    def columns(rows):
        return [
            pl.BlockSpec((rows, width), functools.partial(lambda b, k, c: (0, b * pieces + k), b))
            for b in range(2 * blocks)
        ]

    sorted_shape = jax.ShapeDtypeStruct((pieces, samples, blocks * width), F32)
    return pl.pallas_call(
        functools.partial(nmr_body, blocks),
        name="nmr_pass",
        grid_spec=pltpu.PrefetchScalarGridSpec(
            num_scalar_prefetch=1,
            grid=(pieces,),
            in_specs=columns(samples) + columns(rank) + [whole((rank, channels))],
            out_specs=[whole((2 * rank, 2 * rank))]
            + [pl.BlockSpec((1, samples, blocks * width), lambda k, c: (k, 0, 0))] * 2,
            scratch_shapes=[pltpu.VMEM((2 * samples + 2 * rank, 2 * rank), F32)],
        ),
        out_shape=[jax.ShapeDtypeStruct((2 * rank, 2 * rank), F32), sorted_shape, sorted_shape],
        cost_estimate=cost(2 * 256 * 256 * positions, 4 * 3 * 64 * positions),
    )(core, *([spectra] * (2 * blocks)), *([ppm_factor] * (2 * blocks)), mz_factor)


def lcms_body(lcms_ref, scan_ref, mz_ref, out_ref, weights, scans):
    rank = mz_ref.shape[0]

    @pl.when(pl.program_id(0) == 0)
    def _():
        channels = mz_ref[...].T
        high, low = split(channels)
        weights[...] = jnp.concatenate([high, low], axis=1)
        scan = scan_ref[...].astype(BF16).astype(F32).T
        scans[...] = jnp.concatenate([scan, scan], axis=1)

    count, steps, channels = lcms_ref.shape
    inner = jnp.dot(
        lcms_ref[...].reshape(count * steps, channels), weights[...], preferred_element_type=F32
    )
    sums = jnp.sum(inner.reshape(count, steps, 2 * rank) * scans[...][None], axis=1)
    out_ref[...] = sums + pltpu.roll(sums, rank, 1)


def lcms_pass(lcms, scan_factor, mz_factor):
    samples, steps, channels = lcms.shape
    rank = mz_factor.shape[0]
    count = 8
    return pl.pallas_call(
        lcms_body,
        name="lcms_pass",
        grid=(samples // count,),
        in_specs=[
            pl.BlockSpec((count, steps, channels), lambda i: (i, 0, 0)),
            whole(scan_factor.shape),
            whole(mz_factor.shape),
        ],
        out_specs=pl.BlockSpec((count, 2 * rank), lambda i: (i, 0)),
        out_shape=jax.ShapeDtypeStruct((samples, 2 * rank), F32),
        scratch_shapes=[
            pltpu.VMEM((channels, 2 * rank), BF16),
            pltpu.VMEM((steps, 2 * rank), F32),
        ],
        cost_estimate=cost(2 * samples * steps * channels * 256, 2 * samples * steps * channels),
    )(lcms, scan_factor, mz_factor)


def weights_body(own_ref, other_ref, left_ref, gram_ref):
    rank = own_ref.shape[1]
    own_high, own_low = split(own_ref[...].T)
    other_high, other_low = split(other_ref[...].T)
    left = jnp.concatenate(
        [
            jnp.concatenate([own_high, other_high, own_high, other_high], axis=1),
            jnp.concatenate([own_low, other_low, own_low, other_low], axis=1),
        ],
        axis=0,
    )
    left_ref[...] = left
    right = stack_split([own_ref[...], other_ref[...]])
    products = jnp.dot(left, right, preferred_element_type=F32)
    gram = products[:rank] + products[rank:]
    gram_ref[...] = jnp.concatenate([gram, gram], axis=1)


def weights_pass(own, other):
    samples, rank = own.shape
    return pl.pallas_call(
        weights_body,
        name="weights_pass",
        out_shape=[
            jax.ShapeDtypeStruct((2 * rank, 4 * samples), BF16),
            jax.ShapeDtypeStruct((rank, 2 * rank), F32),
        ],
        cost_estimate=cost(2 * 128 * 256 * 64, 131072),
    )(own, other)


def project_body(left_ref, own_ref, other_ref, *refs):
    rank, columns = left_ref.shape[0] // 2, own_ref.shape[2]
    outs = [ref for ref in refs if ref.shape[1] >= columns]
    extras = [ref for ref in refs if ref.shape[1] < columns]
    right = stack_split([own_ref[0], other_ref[0]])
    products = jnp.dot(left_ref[...], right, preferred_element_type=F32)
    values = products[:rank] + products[rank:]
    for k, out_ref in enumerate(outs):

        @pl.when(pl.program_id(0) == k)
        def _():
            out_ref[:, :columns] = values

    for extra in extras:
        outs[0][:, columns:] = extra[...]


def project_pass(left, own, other, extra, first, count):
    _, samples, columns = own.shape
    rank = left.shape[0] // 2
    extras = [] if extra is None else [extra]
    wide = columns + sum(e.shape[1] for e in extras)
    piece = pl.BlockSpec((1, samples, columns), lambda k: (first + k, 0, 0))
    return pl.pallas_call(
        project_body,
        grid=(count,),
        in_specs=[whole(left.shape), piece, piece] + [whole(e.shape) for e in extras],
        out_specs=[whole((rank, wide))] * count,
        out_shape=[pltpu.VMEM((rank, wide), F32)] * count,
        cost_estimate=cost(2 * 256 * 256 * columns * count, 12 * 64 * columns * count),
    )(left, own, other, *extras)


def fit_body(count, *refs):
    sweeps, refs = refs[: 4 * count], refs[4 * count :]
    own_sum, other_sum, own_ref, other_ref, own_out, other_out = refs[:6]
    _, samples, _ = own_ref.shape
    rank = own_sum.shape[1] // 2
    sums = None
    for k in range(count):
        part, inward, across, outward = (ref[...] for ref in sweeps[4 * k : 4 * k + 4])
        total = part + inward + across + outward
        refs[6 + k][...] = total
        right = stack_split([total])
        rows = jnp.concatenate([stack_split([own_ref[k], other_ref[k]]), right], axis=0)
        products = lax.dot_general(rows, right, NT, preferred_element_type=F32)
        sums = products if sums is None else sums + products
    sums = sums[:, :rank] + sums[:, rank:]
    own_fit = sums[:samples] + sums[2 * samples : 3 * samples]
    other_fit = sums[samples : 2 * samples] + sums[3 * samples : 4 * samples]
    gram = sums[4 * samples : 4 * samples + rank] + sums[4 * samples + rank :]
    own_out[...] = own_sum[...] + jnp.concatenate([own_fit, gram], axis=1)
    other_out[...] = other_sum[...] + jnp.concatenate([other_fit, gram], axis=1)


def fit_pass(sweeps, own_sum, other_sum, own, other, first):
    _, samples, columns = own.shape
    count, rank = len(sweeps), own_sum.shape[1] // 2
    shape = jax.ShapeDtypeStruct((samples, 2 * rank), F32)
    pieces = pl.BlockSpec((count, samples, columns), lambda i: (first // count, 0, 0))
    arrays = [array for sweep in sweeps for array in sweep]
    own_sum, other_sum, *totals = pl.pallas_call(
        functools.partial(fit_body, count),
        grid=(1,),
        in_specs=[whole((rank, columns))] * len(arrays)
        + [whole(own_sum.shape), whole(other_sum.shape), pieces, pieces],
        out_specs=[whole(shape.shape)] * 2 + [whole((rank, columns))] * count,
        out_shape=[shape, shape] + [jax.ShapeDtypeStruct((rank, columns), F32)] * count,
        cost_estimate=cost(2 * 384 * 256 * columns * count, 32 * 64 * columns * count),
    )(*arrays, own_sum, other_sum, own, other)
    return own_sum, other_sum, totals


def eliminate(matrix, right):
    size = matrix.shape[0]
    work = jnp.concatenate([matrix, right], axis=1)
    rows = lax.broadcasted_iota(jnp.int32, (size, 1), 0)
    pivots = jnp.zeros((size, 1), F32)
    for k in range(size):
        inverse = 1.0 / work[k : k + 1, k : k + 1]
        here = rows == k
        factor = jnp.where(here, 0.0, work[:, k : k + 1] * inverse)
        pivots = jnp.where(here, inverse, pivots)
        work = work - factor * work[k : k + 1, :]
    return work[:, size:] * pivots


def dot32(a, b, dims=(((1,), (0,)), ((), ()))):
    return lax.dot_general(a, b, dims, precision=HIGHEST, preferred_element_type=F32)


def mix_body(gram_ref, lcms_gram_ref, ppm_gram_ref, out_ref):
    rank = lcms_gram_ref.shape[0]
    out_ref[...] = eliminate(gram_ref[:, :rank], lcms_gram_ref[...] + ppm_gram_ref[...])


def mix_pass(gram, lcms_gram, ppm_gram):
    return pl.pallas_call(
        mix_body,
        name="mix_pass",
        out_shape=jax.ShapeDtypeStruct(lcms_gram.shape, F32),
        cost_estimate=cost(1 << 22, 65536),
    )(gram, lcms_gram, ppm_gram)


def sample_body(fit_ref, mix_ref, lcms_gram_ref, lcms_ref, out_ref):
    rank = mix_ref.shape[0]
    mix = mix_ref[...]
    fit = dot32(fit_ref[:, :rank], mix)
    new_gram = dot32(mix, dot32(fit_ref[:, rank:], mix), (((0,), (0,)), ((), ())))
    right = lcms_ref[:, :rank] + fit
    out_ref[...] = eliminate(lcms_gram_ref[...] + new_gram, right.T).T


def sample_pass(fit, mix, lcms_gram, lcms_part):
    return pl.pallas_call(
        sample_body,
        name="sample_pass",
        out_shape=jax.ShapeDtypeStruct((fit.shape[0], mix.shape[0]), F32),
        cost_estimate=cost(1 << 22, 65536),
    )(fit, mix, lcms_gram, lcms_part)


def ppm_body(pieces, chip_ref, mix_ref, *refs):
    out_ref = refs[-1]
    rank, width = mix_ref.shape[0], refs[0].shape[1]
    high, low = split(mix_ref[...].T)
    left = jnp.concatenate(
        [jnp.concatenate([high, high], axis=1), jnp.concatenate([low, low], axis=1)], axis=0
    )
    for piece in range(pieces):
        products = jnp.dot(left, stack_split([refs[piece][...]]), preferred_element_type=F32)
        out_ref[:, piece * width : (piece + 1) * width] = products[:rank] + products[rank:]


def ppm_pass(chip, mix, totals, width):
    rank, pieces = mix.shape[0], len(totals)
    return pl.pallas_call(
        functools.partial(ppm_body, pieces),
        name="ppm_pass",
        grid_spec=pltpu.PrefetchScalarGridSpec(
            num_scalar_prefetch=1,
            grid=(1,),
            in_specs=[whole(mix.shape)]
            + [pl.BlockSpec((rank, width), lambda i, c: (0, c[0])) for _ in totals],
            out_specs=whole((rank, pieces * width)),
        ),
        out_shape=jax.ShapeDtypeStruct((rank, pieces * width), F32),
        cost_estimate=cost(2 * 256 * 128 * pieces * width, 8 * 64 * pieces * width),
    )(chip, mix, *totals)


def sum_over_mz(values, count):
    result = values
    for step in range(1, count):
        result = result + lax.ppermute(values, "mz", [(i, (i + step) % count) for i in range(count)])
    return result


def sum_over_chips(parts, runs):
    lines = [4 * line for line in range(runs // 8)]

    def send(values, pairs):
        hops = [
            (2 * (line + a) + core, 2 * (line + b) + core) for line in lines for a, b in pairs for core in (0, 1)
        ]
        return lax.ppermute(values, "run", hops)

    sweeps = []
    for part in parts:
        inward = send(part, [(0, 1), (3, 2)])
        across = send(part + inward, [(1, 2), (2, 1)])
        outward = send(part + across, [(1, 0), (2, 3)])
        if len(lines) > 1:
            line_total = part + inward + across + outward
            for step in range(1, len(lines)):
                shifted = [(i, (i + 8 * step) % runs) for i in range(runs)]
                part = part + lax.ppermute(line_total, "run", shifted)
        sweeps.append((part, inward, across, outward))
    return sweeps


def per_device(runs, mzs, lcms, spectra, scan_factor, mz_factor, ppm_factor):
    rank = mz_factor.shape[0]
    samples, positions = spectra.shape
    blocks = runs // 2
    width = positions // runs
    pieces = min(8, width // 128)
    run = lax.axis_index("run").astype(jnp.int32)
    core, chip = (run % 2).reshape(1), (run // 2).reshape(1)
    swap = [(i, i ^ 1) for i in range(runs)]

    early, own, leaving = nmr_pass(core, spectra, ppm_factor, mz_factor, blocks, pieces)
    other = lax.ppermute(leaving, "run", swap)
    early = sum_over_mz(early, mzs)
    lcms_part = sum_over_mz(lcms_pass(lcms, scan_factor, mz_factor), mzs)
    scan_gram = jnp.dot(scan_factor, scan_factor.T, precision=HIGHEST)
    lcms_gram = scan_gram * early[rank:, :rank]
    ppm_gram = early[:rank, rank:]
    own_rows = lcms_part[:, :rank] + early[:rank, :rank]
    other_rows = lax.ppermute(own_rows, "run", swap)
    left, gram = weights_pass(own_rows, other_rows)
    parts = project_pass(left, own, other, gram, 0, 1) + project_pass(left, own, other, None, 1, pieces - 1)
    sweeps = sum_over_chips(parts, runs)
    totals = []
    own_sum = other_sum = jnp.zeros((samples, 2 * rank), F32)
    for k in range(0, pieces, 2):
        own_sum, other_sum, done = fit_pass(sweeps[k : k + 2], own_sum, other_sum, own, other, k)
        totals += done
    mix = mix_pass(sum(array[:, own.shape[2] :] for array in sweeps[0]), lcms_gram, ppm_gram)
    ppm_new = ppm_pass(chip, mix, totals, width // pieces)
    fit = sum_over_mz(own_sum + lax.ppermute(other_sum, "run", swap), mzs)
    sample_factor = sample_pass(fit, mix, lcms_gram, lcms_part)
    return (sample_factor, ppm_new)


def solution(mesh):
    runs, mzs = mesh.shape["run"], mesh.shape["mz"]

    def whole_step(lcms, spectra, scan_factor, mz_factor, ppm_factor):
        return per_device(runs, mzs, lcms, spectra, scan_factor, mz_factor, ppm_factor)

    return jax.shard_map(
        whole_step,
        mesh=mesh,
        in_specs=(P("run", None, "mz"), P("run", "mz"), P(), P(None, "mz"), P(None, "mz")),
        out_specs=(P("run", None), P(None, ("mz", "run"))),
        check_vma=False,
    )
```

time: 251 us -> 195 us (0.78)
  blocking collectives: 97.7 us -> 0 us
  Pallas kernels: 0 us -> 68.4 us
  matrix products: 45.6 us -> 0.82 us
  starting transfers between devices: 6.74 us -> 50.5 us
  other arithmetic: 36.2 us -> 6.54 us
  waiting for transfers between devices: 44.1 us -> 61 us
  between operations: 14.2 us -> 1.38 us
    psum x3 -> x0, blocking collectives: 83.5 us -> none  [the longest x1 37.8 us: per_device(): new_gram = lax.psum(gram_local, ('run', 'mz'))]
    pallas_call x0 -> x12, Pallas kernels: none -> 68.4 us  [the longest x1 18.1 us: lcms_pass(): pl.pallas_call(lcms_body, name='lcms_pass', grid=(samples // count,), in_...]
    ppermute x0 -> x36, waiting for transfers between devices: none -> 61 us  [the longest x24 55.7 us: send(): return lax.ppermute(values, 'run', hops)]
    ppermute x0 -> x36, starting transfers between devices: none -> 50.5 us  [the longest x24 37.7 us: send(): return lax.ppermute(values, 'run', hops)]
    psum x1 -> x0, waiting for transfers between devices: 44 us -> none  [per_device(): mz_gram, ppm_gram = lax.psum((mz_local, ppm_local), 'mz')]
    dot_general x9 -> x1, matrix products: 42.8 us -> 0.82 us  [per_device(): scan_gram = jnp.dot(scan_factor, scan_factor.T, precision=HIGHEST)]
    another operation x15 -> x0, other arithmetic: 36.2 us -> none  [the longest x6 13 us: solve_rows(): lower_factor = jnp.linalg.cholesky(gram_matrix)]
    all_gather x1 -> x0, blocking collectives: 14.2 us -> none  [per_device(): whole_rows = lax.all_gather(sample_first, 'run', axis=0, tiled=True)]
  transfers between devices with their start and end apart: 3 -> 36, of which waited for: 1 -> 18; matrix products, arithmetic and copies ran while one was open for 27% -> 3% of each run, Pallas kernels for 0% -> 21%
where the time goes in v1:
time: 195 us; the launch traced here: 193 us
  Pallas kernels  68.4 us (35%)
  waiting for transfers between devices  61 us (31%)
  starting transfers between devices  50.5 us (26%)
  other arithmetic  6.54 us (3%)
  local copies, waits for them, and re-layouts  4.1 us (2%)
    ppermute x24, waiting for transfers between devices, send(): return lax.ppermute(values, 'run', hops)  55.7 us
    ppermute x24, starting transfers between devices, send(): return lax.ppermute(values, 'run', hops)  37.7 us
    pallas_call x1, Pallas kernels, lcms_pass(): pl.pallas_call(lcms_body, name='lcms_pass', grid=(samples // count,), in_...  18.1 us
    pallas_call x4, Pallas kernels, fit_pass(): pl.pallas_call(functools.partial(fit_body, count), grid=(1,), in_specs=[w...  13.4 us
    ppermute x9, starting transfers between devices, sum_over_mz(): lax.ppermute(values, 'mz', [(i, (i + step) % count) for i in range(count)])  12.2 us
    pallas_call x1, Pallas kernels, nmr_pass(): pl.pallas_call(functools.partial(nmr_body, blocks), name='nmr_pass', grid...  11.6 us
    pallas_call x1, Pallas kernels, sample_pass(): pl.pallas_call(sample_body, name='sample_pass', out_shape=jax.ShapeDtypeS...  7.55 us
    pallas_call x1, Pallas kernels, mix_pass(): pl.pallas_call(mix_body, name='mix_pass', out_shape=jax.ShapeDtypeStruct(...  7.13 us
  transfers between devices with their start and end apart: 36, of which 18 were waited for; matrix products, arithmetic and copies ran while one was open for 3% of the time, Pallas kernels for 21%

profile of v1, /device:TPU:0, one launch (start us, length us, event | category | flops | bytes accessed | tf_op | source)
XLA Modules:
  0.0 192.7 jit_solution(12563342311316325986)
XLA Ops:
  0.6 11.6 %nmr_pass.1 = (f32[128,128]{1,0:T(8,128)}, f32[8,64,1024]{2,1,0:T(8,128)}, f32[8,64,1024]{2,1,0:T(8,128)}) custom-call(s32[1]{0:T(128)} %bitcast.core_ref, f32[64,16384]{1,0:T(8,128)} %refs_7_.1, f32[64,16384]{1,0:T(8,128)} %refs_7_.1, f32[64,16384]{1,0:T(8,128)} %refs_7_.1, f32[64,16384]{1,0:T(8,128)} %refs_7_.1, f32[64,16384]{1,0:T(8,128)} %refs_7_.1, ...), custom_call_target="tpu_custom_call" | custom-call | flops 2147483648 | bytes 12582912 | tf_op jit(solution)/shard_map/nmr_pass/pallas_call | solution.py:88
  12.8 18.1 %lcms_pass.1 = f32[64,128]{1,0:T(8,128)} custom-call(bf16[64,256,1024]{2,1,0:T(8,128)(2,1)} %lcms_ref.1, f32[64,256]{1,0:T(8,128)} %scan_ref.1, f32[64,1024]{1,0:T(8,128)} %refs_16_.1), custom_call_target="tpu_custom_call" | custom-call | flops 8589934592 | bytes 33554432 | tf_op jit(solution)/shard_map/lcms_pass/pallas_call | solution.py:127
  30.9 2.5 %collective-permute-start = (f32[64,128]{1,0:T(8,128)}, f32[64,128]{1,0:T(8,128)S(1)}, u32[]{:S(2)}, u32[]{:S(2)}) collective-permute-start(f32[64,128]{1,0:T(8,128)} %lcms_pass.1), channel_id=1, source_target_pairs={{0,1},{1,2},{2,3},{3,0},{4,5},{5,6},{6,7},{7,4},{8,9},{9,10},{10,1... | collective-permute-start | bytes 98312 | tf_op jit(solution)/shard_map/ppermute | solution.py:332
  33.4 1.5 collective-permute-start.1
  34.9 1.4 collective-permute-start.2
  36.9 1.5 collective-permute-start.4
  38.4 0.9 collective-permute-start.5
  39.4 0.8 add_add_fusion.2.lcms_ref
  40.2 1.8 collective-permute-done.3
  42.0 0.7 collective-permute-done.5
  42.7 0.8 fusion
  43.6 1.2 collective-permute-done.6.other_ref
  45.4 1.8 weights_pass.1
  47.1 1.4 copy-done.8
  48.5 5.3 %shard_map.68 = (f32[64,1024]{1,0:T(8,128)S(1)}, f32[64,1024]{1,0:T(8,128)S(1)}, f32[64,1024]{1,0:T(8,128)S(1)}, f32[64,1024]{1,0:T(8,128)S(1)}, f32[64,1024]{1,...) custom-call(bf16[128,256]{1,0:T(8,128)(2,1)} %get-tuple-element.31.left_ref, ...), custom_call_target="tpu_custom_call" | custom-call | flops 939524096 | bytes 5505024 | tf_op jit(solution)/shard_map/pallas_call | solution.py:200
  53.9 3.5 %collective-permute-start.29 = (f32[64,1024]{1,0:T(8,128)S(1)}, f32[64,1024]{1,0:T(8,128)S(1)}, u32[]{:S(2)}, u32[]{:S(2)}) collective-permute-start(f32[64,1024]{1,0:T(8,128)S(1)} %get-tuple-element.41.refs_4_), channel_id=1, source_target_pairs={{0,8},{4,12},{24,16},{28,20},{1,9},{5,13},{25,17},{29,21},{2,10},{... | collective-permute-start | bytes 786440 | tf_op jit(solution)/shard_map/ppermute | solution.py:343
  57.4 1.3 collective-permute-start.23
  58.7 2.0 %collective-permute-start.20 = (f32[64,1024]{1,0:T(8,128)S(1)}, f32[64,1024]{1,0:T(8,128)}, u32[]{:S(2)}, u32[]{:S(2)}) collective-permute-start(f32[64,1024]{1,0:T(8,128)S(1)} %get-tuple-element.38.refs_0_), channel_id=1, source_target_pairs={{0,8},{4,12},{24,16},{28,20},{1,9},{5,13},{25,17},{29,21},{2,10},{... | collective-permute-start | bytes 786440 | tf_op jit(solution)/shard_map/ppermute | solution.py:343
  60.7 1.3 collective-permute-start.17
  62.0 1.3 shard_map.69.refs_0_
  63.3 1.3 collective-permute-start.26
  64.7 3.8 %collective-permute-start.14 = (f32[64,1024]{1,0:T(8,128)S(1)}, f32[64,1024]{1,0:T(8,128)S(1)}, u32[]{:S(2)}, u32[]{:S(2)}) collective-permute-start(f32[64,1024]{1,0:T(8,128)S(1)} %get-tuple-element.36.refs_0_), channel_id=1, source_target_pairs={{0,8},{4,12},{24,16},{28,20},{1,9},{5,13},{25,17},{29,21},{2,10},{... | collective-permute-start | bytes 786440 | tf_op jit(solution)/shard_map/ppermute | solution.py:343
  68.4 1.2 collective-permute-done.23.refs_5_
  69.7 4.4 %collective-permute-start.11 = (f32[64,1024]{1,0:T(8,128)S(1)}, f32[64,1024]{1,0:T(8,128)S(1)}, u32[]{:S(2)}, u32[]{:S(2)}) collective-permute-start(f32[64,1024]{1,0:T(8,128)S(1)} %get-tuple-element.35.refs_4_), channel_id=1, source_target_pairs={{0,8},{4,12},{24,16},{28,20},{1,9},{5,13},{25,17},{29,21},{2,10},{... | collective-permute-start | bytes 786440 | tf_op jit(solution)/shard_map/ppermute | solution.py:343
  74.1 1.2 collective-permute-done.20.refs_1_
  75.3 4.5 %collective-permute-start.8 = (f32[64,1024]{1,0:T(8,128)S(1)}, f32[64,1024]{1,0:T(8,128)S(1)}, u32[]{:S(2)}, u32[]{:S(2)}) collective-permute-start(f32[64,1024]{1,0:T(8,128)S(1)} %get-tuple-element.34.refs_0_), channel_id=1, source_target_pairs={{0,8},{4,12},{24,16},{28,20},{1,9},{5,13},{25,17},{29,21},{2,10},{... | collective-permute-start | bytes 786440 | tf_op jit(solution)/shard_map/ppermute | solution.py:343
  79.8 1.1 collective-permute-done.17.refs_5_
  81.6 5.6 %collective-permute-done.26.refs_1_ = f32[64,1152]{1,0:T(8,128)S(1)} collective-permute-done((f32[64,1152]{1,0:T(8,128)S(1)}, f32[64,1152]{1,0:T(8,128)S(1)}, u32[]{:S(2)}, u32[]{:S(2)}) %collective-permute-start.26) | collective-permute-done | bytes 294944 | tf_op jit(solution)/shard_map/ppermute | solution.py:343
  87.9 4.9 %collective-permute-done.14.refs_1_ = f32[64,1024]{1,0:T(8,128)S(1)} collective-permute-done((f32[64,1024]{1,0:T(8,128)S(1)}, f32[64,1024]{1,0:T(8,128)S(1)}, u32[]{:S(2)}, u32[]{:S(2)}) %collective-permute-start.14) | collective-permute-done | bytes 262176 | tf_op jit(solution)/shard_map/ppermute | solution.py:343
  93.5 1.0 add.111
  94.5 4.0 %collective-permute-done.11.refs_5_ = f32[64,1024]{1,0:T(8,128)S(1)} collective-permute-done((f32[64,1024]{1,0:T(8,128)S(1)}, f32[64,1024]{1,0:T(8,128)S(1)}, u32[]{:S(2)}, u32[]{:S(2)}) %collective-permute-start.11) | collective-permute-done | bytes 262176 | tf_op jit(solution)/shard_map/ppermute | solution.py:343
  99.2 4.1 %collective-permute-done.8.refs_1_ = f32[64,1024]{1,0:T(8,128)S(1)} collective-permute-done((f32[64,1024]{1,0:T(8,128)S(1)}, f32[64,1024]{1,0:T(8,128)S(1)}, u32[]{:S(2)}, u32[]{:S(2)}) %collective-permute-start.8) | collective-permute-done | bytes 262176 | tf_op jit(solution)/shard_map/ppermute | solution.py:343
  104.0 0.7 collective-permute-start.15
  105.5 0.7 collective-permute-start.9
  106.3 1.3 collective-permute-start.31
  107.6 1.3 collective-permute-start.28
  109.0 1.3 collective-permute-start.25
  110.3 0.8 add.112
  111.1 1.3 collective-permute-start.22
  112.4 0.7 add.110
  113.2 1.3 collective-permute-start.19
  114.5 11.6 %collective-permute-done.31.refs_7_ = f32[64,1024]{1,0:T(8,128)S(1)} collective-permute-done((f32[64,1024]{1,0:T(8,128)S(1)}, f32[64,1024]{1,0:T(8,128)S(1)}, u32[]{:S(2)}, u32[]{:S(2)}) %collective-permute-start.31) | collective-permute-done | bytes 262176 | tf_op jit(solution)/shard_map/ppermute | solution.py:343
  126.1 1.3 collective-permute-start.16
  127.6 10.5 %collective-permute-done.25.refs_7_ = f32[64,1024]{1,0:T(8,128)S(1)} collective-permute-done((f32[64,1024]{1,0:T(8,128)S(1)}, f32[64,1024]{1,0:T(8,128)S(1)}, u32[]{:S(2)}, u32[]{:S(2)}) %collective-permute-start.25) | collective-permute-done | bytes 262176 | tf_op jit(solution)/shard_map/ppermute | solution.py:343
  138.1 1.3 collective-permute-start.13
  139.4 1.3 collective-permute-start.10
  141.4 3.3 %shard_map.70 = (f32[64,128]{1,0:T(8,128)}, f32[64,128]{1,0:T(8,128)}, f32[64,1024]{1,0:T(8,128)}, f32[64,1024]{1,0:T(8,128)}) custom-call(f32[64,1152]{1,0:T(8,128)} %copy-done, f32[64,1152]{1,0:T(8,128)} %copy-done.9, f32[64,1152]{1,0:T(8,128)} %copy-done.10, f32[64,1152]{1,0:T(8,128)} %copy-done.25, f32[64,1024]{1,0:T(8,128)} %copy-done.7, ...), custom_call_target="tpu_custom_call" | custom-call | flops 402653184 | bytes 4194304 | tf_op jit(solution)/shard_map/pallas_call | solution.py:238
  144.7 3.4 %shard_map.71 = (f32[64,128]{1,0:T(8,128)}, f32[64,128]{1,0:T(8,128)}, f32[64,1024]{1,0:T(8,128)}, f32[64,1024]{1,0:T(8,128)}) custom-call(f32[64,1024]{1,0:T(8,128)} %copy-done.5, f32[64,1024]{1,0:T(8,128)} %collective-permute-done.20.refs_1_, f32[64,1024]{1,0:T(8,128)} %copy-done.23, f32[64,1024]{1,0:T(8,128)} %collective-permute-done.22.refs_3_, ...), custom_call_target="tpu_custom_call" | custom-call | flops 402653184 | bytes 4194304 | tf_op jit(solution)/shard_map/pallas_call | solution.py:238
  148.1 1.2 collective-permute-done.19.refs_7_
  149.3 5.6 %collective-permute-done.16.refs_3_ = f32[64,1024]{1,0:T(8,128)S(1)} collective-permute-done((f32[64,1024]{1,0:T(8,128)S(1)}, f32[64,1024]{1,0:T(8,128)S(1)}, u32[]{:S(2)}, u32[]{:S(2)}) %collective-permute-start.16) | collective-permute-done | bytes 262176 | tf_op jit(solution)/shard_map/ppermute | solution.py:343
  154.9 0.7 copy-done.32
  155.6 3.3 %shard_map.72 = (f32[64,128]{1,0:T(8,128)}, f32[64,128]{1,0:T(8,128)}, f32[64,1024]{1,0:T(8,128)}, f32[64,1024]{1,0:T(8,128)}) custom-call(f32[64,1024]{1,0:T(8,128)} %copy-done.3, f32[64,1024]{1,0:T(8,128)} %copy-done.14, f32[64,1024]{1,0:T(8,128)} %copy-done.22, f32[64,1024]{1,0:T(8,128)} %copy-done.32, f32[64,1024]{1,0:T(8,128)} %copy-done.4, ...), custom_call_target="tpu_custom_call" | custom-call | flops 402653184 | bytes 4194304 | tf_op jit(solution)/shard_map/pallas_call | solution.py:238
  159.0 1.6 collective-permute-done.13.refs_7_
  160.6 3.1 %collective-permute-done.10.refs_3_ = f32[64,1024]{1,0:T(8,128)S(1)} collective-permute-done((f32[64,1024]{1,0:T(8,128)S(1)}, f32[64,1024]{1,0:T(8,128)S(1)}, u32[]{:S(2)}, u32[]{:S(2)}) %collective-permute-start.10) | collective-permute-done | bytes 262176 | tf_op jit(solution)/shard_map/ppermute | solution.py:343
  163.7 0.7 copy-done.29
  164.4 3.4 %shard_map.73 = (f32[64,128]{1,0:T(8,128)}, f32[64,128]{1,0:T(8,128)}, f32[64,1024]{1,0:T(8,128)}, f32[64,1024]{1,0:T(8,128)}) custom-call(f32[64,1024]{1,0:T(8,128)} %copy-done.1, f32[64,1024]{1,0:T(8,128)} %copy-done.13, f32[64,1024]{1,0:T(8,128)} %copy-done.20, f32[64,1024]{1,0:T(8,128)} %copy-done.29, f32[64,1024]{1,0:T(8,128)} %copy-done.2, ...), custom_call_target="tpu_custom_call" | custom-call | flops 402653184 | bytes 4194304 | tf_op jit(solution)/shard_map/pallas_call | solution.py:238
  167.8 1.4 collective-permute-done.32
  169.2 0.8 add.119
  169.9 2.3 %collective-permute-start.33 = (f32[64,128]{1,0:T(8,128)S(1)}, f32[64,128]{1,0:T(8,128)S(1)}, u32[]{:S(2)}, u32[]{:S(2)}) collective-permute-start(f32[64,128]{1,0:T(8,128)S(1)} %add.119), channel_id=1, source_target_pairs={{0,1},{1,2},{2,3},{3,0},{4,5},{5,6},{6,7},{7,4},{8,9},{9,10},{10,1... | collective-permute-start | bytes 98312 | tf_op jit(solution)/shard_map/ppermute | solution.py:332
  172.7 1.0 collective-permute-start.35
  173.7 1.4 slice_add_fusion.gram_ref
  175.2 7.1 %mix_pass.1.mix_ref = f32[64,64]{1,0:T(8,128)} custom-call(f32[64,128]{1,0:T(8,128)} %slice_add_fusion.gram_ref, f32[64,64]{1,0:T(8,128)} %get-tuple-element.59.lcms_gram_ref, f32[64,64]{1,0:T(8,128)} %get-tuple-element.58.ppm_gram_ref), custom_call_target="tpu_custom_call" | custom-call | flops 4194304 | bytes 65536 | tf_op jit(solution)/shard_map/mix_pass/pallas_call | solution.py:274
  182.3 2.3 %ppm_pass.1 = f32[64,2048]{1,0:T(8,128)} custom-call(s32[1]{0:T(128)} %bitcast.1.chip_ref, f32[64,64]{1,0:T(8,128)} %mix_pass.1.mix_ref, f32[64,1024]{1,0:T(8,128)} %get-tuple-element.50.refs_0_, f32[64,1024]{1,0:T(8,128)} %get-tuple-element.51.refs_1_, f32[64,1024]{1,0:T(8,128)} %get-tuple-element.52.refs_2_, f32[64,1024]{1,0:T(8,128)} %get-tuple-element.53.refs_3_, ...), custom_call_target="tpu_custom_call" | custom-call | flops 134217728 | bytes 1048576 | tf_op jit(solution)/shard_map/ppm_pass/pallas_call | solution.py:314
  185.2 7.6 %sample_pass.1 = f32[64,64]{1,0:T(8,128)} custom-call(f32[64,128]{1,0:T(8,128)} %add_add_fusion.1.fit_ref, f32[64,64]{1,0:T(8,128)} %mix_pass.1.mix_ref, f32[64,64]{1,0:T(8,128)} %get-tuple-element.59.lcms_gram_ref, f32[64,128]{1,0:T(8,128)} %copy-done.26), custom_call_target="tpu_custom_call" | custom-call | flops 4194304 | bytes 65536 | tf_op jit(solution)/shard_map/sample_pass/pallas_call | solution.py:292
  (115 shorter events, 8.3 us)
Async XLA Ops:
  12.2 24.1 %copy-start.34 = (f32[128,128]{1,0:T(8,128)S(1)}, f32[128,128]{1,0:T(8,128)}, u32[]{:S(2)}) copy-start(f32[128,128]{1,0:T(8,128)} %get-tuple-element.30) | copy-start | bytes 196612
  12.3 30.5 %copy-start.24 = (f32[64,256]{1,0:T(8,128)S(1)}, f32[64,256]{1,0:T(8,128)}, u32[]{:S(2)}) copy-start(f32[64,256]{1,0:T(8,128)} %scan_ref.1) | copy-start | bytes 196612
  12.3 34.9 %collective-permute-start.7 = (f32[8,64,1024]{2,1,0:T(8,128)}, f32[8,64,1024]{2,1,0:T(8,128)S(1)}, u32[]{:S(2)}, u32[]{:S(2)}) collective-permute-start(f32[8,64,1024]{2,1,0:T(8,128)} %get-tuple-element.33), channel_id=1, source_target_pairs={{0,4},{4,0},{8,12},{12,8},{16,20},{20,16},{24,28},{28,24},{1,5},{5... | collective-permute-start | bytes 6291464 | tf_op jit(solution)/shard_map/ppermute | solution.py:370
  30.9 6.0 %collective-permute-start = (f32[64,128]{1,0:T(8,128)}, f32[64,128]{1,0:T(8,128)S(1)}, u32[]{:S(2)}, u32[]{:S(2)}) collective-permute-start(f32[64,128]{1,0:T(8,128)} %lcms_pass.1), channel_id=1, source_target_pairs={{0,1},{1,2},{2,3},{3,0},{4,5},{5,6},{6,7},{7,4},{8,9},{9,10},{10,1... | collective-permute-start | bytes 98312 | tf_op jit(solution)/shard_map/ppermute | solution.py:332
  33.4 5.0 %collective-permute-start.1 = (f32[64,128]{1,0:T(8,128)}, f32[64,128]{1,0:T(8,128)S(1)}, u32[]{:S(2)}, u32[]{:S(2)}) collective-permute-start(f32[64,128]{1,0:T(8,128)} %lcms_pass.1), channel_id=1, source_target_pairs={{0,2},{1,3},{2,0},{3,1},{4,6},{5,7},{6,4},{7,5},{8,10},{9,11},{10,... | collective-permute-start | bytes 98312 | tf_op jit(solution)/shard_map/ppermute | solution.py:332
  34.9 4.5 %collective-permute-start.2 = (f32[64,128]{1,0:T(8,128)}, f32[64,128]{1,0:T(8,128)S(1)}, u32[]{:S(2)}, u32[]{:S(2)}) collective-permute-start(f32[64,128]{1,0:T(8,128)} %lcms_pass.1), channel_id=1, source_target_pairs={{0,3},{1,0},{2,1},{3,2},{4,7},{5,4},{6,5},{7,6},{8,11},{9,8},{10,9... | collective-permute-start | bytes 98312 | tf_op jit(solution)/shard_map/ppermute | solution.py:332
  36.3 5.6 %collective-permute-start.3 = (f32[128,128]{1,0:T(8,128)S(1)}, f32[128,128]{1,0:T(8,128)S(1)}, u32[]{:S(2)}, u32[]{:S(2)}) collective-permute-start(f32[128,128]{1,0:T(8,128)S(1)} %copy-done.34), channel_id=1, source_target_pairs={{0,1},{1,2},{2,3},{3,0},{4,5},{5,6},{6,7},{7,4},{8,9},{9,10},{10,1... | collective-permute-start | bytes 196616 | tf_op jit(solution)/shard_map/ppermute | solution.py:332
  36.9 5.0 %collective-permute-start.4 = (f32[128,128]{1,0:T(8,128)S(1)}, f32[128,128]{1,0:T(8,128)S(1)}, u32[]{:S(2)}, u32[]{:S(2)}) collective-permute-start(f32[128,128]{1,0:T(8,128)S(1)} %copy-done.34), channel_id=1, source_target_pairs={{0,2},{1,3},{2,0},{3,1},{4,6},{5,7},{6,4},{7,5},{8,10},{9,11},{10,... | collective-permute-start | bytes 196616 | tf_op jit(solution)/shard_map/ppermute | solution.py:332
  38.4 4.3 %collective-permute-start.5 = (f32[128,128]{1,0:T(8,128)S(1)}, f32[128,128]{1,0:T(8,128)S(1)}, u32[]{:S(2)}, u32[]{:S(2)}) collective-permute-start(f32[128,128]{1,0:T(8,128)S(1)} %copy-done.34), channel_id=1, source_target_pairs={{0,3},{1,0},{2,1},{3,2},{4,7},{5,4},{6,5},{7,6},{8,11},{9,8},{10,9... | collective-permute-start | bytes 196616 | tf_op jit(solution)/shard_map/ppermute | solution.py:332
  40.1 23.2 %copy-start.26 = (f32[64,128]{1,0:T(8,128)}, f32[64,128]{1,0:T(8,128)S(1)}, u32[]{:S(2)}) copy-start(f32[64,128]{1,0:T(8,128)S(1)} %add_add_fusion.2.lcms_ref) | copy-start | bytes 98308
  43.6 1.2 collective-permute-start.6
  53.8 51.7 %copy-start.7 = (f32[64,1024]{1,0:T(8,128)}, f32[64,1024]{1,0:T(8,128)S(1)}, u32[]{:S(2)}) copy-start(f32[64,1024]{1,0:T(8,128)S(1)} %get-tuple-element.41.refs_4_) | copy-start | bytes 786436
  53.8 55.1 %copy-start.6 = (f32[64,1024]{1,0:T(8,128)}, f32[64,1024]{1,0:T(8,128)S(1)}, u32[]{:S(2)}) copy-start(f32[64,1024]{1,0:T(8,128)S(1)} %get-tuple-element.39.refs_4_) | copy-start | bytes 786436
  53.8 56.5 %copy-start.5 = (f32[64,1024]{1,0:T(8,128)}, f32[64,1024]{1,0:T(8,128)S(1)}, u32[]{:S(2)}) copy-start(f32[64,1024]{1,0:T(8,128)S(1)} %get-tuple-element.38.refs_0_) | copy-start | bytes 786436
  53.8 58.6 %copy-start.4 = (f32[64,1024]{1,0:T(8,128)}, f32[64,1024]{1,0:T(8,128)S(1)}, u32[]{:S(2)}) copy-start(f32[64,1024]{1,0:T(8,128)S(1)} %get-tuple-element.37.refs_4_) | copy-start | bytes 786436
  53.8 59.3 %copy-start.3 = (f32[64,1024]{1,0:T(8,128)}, f32[64,1024]{1,0:T(8,128)S(1)}, u32[]{:S(2)}) copy-start(f32[64,1024]{1,0:T(8,128)S(1)} %get-tuple-element.36.refs_0_) | copy-start | bytes 786436
  53.8 73.6 %copy-start.2 = (f32[64,1024]{1,0:T(8,128)}, f32[64,1024]{1,0:T(8,128)S(1)}, u32[]{:S(2)}) copy-start(f32[64,1024]{1,0:T(8,128)S(1)} %get-tuple-element.35.refs_4_) | copy-start | bytes 786436
  53.8 73.6 %copy-start.1 = (f32[64,1024]{1,0:T(8,128)}, f32[64,1024]{1,0:T(8,128)S(1)}, u32[]{:S(2)}) copy-start(f32[64,1024]{1,0:T(8,128)S(1)} %get-tuple-element.34.refs_0_) | copy-start | bytes 786436
  53.9 10.8 %collective-permute-start.29 = (f32[64,1024]{1,0:T(8,128)S(1)}, f32[64,1024]{1,0:T(8,128)S(1)}, u32[]{:S(2)}, u32[]{:S(2)}) collective-permute-start(f32[64,1024]{1,0:T(8,128)S(1)} %get-tuple-element.41.refs_4_), channel_id=1, source_target_pairs={{0,8},{4,12},{24,16},{28,20},{1,9},{5,13},{25,17},{29,21},{2,10},{... | collective-permute-start | bytes 786440 | tf_op jit(solution)/shard_map/ppermute | solution.py:343
  57.4 12.3 %collective-permute-start.23 = (f32[64,1024]{1,0:T(8,128)S(1)}, f32[64,1024]{1,0:T(8,128)S(1)}, u32[]{:S(2)}, u32[]{:S(2)}) collective-permute-start(f32[64,1024]{1,0:T(8,128)S(1)} %get-tuple-element.39.refs_4_), channel_id=1, source_target_pairs={{0,8},{4,12},{24,16},{28,20},{1,9},{5,13},{25,17},{29,21},{2,10},{... | collective-permute-start | bytes 786440 | tf_op jit(solution)/shard_map/ppermute | solution.py:343
  58.7 16.6 %collective-permute-start.20 = (f32[64,1024]{1,0:T(8,128)S(1)}, f32[64,1024]{1,0:T(8,128)}, u32[]{:S(2)}, u32[]{:S(2)}) collective-permute-start(f32[64,1024]{1,0:T(8,128)S(1)} %get-tuple-element.38.refs_0_), channel_id=1, source_target_pairs={{0,8},{4,12},{24,16},{28,20},{1,9},{5,13},{25,17},{29,21},{2,10},{... | collective-permute-start | bytes 786440 | tf_op jit(solution)/shard_map/ppermute | solution.py:343
  60.7 20.2 %collective-permute-start.17 = (f32[64,1024]{1,0:T(8,128)S(1)}, f32[64,1024]{1,0:T(8,128)S(1)}, u32[]{:S(2)}, u32[]{:S(2)}) collective-permute-start(f32[64,1024]{1,0:T(8,128)S(1)} %get-tuple-element.37.refs_4_), channel_id=1, source_target_pairs={{0,8},{4,12},{24,16},{28,20},{1,9},{5,13},{25,17},{29,21},{2,10},{... | collective-permute-start | bytes 786440 | tf_op jit(solution)/shard_map/ppermute | solution.py:343
  63.3 45.7 %copy-start = (f32[64,1152]{1,0:T(8,128)}, f32[64,1152]{1,0:T(8,128)S(1)}, u32[]{:S(2)}) copy-start(f32[64,1152]{1,0:T(8,128)S(1)} %shard_map.69.refs_0_) | copy-start | bytes 884740
  63.3 23.9 %collective-permute-start.26 = (f32[64,1152]{1,0:T(8,128)S(1)}, f32[64,1152]{1,0:T(8,128)S(1)}, u32[]{:S(2)}, u32[]{:S(2)}) collective-permute-start(f32[64,1152]{1,0:T(8,128)S(1)} %shard_map.69.refs_0_), channel_id=1, source_target_pairs={{0,8},{4,12},{24,16},{28,20},{1,9},{5,13},{25,17},{29,21},{2,10},{... | collective-permute-start | bytes 884744 | tf_op jit(solution)/shard_map/ppermute | solution.py:343
  64.6 76.7 %copy-start.16 = (f32[64,1024]{1,0:T(8,128)}, f32[64,1024]{1,0:T(8,128)S(1)}, u32[]{:S(2)}) copy-start(f32[64,1024]{1,0:T(8,128)S(1)} %collective-permute-done.29.refs_5_) | copy-start | bytes 786436
  64.7 28.2 %collective-permute-start.14 = (f32[64,1024]{1,0:T(8,128)S(1)}, f32[64,1024]{1,0:T(8,128)S(1)}, u32[]{:S(2)}, u32[]{:S(2)}) collective-permute-start(f32[64,1024]{1,0:T(8,128)S(1)} %get-tuple-element.36.refs_0_), channel_id=1, source_target_pairs={{0,8},{4,12},{24,16},{28,20},{1,9},{5,13},{25,17},{29,21},{2,10},{... | collective-permute-start | bytes 786440 | tf_op jit(solution)/shard_map/ppermute | solution.py:343
  69.7 18.3 %copy-start.15 = (f32[64,1024]{1,0:T(8,128)}, f32[64,1024]{1,0:T(8,128)S(1)}, u32[]{:S(2)}) copy-start(f32[64,1024]{1,0:T(8,128)S(1)} %collective-permute-done.23.refs_5_) | copy-start | bytes 786436
  69.7 28.8 %collective-permute-start.11 = (f32[64,1024]{1,0:T(8,128)S(1)}, f32[64,1024]{1,0:T(8,128)S(1)}, u32[]{:S(2)}, u32[]{:S(2)}) collective-permute-start(f32[64,1024]{1,0:T(8,128)S(1)} %get-tuple-element.35.refs_4_), channel_id=1, source_target_pairs={{0,8},{4,12},{24,16},{28,20},{1,9},{5,13},{25,17},{29,21},{2,10},{... | collective-permute-start | bytes 786440 | tf_op jit(solution)/shard_map/ppermute | solution.py:343
  75.3 28.0 %collective-permute-start.8 = (f32[64,1024]{1,0:T(8,128)S(1)}, f32[64,1024]{1,0:T(8,128)S(1)}, u32[]{:S(2)}, u32[]{:S(2)}) collective-permute-start(f32[64,1024]{1,0:T(8,128)S(1)} %get-tuple-element.34.refs_0_), channel_id=1, source_target_pairs={{0,8},{4,12},{24,16},{28,20},{1,9},{5,13},{25,17},{29,21},{2,10},{... | collective-permute-start | bytes 786440 | tf_op jit(solution)/shard_map/ppermute | solution.py:343
  80.9 30.2 %copy-start.12 = (f32[64,1024]{1,0:T(8,128)}, f32[64,1024]{1,0:T(8,128)S(1)}, u32[]{:S(2)}) copy-start(f32[64,1024]{1,0:T(8,128)S(1)} %collective-permute-done.17.refs_5_) | copy-start | bytes 786436
  80.9 23.1 %collective-permute-start.30 = (f32[64,1024]{1,0:T(8,128)S(1)}, f32[64,1024]{1,0:T(8,128)S(1)}, u32[]{:S(2)}, u32[]{:S(2)}) collective-permute-start(f32[64,1024]{1,0:T(8,128)S(1)} %add.117), channel_id=1, source_target_pairs={{8,16},{12,20},{16,8},{20,12},{9,17},{13,21},{17,9},{21,13},{10,18... | collective-permute-start | bytes 786440 | tf_op jit(solution)/shard_map/ppermute | solution.py:343
  87.2 25.9 %copy-start.9 = (f32[64,1152]{1,0:T(8,128)}, f32[64,1152]{1,0:T(8,128)S(1)}, u32[]{:S(2)}) copy-start(f32[64,1152]{1,0:T(8,128)S(1)} %collective-permute-done.26.refs_1_) | copy-start | bytes 884740
  87.2 17.5 %collective-permute-start.24 = (f32[64,1024]{1,0:T(8,128)S(1)}, f32[64,1024]{1,0:T(8,128)S(1)}, u32[]{:S(2)}, u32[]{:S(2)}) collective-permute-start(f32[64,1024]{1,0:T(8,128)S(1)} %add.113), channel_id=1, source_target_pairs={{8,16},{12,20},{16,8},{20,12},{9,17},{13,21},{17,9},{21,13},{10,18... | collective-permute-start | bytes 786440 | tf_op jit(solution)/shard_map/ppermute | solution.py:343
  92.8 20.4 %copy-start.14 = (f32[64,1024]{1,0:T(8,128)}, f32[64,1024]{1,0:T(8,128)S(1)}, u32[]{:S(2)}) copy-start(f32[64,1024]{1,0:T(8,128)S(1)} %collective-permute-done.14.refs_1_) | copy-start | bytes 786436
  92.8 13.4 %collective-permute-start.27 = (f32[64,1152]{1,0:T(8,128)S(1)}, f32[64,1152]{1,0:T(8,128)S(1)}, u32[]{:S(2)}, u32[]{:S(2)}) collective-permute-start(f32[64,1152]{1,0:T(8,128)S(1)} %add.115), channel_id=1, source_target_pairs={{8,16},{12,20},{16,8},{20,12},{9,17},{13,21},{17,9},{21,13},{10,18... | collective-permute-start | bytes 884744 | tf_op jit(solution)/shard_map/ppermute | solution.py:343
  98.4 29.0 %copy-start.11 = (f32[64,1024]{1,0:T(8,128)}, f32[64,1024]{1,0:T(8,128)S(1)}, u32[]{:S(2)}) copy-start(f32[64,1024]{1,0:T(8,128)S(1)} %collective-permute-done.11.refs_5_) | copy-start | bytes 786436
  98.4 7.1 %collective-permute-start.21 = (f32[64,1024]{1,0:T(8,128)S(1)}, f32[64,1024]{1,0:T(8,128)S(1)}, u32[]{:S(2)}, u32[]{:S(2)}) collective-permute-start(f32[64,1024]{1,0:T(8,128)S(1)} %add.111), channel_id=1, source_target_pairs={{8,16},{12,20},{16,8},{20,12},{9,17},{13,21},{17,9},{21,13},{10,18... | collective-permute-start | bytes 786440 | tf_op jit(solution)/shard_map/ppermute | solution.py:343
  103.3 24.3 %copy-start.13 = (f32[64,1024]{1,0:T(8,128)}, f32[64,1024]{1,0:T(8,128)S(1)}, u32[]{:S(2)}) copy-start(f32[64,1024]{1,0:T(8,128)S(1)} %collective-permute-done.8.refs_1_) | copy-start | bytes 786436
  103.3 4.3 %collective-permute-start.18 = (f32[64,1024]{1,0:T(8,128)S(1)}, f32[64,1024]{1,0:T(8,128)S(1)}, u32[]{:S(2)}, u32[]{:S(2)}) collective-permute-start(f32[64,1024]{1,0:T(8,128)S(1)} %add.109), channel_id=1, source_target_pairs={{8,16},{12,20},{16,8},{20,12},{9,17},{13,21},{17,9},{21,13},{10,18... | collective-permute-start | bytes 786440 | tf_op jit(solution)/shard_map/ppermute | solution.py:343
  104.0 35.4 %copy-start.21 = (f32[64,1024]{1,0:T(8,128)}, f32[64,1024]{1,0:T(8,128)S(1)}, u32[]{:S(2)}) copy-start(f32[64,1024]{1,0:T(8,128)S(1)} %collective-permute-done.30.refs_6_) | copy-start | bytes 786436
  104.0 5.0 %collective-permute-start.15 = (f32[64,1024]{1,0:T(8,128)S(1)}, f32[64,1024]{1,0:T(8,128)S(1)}, u32[]{:S(2)}, u32[]{:S(2)}) collective-permute-start(f32[64,1024]{1,0:T(8,128)S(1)} %add.107), channel_id=1, source_target_pairs={{8,16},{12,20},{16,8},{20,12},{9,17},{13,21},{17,9},{21,13},{10,18... | collective-permute-start | bytes 786440 | tf_op jit(solution)/shard_map/ppermute | solution.py:343
  104.7 40.0 %copy-start.18 = (f32[64,1024]{1,0:T(8,128)}, f32[64,1024]{1,0:T(8,128)S(1)}, u32[]{:S(2)}) copy-start(f32[64,1024]{1,0:T(8,128)S(1)} %collective-permute-done.24.refs_6_) | copy-start | bytes 786436
  104.7 6.3 %collective-permute-start.12 = (f32[64,1024]{1,0:T(8,128)S(1)}, f32[64,1024]{1,0:T(8,128)S(1)}, u32[]{:S(2)}, u32[]{:S(2)}) collective-permute-start(f32[64,1024]{1,0:T(8,128)S(1)} %add.105), channel_id=1, source_target_pairs={{8,16},{12,20},{16,8},{20,12},{9,17},{13,21},{17,9},{21,13},{10,18... | collective-permute-start | bytes 786440 | tf_op jit(solution)/shard_map/ppermute | solution.py:343
  105.5 35.2 %copy-start.23 = (f32[64,1024]{1,0:T(8,128)}, f32[64,1024]{1,0:T(8,128)S(1)}, u32[]{:S(2)}) copy-start(f32[64,1024]{1,0:T(8,128)S(1)} %collective-permute-done.21.refs_2_) | copy-start | bytes 786436
  105.5 7.6 %collective-permute-start.9 = (f32[64,1024]{1,0:T(8,128)S(1)}, f32[64,1024]{1,0:T(8,128)S(1)}, u32[]{:S(2)}, u32[]{:S(2)}) collective-permute-start(f32[64,1024]{1,0:T(8,128)S(1)} %add.103), channel_id=1, source_target_pairs={{8,16},{12,20},{16,8},{20,12},{9,17},{13,21},{17,9},{21,13},{10,18... | collective-permute-start | bytes 786440 | tf_op jit(solution)/shard_map/ppermute | solution.py:343
  106.2 35.1 %copy-start.10 = (f32[64,1152]{1,0:T(8,128)}, f32[64,1152]{1,0:T(8,128)S(1)}, u32[]{:S(2)}) copy-start(f32[64,1152]{1,0:T(8,128)S(1)} %collective-permute-done.27.refs_2_) | copy-start | bytes 884740
  106.3 19.9 %collective-permute-start.31 = (f32[64,1024]{1,0:T(8,128)S(1)}, f32[64,1024]{1,0:T(8,128)S(1)}, u32[]{:S(2)}, u32[]{:S(2)}) collective-permute-start(f32[64,1024]{1,0:T(8,128)S(1)} %add.118), channel_id=1, source_target_pairs={{8,0},{12,4},{16,24},{20,28},{9,1},{13,5},{17,25},{21,29},{10,2},{... | collective-permute-start | bytes 786440 | tf_op jit(solution)/shard_map/ppermute | solution.py:343
  107.6 30.5 %copy-start.19 = (f32[64,1024]{1,0:T(8,128)}, f32[64,1024]{1,0:T(8,128)S(1)}, u32[]{:S(2)}) copy-start(f32[64,1024]{1,0:T(8,128)S(1)} %collective-permute-done.18.refs_6_) | copy-start | bytes 786436
  107.6 31.8 %collective-permute-start.28 = (f32[64,1152]{1,0:T(8,128)S(1)}, f32[64,1152]{1,0:T(8,128)S(1)}, u32[]{:S(2)}, u32[]{:S(2)}) collective-permute-start(f32[64,1152]{1,0:T(8,128)S(1)} %add.116), channel_id=1, source_target_pairs={{8,0},{12,4},{16,24},{20,28},{9,1},{13,5},{17,25},{21,29},{10,2},{... | collective-permute-start | bytes 884744 | tf_op jit(solution)/shard_map/ppermute | solution.py:343
  109.0 30.4 %copy-start.22 = (f32[64,1024]{1,0:T(8,128)}, f32[64,1024]{1,0:T(8,128)S(1)}, u32[]{:S(2)}) copy-start(f32[64,1024]{1,0:T(8,128)S(1)} %collective-permute-done.15.refs_2_) | copy-start | bytes 786436
  109.0 29.1 %collective-permute-start.25 = (f32[64,1024]{1,0:T(8,128)S(1)}, f32[64,1024]{1,0:T(8,128)S(1)}, u32[]{:S(2)}, u32[]{:S(2)}) collective-permute-start(f32[64,1024]{1,0:T(8,128)S(1)} %add.114), channel_id=1, source_target_pairs={{8,0},{12,4},{16,24},{20,28},{9,1},{13,5},{17,25},{21,29},{10,2},{... | collective-permute-start | bytes 786440 | tf_op jit(solution)/shard_map/ppermute | solution.py:343
  111.1 33.6 %copy-start.17 = (f32[64,1024]{1,0:T(8,128)}, f32[64,1024]{1,0:T(8,128)S(1)}, u32[]{:S(2)}) copy-start(f32[64,1024]{1,0:T(8,128)S(1)} %collective-permute-done.12.refs_6_) | copy-start | bytes 786436
  111.1 33.6 %collective-permute-start.22 = (f32[64,1024]{1,0:T(8,128)}, f32[64,1024]{1,0:T(8,128)}, u32[]{:S(2)}, u32[]{:S(2)}) collective-permute-start(f32[64,1024]{1,0:T(8,128)} %add.112), channel_id=1, source_target_pairs={{8,0},{12,4},{16,24},{20,28},{9,1},{13,5},{17,25},{21,29},{10,2},{... | collective-permute-start | bytes 786440 | tf_op jit(solution)/shard_map/ppermute | solution.py:343
  113.2 34.9 %copy-start.20 = (f32[64,1024]{1,0:T(8,128)}, f32[64,1024]{1,0:T(8,128)S(1)}, u32[]{:S(2)}) copy-start(f32[64,1024]{1,0:T(8,128)S(1)} %collective-permute-done.9.refs_2_) | copy-start | bytes 786436
  113.2 36.1 %collective-permute-start.19 = (f32[64,1024]{1,0:T(8,128)}, f32[64,1024]{1,0:T(8,128)S(1)}, u32[]{:S(2)}, u32[]{:S(2)}) collective-permute-start(f32[64,1024]{1,0:T(8,128)} %add.110), channel_id=1, source_target_pairs={{8,0},{12,4},{16,24},{20,28},{9,1},{13,5},{17,25},{21,29},{10,2},{... | collective-permute-start | bytes 786440 | tf_op jit(solution)/shard_map/ppermute | solution.py:343
  126.1 14.6 %copy-start.30 = (f32[64,1024]{1,0:T(8,128)}, f32[64,1024]{1,0:T(8,128)S(1)}, u32[]{:S(2)}) copy-start(f32[64,1024]{1,0:T(8,128)S(1)} %collective-permute-done.31.refs_7_) | copy-start | bytes 786436
  126.1 28.8 %collective-permute-start.16 = (f32[64,1024]{1,0:T(8,128)S(1)}, f32[64,1024]{1,0:T(8,128)S(1)}, u32[]{:S(2)}, u32[]{:S(2)}) collective-permute-start(f32[64,1024]{1,0:T(8,128)S(1)} %add.108), channel_id=1, source_target_pairs={{8,0},{12,4},{16,24},{20,28},{9,1},{13,5},{17,25},{21,29},{10,2},{... | collective-permute-start | bytes 786440 | tf_op jit(solution)/shard_map/ppermute | solution.py:343
  138.1 6.7 %copy-start.31 = (f32[64,1024]{1,0:T(8,128)}, f32[64,1024]{1,0:T(8,128)S(1)}, u32[]{:S(2)}) copy-start(f32[64,1024]{1,0:T(8,128)S(1)} %collective-permute-done.25.refs_7_) | copy-start | bytes 786436
  138.1 22.5 %collective-permute-start.13 = (f32[64,1024]{1,0:T(8,128)S(1)}, f32[64,1024]{1,0:T(8,128)S(1)}, u32[]{:S(2)}, u32[]{:S(2)}) collective-permute-start(f32[64,1024]{1,0:T(8,128)S(1)} %add.106), channel_id=1, source_target_pairs={{8,0},{12,4},{16,24},{20,28},{9,1},{13,5},{17,25},{21,29},{10,2},{... | collective-permute-start | bytes 786440 | tf_op jit(solution)/shard_map/ppermute | solution.py:343
  139.4 24.3 %collective-permute-start.10 = (f32[64,1024]{1,0:T(8,128)S(1)}, f32[64,1024]{1,0:T(8,128)S(1)}, u32[]{:S(2)}, u32[]{:S(2)}) collective-permute-start(f32[64,1024]{1,0:T(8,128)S(1)} %add.104), channel_id=1, source_target_pairs={{8,0},{12,4},{16,24},{20,28},{9,1},{13,5},{17,25},{21,29},{10,2},{... | collective-permute-start | bytes 786440 | tf_op jit(solution)/shard_map/ppermute | solution.py:343
  167.7 1.4 collective-permute-start.32
  169.9 14.6 %collective-permute-start.33 = (f32[64,128]{1,0:T(8,128)S(1)}, f32[64,128]{1,0:T(8,128)S(1)}, u32[]{:S(2)}, u32[]{:S(2)}) collective-permute-start(f32[64,128]{1,0:T(8,128)S(1)} %add.119), channel_id=1, source_target_pairs={{0,1},{1,2},{2,3},{3,0},{4,5},{5,6},{6,7},{7,4},{8,9},{9,10},{10,1... | collective-permute-start | bytes 98312 | tf_op jit(solution)/shard_map/ppermute | solution.py:332
  172.2 12.4 %collective-permute-start.34 = (f32[64,128]{1,0:T(8,128)S(1)}, f32[64,128]{1,0:T(8,128)S(1)}, u32[]{:S(2)}, u32[]{:S(2)}) collective-permute-start(f32[64,128]{1,0:T(8,128)S(1)} %add.119), channel_id=1, source_target_pairs={{0,2},{1,3},{2,0},{3,1},{4,6},{5,7},{6,4},{7,5},{8,10},{9,11},{10,... | collective-permute-start | bytes 98312 | tf_op jit(solution)/shard_map/ppermute | solution.py:332
  172.7 11.9 %collective-permute-start.35 = (f32[64,128]{1,0:T(8,128)S(1)}, f32[64,128]{1,0:T(8,128)S(1)}, u32[]{:S(2)}, u32[]{:S(2)}) collective-permute-start(f32[64,128]{1,0:T(8,128)S(1)} %add.119), channel_id=1, source_target_pairs={{0,3},{1,0},{2,1},{3,2},{4,7},{5,4},{6,5},{7,6},{8,11},{9,8},{10,9... | collective-permute-start | bytes 98312 | tf_op jit(solution)/shard_map/ppermute | solution.py:332
  (8 other events, 14.6 us)

commit v2 on v1

v2 whole, which is shorter than its diff:
```python
import functools

import jax
import jax.numpy as jnp
from jax import lax
from jax.experimental import pallas as pl
from jax.experimental.pallas import tpu as pltpu
from jax.sharding import PartitionSpec as P


F32, BF16 = jnp.float32, jnp.bfloat16
HIGHEST = lax.Precision.HIGHEST
NT = (((1,), (1,)), ((), ()))


def split(values):
    high = values.astype(BF16)
    return high, (values - high.astype(F32)).astype(BF16)


def stack_split(blocks):
    pairs = [split(block) for block in blocks]
    return jnp.concatenate([pair[0] for pair in pairs] + [pair[1] for pair in pairs], axis=0)


def cost(flops, transferred):
    return pl.CostEstimate(flops=int(flops), bytes_accessed=int(transferred), transcendentals=0)


def whole(shape):
    return pl.BlockSpec(shape, lambda *_: (0,) * len(shape))


def nmr_body(blocks, swept, core_ref, chip_ref, *refs):
    spectra_refs, ppm_refs = refs[: 2 * blocks], refs[2 * blocks : 4 * blocks]
    mz_ref, part_ref, keep_ref, send_ref, *parcels = refs[4 * blocks : -1]
    total = refs[-1]
    piece = pl.program_id(0)
    rank = mz_ref.shape[0]

    @pl.when(piece == 0)
    def _():
        total[...] = jnp.zeros_like(total)
        channels = stack_split([mz_ref[...]])
        products = lax.dot_general(channels, channels, NT, preferred_element_type=F32)
        rows = products[:rank] + products[rank:]
        part_ref[:, rank:] = jnp.zeros_like(part_ref[:, rank:])
        part_ref[rank:, rank:] = rows[:, :rank] + rows[:, rank:]

    halves = [
        jnp.concatenate([spectra_refs[2 * b + core][...] for b in range(blocks)], axis=1) for core in (0, 1)
    ]
    values = jnp.concatenate(halves, axis=1)
    positions = stack_split([jnp.concatenate([ref[...] for core in (0, 1) for ref in ppm_refs[core::2]], axis=1)])
    left = jnp.concatenate([stack_split([values]), positions[:rank]], axis=0)
    total[...] += lax.dot_general(left, positions, NT, preferred_element_type=F32)

    for core in (0, 1):

        @pl.when(core_ref[0] == core)
        def _():
            keep_ref[0] = halves[core]
            send_ref[0] = halves[1 - core]

    if parcels:
        width = parcels[0].shape[3]

        @pl.when(piece >= swept)
        def _():
            for step, parcel in enumerate(parcels, 1):
                columns = pl.ds(pl.multiple_of((chip_ref[0] ^ step) * width, width), width)
                parcel[0, 0] = keep_ref[0, :, columns]
                parcel[0, 1] = send_ref[0, :, columns]

    @pl.when(piece == pl.num_programs(0) - 1)
    def _():
        samples = spectra_refs[0].shape[0]
        products = total[...]
        fit = products[:samples] + products[samples : 2 * samples]
        gram = products[2 * samples :]
        mixed = gram[:, rank:]
        part_ref[:rank, :rank] = fit[:, :rank] + fit[:, rank:]
        part_ref[rank:, :rank] = gram[:, :rank] + (mixed + mixed.T)


def nmr_pass(core, chip, spectra, ppm_factor, mz_factor, blocks, pieces, swept):
    samples, positions = spectra.shape
    rank, channels = mz_factor.shape
    width = positions // (2 * blocks * pieces)

    def columns(rows):
        return [
            pl.BlockSpec((rows, width), functools.partial(lambda b, k, c, h: (0, b * pieces + k), b))
            for b in range(2 * blocks)
        ]

    sorted_shape = jax.ShapeDtypeStruct((pieces, samples, blocks * width), F32)
    parcels = blocks - 1 if swept < pieces else 0
    parcel_shape = jax.ShapeDtypeStruct((pieces - swept, 2, samples, width), F32)
    return pl.pallas_call(
        functools.partial(nmr_body, blocks, swept),
        name="nmr_pass",
        grid_spec=pltpu.PrefetchScalarGridSpec(
            num_scalar_prefetch=2,
            grid=(pieces,),
            in_specs=columns(samples) + columns(rank) + [whole((rank, channels))],
            out_specs=[whole((2 * rank, 2 * rank))]
            + [pl.BlockSpec((1, samples, blocks * width), lambda k, c, h: (k, 0, 0))] * 2
            + [pl.BlockSpec((1, 2, samples, width), lambda k, c, h: (jnp.maximum(k - swept, 0), 0, 0, 0))] * parcels,
            scratch_shapes=[pltpu.VMEM((2 * samples + rank, 2 * rank), F32)],
        ),
        out_shape=[jax.ShapeDtypeStruct((2 * rank, 2 * rank), F32), sorted_shape, sorted_shape]
        + [parcel_shape] * parcels,
        cost_estimate=cost(2 * 256 * 256 * positions, 4 * 3 * 64 * positions),
    )(core, chip, *([spectra] * (2 * blocks)), *([ppm_factor] * (2 * blocks)), mz_factor)


def lcms_body(lcms_ref, scan_ref, mz_ref, part_ref, out_ref, weights, scans):
    rank = mz_ref.shape[0]
    step = pl.program_id(0)
    count, steps, channels = lcms_ref.shape

    @pl.when(step == 0)
    def _():
        high, low = split(mz_ref[...].T)
        weights[...] = jnp.concatenate([high, low], axis=1)
        scan = scan_ref[...].astype(BF16).astype(F32).T
        scans[...] = jnp.concatenate([scan, scan], axis=1)
        out_ref[rank:, :] = part_ref[rank:, :]

    inner = jnp.dot(
        lcms_ref[...].reshape(count * steps, channels), weights[...], preferred_element_type=F32
    )
    sums = jnp.sum(inner.reshape(count, steps, 2 * rank) * scans[...][None], axis=1)
    rows = pl.ds(pl.multiple_of(step * count, count), count)
    out_ref[rows, :] = sums + pltpu.roll(sums, rank, 1) + part_ref[rows, :]


def lcms_pass(lcms, scan_factor, mz_factor, part):
    samples, steps, channels = lcms.shape
    rank = mz_factor.shape[0]
    count = 8
    return pl.pallas_call(
        lcms_body,
        name="lcms_pass",
        grid=(samples // count,),
        in_specs=[
            pl.BlockSpec((count, steps, channels), lambda i: (i, 0, 0)),
            whole(scan_factor.shape),
            whole(mz_factor.shape),
            whole(part.shape),
        ],
        out_specs=whole(part.shape),
        out_shape=jax.ShapeDtypeStruct(part.shape, F32),
        scratch_shapes=[
            pltpu.VMEM((channels, 2 * rank), BF16),
            pltpu.VMEM((steps, 2 * rank), F32),
        ],
        cost_estimate=cost(2 * samples * steps * channels * 256, 2 * samples * steps * channels),
    )(lcms, scan_factor, mz_factor, part)


def first_body(own_pack, other_pack, own_ref, other_ref, left_ref, rows_ref, out_ref):
    rank, columns = rows_ref.shape[1] // 2, own_ref.shape[2]
    samples = own_ref.shape[1]
    rows = jnp.concatenate([own_pack[:samples, :rank], other_pack[:samples, :rank]], axis=1)
    rows_ref[...] = rows
    left = wide_rows(rows)
    left_ref[...] = left
    sides = [(own_ref[0], other_ref[0], 0), (rows[:, :rank], rows[:, rank:], columns)]
    for own, other, start in sides:
        products = jnp.dot(left, stack_split([own, other]), preferred_element_type=F32)
        out_ref[:, start : start + own.shape[1]] = products[:rank] + products[rank:]
    out_ref[:, columns + rank :] = jnp.zeros_like(out_ref[:, columns + rank :])


def wide_rows(rows):
    rank = rows.shape[1] // 2
    turned = rows.T
    return jnp.concatenate(
        [
            jnp.concatenate([part[:rank], part[rank:], part[:rank], part[rank:]], axis=1)
            for part in split(turned)
        ],
        axis=0,
    )


def first_pass(own_pack, other_pack, own, other):
    _, samples, columns = own.shape
    rank = own_pack.shape[1] // 2
    piece = pl.BlockSpec((1, samples, columns), lambda k: (0, 0, 0))
    return pl.pallas_call(
        first_body,
        name="first_pass",
        grid=(1,),
        in_specs=[whole(own_pack.shape)] * 2 + [piece] * 2,
        out_specs=[
            whole((2 * rank, 4 * samples)),
            whole((samples, 2 * rank)),
            whole((rank, columns + 2 * rank)),
        ],
        out_shape=[
            jax.ShapeDtypeStruct((2 * rank, 4 * samples), BF16),
            jax.ShapeDtypeStruct((samples, 2 * rank), F32),
            pltpu.VMEM((rank, columns + 2 * rank), F32),
        ],
        cost_estimate=cost(2 * 256 * 256 * columns, 12 * 64 * columns),
    )(own_pack, other_pack, own, other)


def project_body(left_ref, own_ref, other_ref, *outs):
    rank = left_ref.shape[0] // 2
    right = stack_split([own_ref[0], other_ref[0]])
    products = jnp.dot(left_ref[...], right, preferred_element_type=F32)
    values = products[:rank] + products[rank:]
    for k, out_ref in enumerate(outs):

        @pl.when(pl.program_id(0) == k)
        def _():
            out_ref[...] = values


def project_pass(left, own, other, first, count):
    _, samples, columns = own.shape
    rank = left.shape[0] // 2
    piece = pl.BlockSpec((1, samples, columns), lambda k: (first + k, 0, 0))
    return pl.pallas_call(
        project_body,
        name="project_pass",
        grid=(count,),
        in_specs=[whole(left.shape), piece, piece],
        out_specs=[whole((rank, columns))] * count,
        out_shape=[pltpu.VMEM((rank, columns), F32)] * count,
        cost_estimate=cost(2 * 256 * 256 * columns * count, 12 * 64 * columns * count),
    )(left, own, other)


def fit_body(count, earlier, *refs):
    sweeps, refs = refs[: 4 * count], refs[4 * count :]
    own_ref, other_ref, sums_ref = refs[0], refs[1], refs[2 + earlier]
    _, samples, _ = own_ref.shape
    rank = sums_ref.shape[2] // 2
    sums = None
    for k in range(count):
        part, inward, across, outward = (ref[...] for ref in sweeps[4 * k : 4 * k + 4])
        total = part + inward + across + outward
        refs[3 + earlier + k][...] = total
        right = stack_split([total])
        rows = jnp.concatenate([stack_split([own_ref[k], other_ref[k]]), right], axis=0)
        products = lax.dot_general(rows, right, NT, preferred_element_type=F32)
        sums = products if sums is None else sums + products
    sums = sums[:, :rank] + sums[:, rank:]
    gram = sums[4 * samples : 4 * samples + rank] + sums[4 * samples + rank :]
    for side in (0, 1):
        fit = sums[side * samples : (side + 1) * samples] + sums[(side + 2) * samples : (side + 3) * samples]
        total = jnp.concatenate([fit, gram], axis=1)
        for ref in refs[2 : 2 + earlier]:
            total = total + ref[side]
        sums_ref[side] = total


def fit_pass(sweeps, earlier, own, other, first):
    _, samples, columns = own.shape
    count, rank = len(sweeps), sweeps[0][0].shape[0]
    pieces = pl.BlockSpec((count, samples, columns), lambda i: (first // count, 0, 0))
    assert first % count == 0
    arrays = [array for sweep in sweeps for array in sweep]
    sums_shape = (2, samples, 2 * rank)
    sums, *totals = pl.pallas_call(
        functools.partial(fit_body, count, len(earlier)),
        grid=(1,),
        in_specs=[whole((rank, columns))] * len(arrays)
        + [pieces, pieces]
        + [whole(sums_shape)] * len(earlier),
        out_specs=[whole(sums_shape)] + [whole((rank, columns))] * count,
        out_shape=[jax.ShapeDtypeStruct(sums_shape, F32)]
        + [jax.ShapeDtypeStruct((rank, columns), F32)] * count,
        cost_estimate=cost(2 * 384 * 256 * columns * count, 32 * 64 * columns * count),
    )(*arrays, own, other, *earlier)
    return sums, totals


def eliminate(matrix, right):
    size, ahead = matrix.shape[0], 4
    whole_rows = jnp.concatenate([matrix, right], axis=1)
    groups = [whole_rows[i : i + 8] for i in range(0, size, 8)]
    lanes = whole_rows.shape[1]
    sublane = lax.broadcasted_iota(jnp.int32, (8, lanes), 0)

    def reduce(targets, columns, home, place, inverse):
        row = jnp.broadcast_to(targets[home][place : place + 1], (8, lanes)) * inverse
        reduced = [target - column * row for target, column in zip(targets, columns)]
        reduced[home] = jnp.where(sublane == place, row, reduced[home])
        return reduced

    for base in range(0, size, ahead):
        spread = [
            [jnp.broadcast_to(group[:, k : k + 1], (8, lanes)) for group in groups]
            for k in range(base, base + ahead)
        ]
        for j in range(ahead):
            home, place = divmod(base + j, 8)
            inverse = 1.0 / jnp.broadcast_to(spread[j][home][place : place + 1], (8, lanes))
            for i in range(j + 1, ahead):
                spread[i] = reduce(spread[i], spread[j], home, place, inverse)
            groups = reduce(groups, spread[j], home, place, inverse)
    return jnp.concatenate(groups, axis=0)[:, size:]


def dot32(a, b, dims=(((1,), (0,)), ((), ()))):
    return lax.dot_general(a, b, dims, precision=HIGHEST, preferred_element_type=F32)


def mix_body(*refs):
    parts, (pack_ref, scan_ref, out_ref, lcms_gram_ref) = refs[:-4], refs[-4:]
    rank = out_ref.shape[0]
    scan = scan_ref[...]
    lcms_gram = dot32(scan, scan, NT) * pack_ref[rank:, rank:]
    lcms_gram_ref[...] = lcms_gram
    gram = sum(part[...] for part in parts)
    out_ref[...] = eliminate(gram[:, :rank], lcms_gram + pack_ref[rank:, :rank])


def mix_pass(sweep, pack, scan_factor, columns):
    rank = scan_factor.shape[0]
    shape = jax.ShapeDtypeStruct((rank, rank), F32)
    return pl.pallas_call(
        mix_body,
        name="mix_pass",
        grid=(1,),
        in_specs=[pl.BlockSpec((rank, 2 * rank), lambda i: (0, columns // (2 * rank)))] * len(sweep)
        + [whole(pack.shape), whole(scan_factor.shape)],
        out_specs=[whole(shape.shape)] * 2,
        out_shape=[shape, shape],
        cost_estimate=cost(1 << 22, 65536),
    )(*sweep, pack, scan_factor)


def sample_body(fit_ref, mix_ref, lcms_gram_ref, pack_ref, out_ref):
    rank = mix_ref.shape[0]
    mix = mix_ref[...]
    fit = dot32(fit_ref[:, :rank], mix)
    new_gram = dot32(mix, dot32(fit_ref[:, rank:], mix), (((0,), (0,)), ((), ())))
    right = pack_ref[: fit.shape[0], rank:] + fit
    out_ref[...] = eliminate(lcms_gram_ref[...] + new_gram, right.T).T


def sample_pass(fit, mix, lcms_gram, pack):
    return pl.pallas_call(
        sample_body,
        name="sample_pass",
        out_shape=jax.ShapeDtypeStruct((fit.shape[0], mix.shape[0]), F32),
        cost_estimate=cost(1 << 22, 65536),
    )(fit, mix, lcms_gram, pack)


def ppm_body(chip_ref, mix_ref, *refs):
    out_ref = refs[-1]
    rank = mix_ref.shape[0]
    high, low = split(mix_ref[...].T)
    left = jnp.concatenate(
        [jnp.concatenate([high, high], axis=1), jnp.concatenate([low, low], axis=1)], axis=0
    )
    start = 0
    for ref in refs[:-1]:
        products = jnp.dot(left, stack_split([ref[...]]), preferred_element_type=F32)
        out_ref[:, start : start + ref.shape[1]] = products[:rank] + products[rank:]
        start += ref.shape[1]


def ppm_pass(chip, mix, totals, direct, width):
    rank, pieces = mix.shape[0], len(totals)
    directs = [] if direct is None else [direct]
    columns = pieces * width + sum(d.shape[1] for d in directs)
    return pl.pallas_call(
        ppm_body,
        name="ppm_pass",
        grid_spec=pltpu.PrefetchScalarGridSpec(
            num_scalar_prefetch=1,
            grid=(1,),
            in_specs=[whole(mix.shape)]
            + [pl.BlockSpec((rank, width), lambda i, c: (0, c[0])) for _ in totals]
            + [whole(d.shape) for d in directs],
            out_specs=whole((rank, columns)),
        ),
        out_shape=jax.ShapeDtypeStruct((rank, columns), F32),
        cost_estimate=cost(2 * 256 * 128 * columns, 8 * 64 * columns),
    )(chip, mix, *totals, *directs)


def direct_body(chips, count, chip_ref, *refs):
    rows, refs = refs[:chips], refs[chips:]
    own, other, refs = refs[:count], refs[count : 2 * count], refs[2 * count :]
    came, swapped, projected_ref, sums_refs = refs[: chips - 1], refs[chips - 1 : 2 * chips - 2], refs[2 * chips - 2], refs[2 * chips - 1 :]
    samples, width = own[0].shape[1:]
    rank = rows[0].shape[1] // 2
    left = [wide_rows(pair[...]) for pair in rows]
    sums = [None] * chips
    gram = None
    for j in range(count):
        stacks = [stack_split([own[j][0], other[j][0]])] + [
            stack_split([came[x][j, 0], swapped[x][j, 0]]) for x in range(chips - 1)
        ]
        products = sum(
            jnp.dot(left[x], stacks[x], preferred_element_type=F32) for x in range(chips)
        )
        values = products[:rank] + products[rank:]
        projected_ref[:, j * width : (j + 1) * width] = values
        right = stack_split([values])
        for x in range(chips):
            fit = lax.dot_general(stacks[x], right, NT, preferred_element_type=F32)
            sums[x] = fit if j == 0 else sums[x] + fit
        square = lax.dot_general(right, right, NT, preferred_element_type=F32)
        gram = square if j == 0 else gram + square
    gram = gram[:rank] + gram[rank:]
    gram = gram[:, :rank] + gram[:, rank:]
    for x in range(chips):
        fit = sums[x][: 2 * samples] + sums[x][2 * samples :]
        fit = fit[:, :rank] + fit[:, rank:]
        for side in (0, 1):
            sums_refs[x][side] = jnp.concatenate([fit[side * samples : (side + 1) * samples], gram], axis=1)


def direct_pass(chip, rows, own, other, came, swapped, first):
    chips, count = len(rows), own.shape[0] - first
    samples, rank = own.shape[1], rows[0].shape[1] // 2
    width = came[0].shape[3]
    pieces = [
        pl.BlockSpec((1, samples, width), functools.partial(lambda j, i, c: (first + j, 0, c[0]), j))
        for j in range(count)
    ]
    return pl.pallas_call(
        functools.partial(direct_body, chips, count),
        name="direct_pass",
        grid_spec=pltpu.PrefetchScalarGridSpec(
            num_scalar_prefetch=1,
            grid=(1,),
            in_specs=[whole(r.shape) for r in rows]
            + pieces
            + pieces
            + [pl.BlockSpec((count, 1, samples, width), lambda i, c: (0, 0, 0, 0))] * (chips - 1)
            + [pl.BlockSpec((count, 1, samples, width), lambda i, c: (0, 1, 0, 0))] * (chips - 1),
            out_specs=[whole((rank, count * width))] + [whole((2, samples, 2 * rank))] * chips,
        ),
        out_shape=[jax.ShapeDtypeStruct((rank, count * width), F32)]
        + [jax.ShapeDtypeStruct((2, samples, 2 * rank), F32)] * chips,
        cost_estimate=cost(2 * 512 * 512 * count * width * 2, 4 * 512 * count * width),
    )(chip, *rows, *([own] * count), *([other] * count), *came, *swapped)


def sum_over_mz(values, count):
    result = values
    for step in range(1, count):
        hops = [(i, (i + step) % count) for i in range(count)]
        result = result + lax.ppermute(values, "mz", hops)
    return result


def from_chips(values, runs):
    chips = runs // 2
    return [
        lax.ppermute(values[step - 1], "run", [(i, i ^ (2 * step)) for i in range(runs)])
        for step in range(1, chips)
    ]


def sum_over_chips(parts, runs):
    lines = [4 * line for line in range(runs // 8)]

    def send(values, pairs):
        hops = [
            (2 * (line + a) + core, 2 * (line + b) + core) for line in lines for a, b in pairs for core in (0, 1)
        ]
        return lax.ppermute(values, "run", hops)

    sweeps = []
    for part in parts:
        inward = send(part, [(0, 1), (3, 2)])
        across = send(part + inward, [(1, 2), (2, 1)])
        outward = send(part + across, [(1, 0), (2, 3)])
        if len(lines) > 1:
            line_total = part + inward + across + outward
            for step in range(1, len(lines)):
                shifted = [(i, (i + 8 * step) % runs) for i in range(runs)]
                part = part + lax.ppermute(line_total, "run", shifted)
        sweeps.append((part, inward, across, outward))
    return sweeps


def per_device(runs, mzs, lcms, spectra, scan_factor, mz_factor, ppm_factor):
    _, positions = spectra.shape
    chips = runs // 2
    width = positions // runs
    pieces = min(8, width // 128)
    swept = pieces // 2 if chips == 4 else pieces
    width = width // pieces
    run = lax.axis_index("run").astype(jnp.int32)
    core, chip = (run % 2).reshape(1), (run // 2).reshape(1)
    swap = [(i, i ^ 1) for i in range(runs)]

    part, own, leaving, *parcels = nmr_pass(core, chip, spectra, ppm_factor, mz_factor, chips, pieces, swept)
    came = from_chips(parcels, runs) if parcels else []
    other = lax.ppermute(leaving, "run", swap)
    pack = lcms_pass(lcms, scan_factor, mz_factor, part)
    pack = sum_over_mz(pack, mzs)
    left, rows, first = first_pass(pack, lax.ppermute(pack, "run", swap), own, other)
    sweeps = sum_over_chips([first, *project_pass(left, own, other, 1, swept - 1)], runs)
    projected, direct = None, []
    if parcels:
        rows = [rows] + from_chips([rows] * (chips - 1), runs)
        swapped = [lax.ppermute(array, "run", swap) for array in came]
        projected, *sums = direct_pass(chip, rows, own, other, came, swapped, swept)
        direct = sums[:1] + from_chips(sums[1:], runs)
    totals, sums = [], []
    for k in range(0, swept, 2):
        earlier = sums + (direct if k + 2 == swept else [])
        sums, done = fit_pass(sweeps[k : k + 2], earlier, own, other, k)
        totals, sums = totals + done, [sums]
    mix, lcms_gram = mix_pass(sweeps[0], pack, scan_factor, own.shape[2])
    ppm_new = ppm_pass(chip, mix, totals, projected, width)
    fit = sum_over_mz(sums[0][0] + lax.ppermute(sums[0], "run", swap)[1], mzs)
    sample_factor = sample_pass(fit, mix, lcms_gram, pack)
    return (sample_factor, ppm_new)


def solution(mesh):
    runs, mzs = mesh.shape["run"], mesh.shape["mz"]

    def whole_step(lcms, spectra, scan_factor, mz_factor, ppm_factor):
        return per_device(runs, mzs, lcms, spectra, scan_factor, mz_factor, ppm_factor)

    return jax.shard_map(
        whole_step,
        mesh=mesh,
        in_specs=(P("run", None, "mz"), P("run", "mz"), P(), P(None, "mz"), P(None, "mz")),
        out_specs=(P("run", None), P(None, ("mz", "run"))),
        check_vma=False,
    )
```

time: 195 us -> 167 us (0.86)
  waiting for transfers between devices: 61 us -> 37.9 us
  starting transfers between devices: 50.5 us -> 65 us
  Pallas kernels: 68.4 us -> 55.4 us
  local copies, waits for them, and re-layouts: 4.1 us -> 2.07 us
    ppermute x24 -> x12, waiting for transfers between devices: 55.7 us -> 6.73 us  [send(): return lax.ppermute(values, 'run', hops)]
    ppermute x11 -> x20, starting transfers between devices: 12.2 us -> 48.8 us  [the longest x9 38.8 us: from_chips(): lax.ppermute(values[step - 1], 'run', [(i, i ^ 2 * step) for i in range(r...]
    ppermute x11 -> x20, waiting for transfers between devices: 5.21 us -> 31.1 us  [the longest x9 27.8 us: from_chips(): lax.ppermute(values[step - 1], 'run', [(i, i ^ 2 * step) for i in range(r...]
    ppermute x24 -> x12, starting transfers between devices: 37.7 us -> 15.6 us  [send(): return lax.ppermute(values, 'run', hops)]
    pallas_call x10 -> x8, Pallas kernels: 42.8 us -> 33 us  [the longest x1 9.9 us: nmr_pass(): pl.pallas_call(functools.partial(nmr_body, blocks, swept), name='nmr_pass...]
    pallas_call x1, Pallas kernels: 7.55 us -> 5.3 us  [sample_pass(): pl.pallas_call(sample_body, name='sample_pass', out_shape=jax.ShapeDtypeS...]
  transfers between devices with their start and end apart: 36 -> 33, of which waited for: 18 -> 9; matrix products, arithmetic and copies ran while one was open for 3% -> 2% of each run, Pallas kernels for 21% -> 22%
where the time goes in v2:
time: 167 us; the launch traced here: 166 us
  starting transfers between devices  65 us (39%)
  Pallas kernels  55.4 us (33%)
  waiting for transfers between devices  37.9 us (23%)
  other arithmetic  4.62 us (3%)
  local copies, waits for them, and re-layouts  2.07 us (1%)
    ppermute x9, starting transfers between devices, from_chips(): lax.ppermute(values[step - 1], 'run', [(i, i ^ 2 * step) for i in range(r...  38.8 us
    ppermute x9, waiting for transfers between devices, from_chips(): lax.ppermute(values[step - 1], 'run', [(i, i ^ 2 * step) for i in range(r...  27.8 us
    pallas_call x1, Pallas kernels, lcms_pass(): pl.pallas_call(lcms_body, name='lcms_pass', grid=(samples // count,), in_...  17.1 us
    ppermute x12, starting transfers between devices, send(): return lax.ppermute(values, 'run', hops)  15.6 us
    pallas_call x1, Pallas kernels, nmr_pass(): pl.pallas_call(functools.partial(nmr_body, blocks, swept), name='nmr_pass...  9.9 us
    ppermute x6, starting transfers between devices, sum_over_mz(): result = result + lax.ppermute(values, 'mz', hops)  8.85 us
    ppermute x12, waiting for transfers between devices, send(): return lax.ppermute(values, 'run', hops)  6.73 us
    pallas_call x2, Pallas kernels, fit_pass(): pl.pallas_call(functools.partial(fit_body, count, len(earlier)), grid=(1,...  6.49 us
  transfers between devices with their start and end apart: 33, of which 9 were waited for; matrix products, arithmetic and copies ran while one was open for 2% of the time, Pallas kernels for 22%

profile of v2, /device:TPU:0, one launch (start us, length us, event | category | flops | bytes accessed | tf_op | source)
XLA Modules:
  0.0 166.1 jit_solution(4817681239130683615)
XLA Ops:
  0.6 9.9 %nmr_pass.1 = (f32[128,128]{1,0:T(8,128)}, f32[8,64,1024]{2,1,0:T(8,128)}, f32[8,64,1024]{2,1,0:T(8,128)}, f32[4,2,64,256]{3,2,1,0:T(8,128)}, f32[4,2,64,256]{3,2,1,0:T(8,128)}, /*index=5*/f32[4,2,64,256]{3,2,1,0:T(8,128)}) custom-call(s32[1]{0:T(128)} %bitcast.core_ref, s32[1]{0:T(128)} %bitcast.1.chip_ref, f32[64,16384]{1,0:T(8,128)} %refs_7_.1, ...), custom_call_target="tpu_custom_call" | custom-call | flops 2147483648 | bytes 12582912 | tf_op jit(solution)/shard_map/nmr_pass/pallas_call | solution.py:100
  10.6 0.6 collective-permute-start.4
  11.2 2.6 %collective-permute-start.20 = (f32[4,2,64,256]{3,2,1,0:T(8,128)}, f32[4,2,64,256]{3,2,1,0:T(8,128)}, u32[]{:S(2)}, u32[]{:S(2)}) collective-permute-start(f32[4,2,64,256]{3,2,1,0:T(8,128)} %get-tuple-element.37), channel_id=1, source_target_pairs={{0,8},{4,12},{8,0},{12,4},{16,24},{20,28},{24,16},{28,20},{1,9},{5... | collective-permute-start | bytes 1572872 | tf_op jit(solution)/shard_map/ppermute | solution.py:463
  13.8 17.1 %lcms_pass.1 = f32[128,128]{1,0:T(8,128)} custom-call(bf16[64,256,1024]{2,1,0:T(8,128)(2,1)} %lcms_ref.1, f32[64,256]{1,0:T(8,128)} %refs_5_.3, f32[64,1024]{1,0:T(8,128)} %mz_ref.1, f32[128,128]{1,0:T(8,128)} %get-tuple-element.27.part_ref), custom_call_target="tpu_custom_call" | custom-call | flops 8589934592 | bytes 33554432 | tf_op jit(solution)/shard_map/lcms_pass/pallas_call | solution.py:143
  30.8 1.5 collective-permute-start
  32.3 1.5 collective-permute-start.1
  33.8 1.4 collective-permute-start.2
  35.3 1.0 collective-permute-done
  36.2 2.6 %collective-permute-start.21 = (f32[4,2,64,256]{3,2,1,0:T(8,128)}, f32[4,2,64,256]{3,2,1,0:T(8,128)}, u32[]{:S(2)}, u32[]{:S(2)}) collective-permute-start(f32[4,2,64,256]{3,2,1,0:T(8,128)} %get-tuple-element.38), channel_id=1, source_target_pairs={{0,16},{4,20},{8,24},{12,28},{16,0},{20,4},{24,8},{28,12},{1,17},{... | collective-permute-start | bytes 1572872 | tf_op jit(solution)/shard_map/ppermute | solution.py:463
  38.8 1.2 collective-permute-start.22
  40.0 0.0 collective-permute-done.20.refs_12_
  40.0 0.0 collective-permute-start.23
  40.0 0.0 collective-permute-done.2
  40.0 0.9 add_add_fusion.own_pack.refs_4_.pack_ref
  40.9 0.6 collective-permute-start.3
  41.4 0.9 collective-permute-done.3.other_pack
  42.3 0.0 collective-permute-done.4.other_ref.refs_9_.refs_8_.refs_10_.refs_11_
  42.3 0.6 copy-done.18
  43.0 0.8 copy-done.4
  43.7 2.0 %first_pass.1 = (bf16[128,256]{1,0:T(8,128)(2,1)}, f32[64,128]{1,0:T(8,128)}, f32[64,1152]{1,0:T(8,128)S(1)}) custom-call(f32[128,128]{1,0:T(8,128)} %copy-done.8, f32[128,128]{1,0:T(8,128)} %copy-done.18, f32[8,64,1024]{2,1,0:T(8,128)} %get-tuple-element.28.own_ref.refs_8_.refs_4_.refs_5_.refs_6_.refs_7_, f32[8,64,1024]{2,1,0:T(8,128)} %copy-done.4), custom_call_target="tpu_custom_call" | custom-call | flops 134217728 | bytes 786432 | tf_op jit(solution)/shard_map/first_pass/pallas_call | solution.py:193
  45.7 2.6 %collective-permute-start.11 = (f32[64,1152]{1,0:T(8,128)S(1)}, f32[64,1152]{1,0:T(8,128)S(1)}, u32[]{:S(2)}, u32[]{:S(2)}) collective-permute-start(f32[64,1152]{1,0:T(8,128)S(1)} %get-tuple-element.33.refs_0_), channel_id=1, source_target_pairs={{0,8},{4,12},{24,16},{28,20},{1,9},{5,13},{25,17},{29,21},{2,10},{... | collective-permute-start | bytes 884744 | tf_op jit(solution)/shard_map/ppermute | solution.py:475
  48.3 2.6 %project_pass.1 = (f32[64,1024]{1,0:T(8,128)S(1)}, f32[64,1024]{1,0:T(8,128)S(1)}, f32[64,1024]{1,0:T(8,128)S(1)}) custom-call(bf16[128,256]{1,0:T(8,128)(2,1)} %get-tuple-element.30.left_ref, f32[8,64,1024]{2,1,0:T(8,128)} %get-tuple-element.28.own_ref.refs_8_.refs_4_.refs_5_.refs_6_.refs_7_, f32[8,64,1024]{2,1,0:T(8,128)} %copy-done.4), custom_call_target="tpu_custom_call" | custom-call | flops 402653184 | bytes 2359296 | tf_op jit(solution)/shard_map/project_pass/pallas_call | solution.py:228
  50.9 0.0 copy-start.19
  51.0 1.4 collective-permute-start.14
  52.4 20.6 %collective-permute-done.21.refs_13_ = f32[4,2,64,256]{3,2,1,0:T(8,128)} collective-permute-done((f32[4,2,64,256]{3,2,1,0:T(8,128)}, f32[4,2,64,256]{3,2,1,0:T(8,128)}, u32[]{:S(2)}, u32[]{:S(2)}) %collective-permute-start.21) | collective-permute-done | bytes 524320 | tf_op jit(solution)/shard_map/ppermute | solution.py:463
  73.0 2.5 %collective-permute-start.8 = (f32[64,1024]{1,0:T(8,128)S(1)}, f32[64,1024]{1,0:T(8,128)S(1)}, u32[]{:S(2)}, u32[]{:S(2)}) collective-permute-start(f32[64,1024]{1,0:T(8,128)S(1)} %get-tuple-element.32.refs_4_), channel_id=1, source_target_pairs={{0,8},{4,12},{24,16},{28,20},{1,9},{5,13},{25,17},{29,21},{2,10},{... | collective-permute-start | bytes 786440 | tf_op jit(solution)/shard_map/ppermute | solution.py:475
  75.5 1.3 collective-permute-start.5
  76.8 0.7 collective-permute-start.12
  77.5 0.1 collective-permute-start.24
  77.6 0.5 collective-permute-start.25
  78.1 4.0 %collective-permute-done.8.refs_5_ = f32[64,1024]{1,0:T(8,128)S(1)} collective-permute-done((f32[64,1024]{1,0:T(8,128)S(1)}, f32[64,1024]{1,0:T(8,128)S(1)}, u32[]{:S(2)}, u32[]{:S(2)}) %collective-permute-start.8) | collective-permute-done | bytes 262176 | tf_op jit(solution)/shard_map/ppermute | solution.py:475
  82.1 0.7 collective-permute-start.15
  82.8 2.7 %collective-permute-done.5.refs_1_ = f32[64,1024]{1,0:T(8,128)S(1)} collective-permute-done((f32[64,1024]{1,0:T(8,128)S(1)}, f32[64,1024]{1,0:T(8,128)S(1)}, u32[]{:S(2)}, u32[]{:S(2)}) %collective-permute-start.5) | collective-permute-done | bytes 262176 | tf_op jit(solution)/shard_map/ppermute | solution.py:475
  85.6 0.7 collective-permute-start.9
  86.3 0.7 collective-permute-start.6
  87.1 1.3 collective-permute-start.13
  88.4 0.7 add.64
  89.1 1.3 collective-permute-start.16
  90.4 21.7 %collective-permute-start.17 = (f32[64,128]{1,0:T(8,128)S(1)}, f32[64,128]{1,0:T(8,128)S(1)}, u32[]{:S(2)}, u32[]{:S(2)}) collective-permute-start(f32[64,128]{1,0:T(8,128)S(1)} %copy-done.19), channel_id=1, source_target_pairs={{0,8},{4,12},{8,0},{12,4},{16,24},{20,28},{24,16},{28,20},{1,9},{5... | collective-permute-start | bytes 98312 | tf_op jit(solution)/shard_map/ppermute | solution.py:463
  112.1 0.7 add.60
  112.9 0.7 add.58
  113.6 1.3 collective-permute-start.10
  114.9 1.3 collective-permute-start.7
  116.2 4.1 %collective-permute-start.18 = (f32[64,128]{1,0:T(8,128)S(1)}, f32[64,128]{1,0:T(8,128)S(1)}, u32[]{:S(2)}, u32[]{:S(2)}) collective-permute-start(f32[64,128]{1,0:T(8,128)S(1)} %copy-done.19), channel_id=1, source_target_pairs={{0,16},{4,20},{8,24},{12,28},{16,0},{20,4},{24,8},{28,12},{1,17},{... | collective-permute-start | bytes 98312 | tf_op jit(solution)/shard_map/ppermute | solution.py:463
  120.4 2.1 %collective-permute-done.18.refs_2_ = f32[64,128]{1,0:T(8,128)S(1)} collective-permute-done((f32[64,128]{1,0:T(8,128)S(1)}, f32[64,128]{1,0:T(8,128)S(1)}, u32[]{:S(2)}, u32[]{:S(2)}) %collective-permute-start.18) | collective-permute-done | bytes 32800 | tf_op jit(solution)/shard_map/ppermute | solution.py:463
  122.5 2.1 %collective-permute-start.19 = (f32[64,128]{1,0:T(8,128)S(1)}, f32[64,128]{1,0:T(8,128)}, u32[]{:S(2)}, u32[]{:S(2)}) collective-permute-start(f32[64,128]{1,0:T(8,128)S(1)} %copy-done.19), channel_id=1, source_target_pairs={{0,24},{4,28},{8,16},{12,20},{16,8},{20,12},{24,0},{28,4},{1,25},{... | collective-permute-start | bytes 98312 | tf_op jit(solution)/shard_map/ppermute | solution.py:463
  124.6 3.8 %collective-permute-done.19.refs_3_ = f32[64,128]{1,0:T(8,128)} collective-permute-done((f32[64,128]{1,0:T(8,128)S(1)}, f32[64,128]{1,0:T(8,128)}, u32[]{:S(2)}, u32[]{:S(2)}) %collective-permute-start.19) | collective-permute-done | bytes 32800 | tf_op jit(solution)/shard_map/ppermute | solution.py:463
  128.4 4.5 %direct_pass.1 = (f32[64,1024]{1,0:T(8,128)}, f32[2,64,128]{2,1,0:T(8,128)}, f32[2,64,128]{2,1,0:T(8,128)}, f32[2,64,128]{2,1,0:T(8,128)}, f32[2,64,128]{2,1,0:T(8,128)}) custom-call(s32[1]{0:T(128)} %bitcast.1.chip_ref, f32[64,128]{1,0:T(8,128)} %get-tuple-element.36.refs_0_, f32[64,128]{1,0:T(8,128)} %copy-done.20, f32[64,128]{1,0:T(8,128)} %copy-done.21, ...), custom_call_target="tpu_custom_call" | custom-call | flops 1073741824 | bytes 2097152 | tf_op jit(solution)/shard_map/direct_pass/pallas_call | solution.py:433
  133.0 0.9 collective-permute-start.26
  133.9 1.9 %collective-permute-start.27 = (f32[2,64,128]{2,1,0:T(8,128)}, f32[2,64,128]{2,1,0:T(8,128)S(1)}, u32[]{:S(2)}, u32[]{:S(2)}) collective-permute-start(f32[2,64,128]{2,1,0:T(8,128)} %get-tuple-element.42), channel_id=1, source_target_pairs={{0,16},{4,20},{8,24},{12,28},{16,0},{20,4},{24,8},{28,12},{1,17},{... | collective-permute-start | bytes 196616 | tf_op jit(solution)/shard_map/ppermute | solution.py:463
  135.8 1.7 %collective-permute-start.28 = (f32[2,64,128]{2,1,0:T(8,128)}, f32[2,64,128]{2,1,0:T(8,128)S(1)}, u32[]{:S(2)}, u32[]{:S(2)}) collective-permute-start(f32[2,64,128]{2,1,0:T(8,128)} %get-tuple-element.43), channel_id=1, source_target_pairs={{0,24},{4,28},{8,16},{12,20},{16,8},{20,12},{24,0},{28,4},{1,25},{... | collective-permute-start | bytes 196616 | tf_op jit(solution)/shard_map/ppermute | solution.py:463
  137.5 3.2 %shard_map.68 = (f32[2,64,128]{2,1,0:T(8,128)}, f32[64,1024]{1,0:T(8,128)}, f32[64,1024]{1,0:T(8,128)}) custom-call(f32[64,1152]{1,0:T(8,128)} %copy-done, f32[64,1152]{1,0:T(8,128)} %copy-done.5, f32[64,1152]{1,0:T(8,128)} %copy-done.6, f32[64,1152]{1,0:T(8,128)} %copy-done.7, f32[64,1024]{1,0:T(8,128)} %copy-done.3, f32[64,1024]{1,0:T(8,128)} %copy-done.11, ...), custom_call_target="tpu_custom_call" | custom-call | flops 402653184 | bytes 4194304 | tf_op jit(solution)/shard_map/pallas_call | solution.py:270
  140.7 1.3 collective-permute-done.28.refs_14_
  142.1 0.6 copy-done.17
  142.7 3.3 %shard_map.69 = (f32[2,64,128]{2,1,0:T(8,128)}, f32[64,1024]{1,0:T(8,128)}, f32[64,1024]{1,0:T(8,128)}) custom-call(f32[64,1024]{1,0:T(8,128)} %copy-done.1, f32[64,1024]{1,0:T(8,128)} %copy-done.10, f32[64,1024]{1,0:T(8,128)} %copy-done.13, f32[64,1024]{1,0:T(8,128)} %collective-permute-done.7.refs_3_, f32[64,1024]{1,0:T(8,128)} %copy-done.2, ...), custom_call_target="tpu_custom_call" | custom-call | flops 402653184 | bytes 4194304 | tf_op jit(solution)/shard_map/pallas_call | solution.py:270
  146.0 1.5 collective-permute-done.29
  147.4 0.8 fusion
  148.2 0.5 collective-permute-start.30
  148.7 1.5 collective-permute-start.31
  150.2 2.4 %collective-permute-start.32 = (f32[64,128]{1,0:T(8,128)S(1)}, f32[64,128]{1,0:T(8,128)S(1)}, u32[]{:S(2)}, u32[]{:S(2)}) collective-permute-start(f32[64,128]{1,0:T(8,128)S(1)} %fusion), channel_id=1, source_target_pairs={{0,3},{1,0},{2,1},{3,2},{4,7},{5,4},{6,5},{7,6},{8,11},{9,8},{10,9... | collective-permute-start | bytes 98312 | tf_op jit(solution)/shard_map/ppermute | solution.py:456
  152.6 5.2 %mix_pass.1 = (f32[64,64]{1,0:T(8,128)}, f32[64,64]{1,0:T(8,128)}) custom-call(f32[64,1152]{1,0:T(8,128)} %copy-done, f32[64,1152]{1,0:T(8,128)} %copy-done.5, f32[64,1152]{1,0:T(8,128)} %copy-done.6, f32[64,1152]{1,0:T(8,128)} %copy-done.7, f32[128,128]{1,0:T(8,128)} %copy-done.8, f32[64,256]{1,0:T(8,128)} %refs_5_.3), custom_call_target="tpu_custom_call" | custom-call | flops 4194304 | bytes 65536 | tf_op jit(solution)/shard_map/mix_pass/pallas_call | solution.py:328
  157.8 2.3 %ppm_pass.1 = f32[64,2048]{1,0:T(8,128)} custom-call(s32[1]{0:T(128)} %bitcast.1.chip_ref, f32[64,64]{1,0:T(8,128)} %get-tuple-element.45.mix_ref, f32[64,1024]{1,0:T(8,128)} %get-tuple-element.47.refs_0_, f32[64,1024]{1,0:T(8,128)} %get-tuple-element.48.refs_1_, f32[64,1024]{1,0:T(8,128)} %get-tuple-element.49.refs_2_, ...), custom_call_target="tpu_custom_call" | custom-call | flops 134217728 | bytes 1048576 | tf_op jit(solution)/shard_map/ppm_pass/pallas_call | solution.py:376
  160.2 0.6 add_add_fusion.1.fit_ref
  160.8 5.3 %sample_pass.1 = f32[64,64]{1,0:T(8,128)} custom-call(f32[64,128]{1,0:T(8,128)} %add_add_fusion.1.fit_ref, f32[64,64]{1,0:T(8,128)} %get-tuple-element.45.mix_ref, f32[64,64]{1,0:T(8,128)} %get-tuple-element.46.lcms_gram_ref, f32[128,128]{1,0:T(8,128)} %copy-done.8), custom_call_target="tpu_custom_call" | custom-call | flops 4194304 | bytes 65536 | tf_op jit(solution)/shard_map/sample_pass/pallas_call | solution.py:350
  (69 shorter events, 0.3 us)
Async XLA Ops:
  10.6 31.8 %collective-permute-start.4 = (f32[8,64,1024]{2,1,0:T(8,128)}, f32[8,64,1024]{2,1,0:T(8,128)S(1)}, u32[]{:S(2)}, u32[]{:S(2)}) collective-permute-start(f32[8,64,1024]{2,1,0:T(8,128)} %get-tuple-element.29), channel_id=1, source_target_pairs={{0,4},{4,0},{8,12},{12,8},{16,20},{20,16},{24,28},{28,24},{1,5},{5... | collective-permute-start | bytes 6291464 | tf_op jit(solution)/shard_map/ppermute | solution.py:504
  11.2 28.8 %collective-permute-start.20 = (f32[4,2,64,256]{3,2,1,0:T(8,128)}, f32[4,2,64,256]{3,2,1,0:T(8,128)}, u32[]{:S(2)}, u32[]{:S(2)}) collective-permute-start(f32[4,2,64,256]{3,2,1,0:T(8,128)} %get-tuple-element.37), channel_id=1, source_target_pairs={{0,8},{4,12},{8,0},{12,4},{16,24},{20,28},{24,16},{28,20},{1,9},{5... | collective-permute-start | bytes 1572872 | tf_op jit(solution)/shard_map/ppermute | solution.py:463
  13.8 25.1 %copy-start.22 = (f32[4,2,64,256]{3,2,1,0:T(8,128)S(1)}, f32[4,2,64,256]{3,2,1,0:T(8,128)}, u32[]{:S(2)}) copy-start(f32[4,2,64,256]{3,2,1,0:T(8,128)} %get-tuple-element.39) | copy-start | bytes 1572868
  30.8 5.4 %collective-permute-start = (f32[128,128]{1,0:T(8,128)}, f32[128,128]{1,0:T(8,128)S(1)}, u32[]{:S(2)}, u32[]{:S(2)}) collective-permute-start(f32[128,128]{1,0:T(8,128)} %lcms_pass.1), channel_id=1, source_target_pairs={{0,1},{1,2},{2,3},{3,0},{4,5},{5,6},{6,7},{7,4},{8,9},{9,10},{10,1... | collective-permute-start | bytes 196616 | tf_op jit(solution)/shard_map/ppermute | solution.py:456
  32.3 6.5 %collective-permute-start.1 = (f32[128,128]{1,0:T(8,128)}, f32[128,128]{1,0:T(8,128)S(1)}, u32[]{:S(2)}, u32[]{:S(2)}) collective-permute-start(f32[128,128]{1,0:T(8,128)} %lcms_pass.1), channel_id=1, source_target_pairs={{0,2},{1,3},{2,0},{3,1},{4,6},{5,7},{6,4},{7,5},{8,10},{9,11},{10,... | collective-permute-start | bytes 196616 | tf_op jit(solution)/shard_map/ppermute | solution.py:456
  33.8 6.2 %collective-permute-start.2 = (f32[128,128]{1,0:T(8,128)}, f32[128,128]{1,0:T(8,128)S(1)}, u32[]{:S(2)}, u32[]{:S(2)}) collective-permute-start(f32[128,128]{1,0:T(8,128)} %lcms_pass.1), channel_id=1, source_target_pairs={{0,3},{1,0},{2,1},{3,2},{4,7},{5,4},{6,5},{7,6},{8,11},{9,8},{10,9... | collective-permute-start | bytes 196616 | tf_op jit(solution)/shard_map/ppermute | solution.py:456
  36.2 36.8 %collective-permute-start.21 = (f32[4,2,64,256]{3,2,1,0:T(8,128)}, f32[4,2,64,256]{3,2,1,0:T(8,128)}, u32[]{:S(2)}, u32[]{:S(2)}) collective-permute-start(f32[4,2,64,256]{3,2,1,0:T(8,128)} %get-tuple-element.38), channel_id=1, source_target_pairs={{0,16},{4,20},{8,24},{12,28},{16,0},{20,4},{24,8},{28,12},{1,17},{... | collective-permute-start | bytes 1572872 | tf_op jit(solution)/shard_map/ppermute | solution.py:463
  38.8 38.0 %collective-permute-start.22 = (f32[4,2,64,256]{3,2,1,0:T(8,128)S(1)}, f32[4,2,64,256]{3,2,1,0:T(8,128)}, u32[]{:S(2)}, u32[]{:S(2)}) collective-permute-start(f32[4,2,64,256]{3,2,1,0:T(8,128)S(1)} %copy-done.22), channel_id=1, source_target_pairs={{0,24},{4,28},{8,16},{12,20},{16,8},{20,12},{24,0},{28,4},{1,25},{... | collective-permute-start | bytes 1572872 | tf_op jit(solution)/shard_map/ppermute | solution.py:463
  40.0 37.5 %collective-permute-start.23 = (f32[4,2,64,256]{3,2,1,0:T(8,128)}, f32[4,2,64,256]{3,2,1,0:T(8,128)}, u32[]{:S(2)}, u32[]{:S(2)}) collective-permute-start(f32[4,2,64,256]{3,2,1,0:T(8,128)} %collective-permute-done.20.refs_12_), channel_id=1, source_target_pairs={{0,4},{4,0},{8,12},{12,8},{16,20},{20,16},{24,28},{28,24},{1,5},{5... | collective-permute-start | bytes 1572872 | tf_op jit(solution)/shard_map/ppermute | solution.py:512
  40.8 1.5 copy-start.8
  40.9 1.5 collective-permute-start.3
  42.3 0.6 copy-start.18
  42.3 1.4 copy-start.4
  45.7 41.3 %copy-start = (f32[64,1152]{1,0:T(8,128)}, f32[64,1152]{1,0:T(8,128)S(1)}, u32[]{:S(2)}) copy-start(f32[64,1152]{1,0:T(8,128)S(1)} %get-tuple-element.33.refs_0_) | copy-start | bytes 884740
  45.7 29.7 %collective-permute-start.11 = (f32[64,1152]{1,0:T(8,128)S(1)}, f32[64,1152]{1,0:T(8,128)S(1)}, u32[]{:S(2)}, u32[]{:S(2)}) collective-permute-start(f32[64,1152]{1,0:T(8,128)S(1)} %get-tuple-element.33.refs_0_), channel_id=1, source_target_pairs={{0,8},{4,12},{24,16},{28,20},{1,9},{5,13},{25,17},{29,21},{2,10},{... | collective-permute-start | bytes 884744 | tf_op jit(solution)/shard_map/ppermute | solution.py:475
  50.9 82.0 %copy-start.1 = (f32[64,1024]{1,0:T(8,128)}, f32[64,1024]{1,0:T(8,128)S(1)}, u32[]{:S(2)}) copy-start(f32[64,1024]{1,0:T(8,128)S(1)} %get-tuple-element.31.refs_0_) | copy-start | bytes 786436
  50.9 82.0 %copy-start.2 = (f32[64,1024]{1,0:T(8,128)}, f32[64,1024]{1,0:T(8,128)S(1)}, u32[]{:S(2)}) copy-start(f32[64,1024]{1,0:T(8,128)S(1)} %get-tuple-element.32.refs_4_) | copy-start | bytes 786436
  50.9 82.0 %copy-start.3 = (f32[64,1024]{1,0:T(8,128)}, f32[64,1024]{1,0:T(8,128)S(1)}, u32[]{:S(2)}) copy-start(f32[64,1024]{1,0:T(8,128)S(1)} %get-tuple-element.34.refs_4_) | copy-start | bytes 786436
  50.9 39.5 %copy-start.19 = (f32[64,128]{1,0:T(8,128)S(1)}, f32[64,128]{1,0:T(8,128)}, u32[]{:S(2)}) copy-start(f32[64,128]{1,0:T(8,128)} %get-tuple-element.36.refs_0_) | copy-start | bytes 98308
  51.0 26.7 %collective-permute-start.14 = (f32[64,1024]{1,0:T(8,128)S(1)}, f32[64,1024]{1,0:T(8,128)S(1)}, u32[]{:S(2)}, u32[]{:S(2)}) collective-permute-start(f32[64,1024]{1,0:T(8,128)S(1)} %get-tuple-element.34.refs_4_), channel_id=1, source_target_pairs={{0,8},{4,12},{24,16},{28,20},{1,9},{5,13},{25,17},{29,21},{2,10},{... | collective-permute-start | bytes 786440 | tf_op jit(solution)/shard_map/ppermute | solution.py:475
  73.0 9.1 %collective-permute-start.8 = (f32[64,1024]{1,0:T(8,128)S(1)}, f32[64,1024]{1,0:T(8,128)S(1)}, u32[]{:S(2)}, u32[]{:S(2)}) collective-permute-start(f32[64,1024]{1,0:T(8,128)S(1)} %get-tuple-element.32.refs_4_), channel_id=1, source_target_pairs={{0,8},{4,12},{24,16},{28,20},{1,9},{5,13},{25,17},{29,21},{2,10},{... | collective-permute-start | bytes 786440 | tf_op jit(solution)/shard_map/ppermute | solution.py:475
  75.5 57.5 %copy-start.5 = (f32[64,1152]{1,0:T(8,128)}, f32[64,1152]{1,0:T(8,128)S(1)}, u32[]{:S(2)}) copy-start(f32[64,1152]{1,0:T(8,128)S(1)} %collective-permute-done.11.refs_1_) | copy-start | bytes 884740
  75.5 10.1 %collective-permute-start.5 = (f32[64,1024]{1,0:T(8,128)S(1)}, f32[64,1024]{1,0:T(8,128)S(1)}, u32[]{:S(2)}, u32[]{:S(2)}) collective-permute-start(f32[64,1024]{1,0:T(8,128)S(1)} %get-tuple-element.31.refs_0_), channel_id=1, source_target_pairs={{0,8},{4,12},{24,16},{28,20},{1,9},{5,13},{25,17},{29,21},{2,10},{... | collective-permute-start | bytes 786440 | tf_op jit(solution)/shard_map/ppermute | solution.py:475
  76.8 9.4 %collective-permute-start.12 = (f32[64,1152]{1,0:T(8,128)S(1)}, f32[64,1152]{1,0:T(8,128)S(1)}, u32[]{:S(2)}, u32[]{:S(2)}) collective-permute-start(f32[64,1152]{1,0:T(8,128)S(1)} %add.61), channel_id=1, source_target_pairs={{8,16},{12,20},{16,8},{20,12},{9,17},{13,21},{17,9},{21,13},{10,18... | collective-permute-start | bytes 884744 | tf_op jit(solution)/shard_map/ppermute | solution.py:475
  77.5 36.1 %collective-permute-start.24 = (f32[4,2,64,256]{3,2,1,0:T(8,128)}, f32[4,2,64,256]{3,2,1,0:T(8,128)}, u32[]{:S(2)}, u32[]{:S(2)}) collective-permute-start(f32[4,2,64,256]{3,2,1,0:T(8,128)} %collective-permute-done.21.refs_13_), channel_id=1, source_target_pairs={{0,4},{4,0},{8,12},{12,8},{16,20},{20,16},{24,28},{28,24},{1,5},{5... | collective-permute-start | bytes 1572872 | tf_op jit(solution)/shard_map/ppermute | solution.py:512
  77.6 55.3 %copy-start.11 = (f32[64,1024]{1,0:T(8,128)}, f32[64,1024]{1,0:T(8,128)S(1)}, u32[]{:S(2)}) copy-start(f32[64,1024]{1,0:T(8,128)S(1)} %collective-permute-done.14.refs_5_) | copy-start | bytes 786436
  77.6 37.3 %collective-permute-start.25 = (f32[4,2,64,256]{3,2,1,0:T(8,128)}, f32[4,2,64,256]{3,2,1,0:T(8,128)}, u32[]{:S(2)}, u32[]{:S(2)}) collective-permute-start(f32[4,2,64,256]{3,2,1,0:T(8,128)} %collective-permute-done.22.refs_14_), channel_id=1, source_target_pairs={{0,4},{4,0},{8,12},{12,8},{16,20},{20,16},{24,28},{28,24},{1,5},{5... | collective-permute-start | bytes 1572872 | tf_op jit(solution)/shard_map/ppermute | solution.py:512
  82.1 50.9 %copy-start.9 = (f32[64,1024]{1,0:T(8,128)}, f32[64,1024]{1,0:T(8,128)S(1)}, u32[]{:S(2)}) copy-start(f32[64,1024]{1,0:T(8,128)S(1)} %collective-permute-done.8.refs_5_) | copy-start | bytes 786436
  82.1 4.9 %collective-permute-start.15 = (f32[64,1024]{1,0:T(8,128)S(1)}, f32[64,1024]{1,0:T(8,128)S(1)}, u32[]{:S(2)}, u32[]{:S(2)}) collective-permute-start(f32[64,1024]{1,0:T(8,128)S(1)} %add.63), channel_id=1, source_target_pairs={{8,16},{12,20},{16,8},{20,12},{9,17},{13,21},{17,9},{21,13},{10,18... | collective-permute-start | bytes 786440 | tf_op jit(solution)/shard_map/ppermute | solution.py:475
  85.6 47.4 %copy-start.10 = (f32[64,1024]{1,0:T(8,128)}, f32[64,1024]{1,0:T(8,128)S(1)}, u32[]{:S(2)}) copy-start(f32[64,1024]{1,0:T(8,128)S(1)} %collective-permute-done.5.refs_1_) | copy-start | bytes 786436
  85.6 3.5 %collective-permute-start.9 = (f32[64,1024]{1,0:T(8,128)S(1)}, f32[64,1024]{1,0:T(8,128)S(1)}, u32[]{:S(2)}, u32[]{:S(2)}) collective-permute-start(f32[64,1024]{1,0:T(8,128)S(1)} %add.59), channel_id=1, source_target_pairs={{8,16},{12,20},{16,8},{20,12},{9,17},{13,21},{17,9},{21,13},{10,18... | collective-permute-start | bytes 786440 | tf_op jit(solution)/shard_map/ppermute | solution.py:475
  86.3 46.7 %copy-start.6 = (f32[64,1152]{1,0:T(8,128)}, f32[64,1152]{1,0:T(8,128)S(1)}, u32[]{:S(2)}) copy-start(f32[64,1152]{1,0:T(8,128)S(1)} %collective-permute-done.12.refs_2_) | copy-start | bytes 884740
  86.3 4.1 %collective-permute-start.6 = (f32[64,1024]{1,0:T(8,128)S(1)}, f32[64,1024]{1,0:T(8,128)S(1)}, u32[]{:S(2)}, u32[]{:S(2)}) collective-permute-start(f32[64,1024]{1,0:T(8,128)S(1)} %add.57), channel_id=1, source_target_pairs={{8,16},{12,20},{16,8},{20,12},{9,17},{13,21},{17,9},{21,13},{10,18... | collective-permute-start | bytes 786440 | tf_op jit(solution)/shard_map/ppermute | solution.py:475
  87.0 46.0 %copy-start.14 = (f32[64,1024]{1,0:T(8,128)}, f32[64,1024]{1,0:T(8,128)S(1)}, u32[]{:S(2)}) copy-start(f32[64,1024]{1,0:T(8,128)S(1)} %collective-permute-done.15.refs_6_) | copy-start | bytes 786436
  87.1 48.7 %collective-permute-start.13 = (f32[64,1152]{1,0:T(8,128)S(1)}, f32[64,1152]{1,0:T(8,128)S(1)}, u32[]{:S(2)}, u32[]{:S(2)}) collective-permute-start(f32[64,1152]{1,0:T(8,128)S(1)} %add.62), channel_id=1, source_target_pairs={{8,0},{12,4},{16,24},{20,28},{9,1},{13,5},{17,25},{21,29},{10,2},{... | collective-permute-start | bytes 884744 | tf_op jit(solution)/shard_map/ppermute | solution.py:475
  89.1 43.9 %copy-start.12 = (f32[64,1024]{1,0:T(8,128)}, f32[64,1024]{1,0:T(8,128)S(1)}, u32[]{:S(2)}) copy-start(f32[64,1024]{1,0:T(8,128)S(1)} %collective-permute-done.9.refs_6_) | copy-start | bytes 786436
  89.1 44.8 %collective-permute-start.16 = (f32[64,1024]{1,0:T(8,128)}, f32[64,1024]{1,0:T(8,128)}, u32[]{:S(2)}, u32[]{:S(2)}) collective-permute-start(f32[64,1024]{1,0:T(8,128)} %add.64), channel_id=1, source_target_pairs={{8,0},{12,4},{16,24},{20,28},{9,1},{13,5},{17,25},{21,29},{10,2},{... | collective-permute-start | bytes 786440 | tf_op jit(solution)/shard_map/ppermute | solution.py:475
  90.4 42.6 %copy-start.13 = (f32[64,1024]{1,0:T(8,128)}, f32[64,1024]{1,0:T(8,128)S(1)}, u32[]{:S(2)}) copy-start(f32[64,1024]{1,0:T(8,128)S(1)} %collective-permute-done.6.refs_2_) | copy-start | bytes 786436
  90.4 25.8 %collective-permute-start.17 = (f32[64,128]{1,0:T(8,128)S(1)}, f32[64,128]{1,0:T(8,128)S(1)}, u32[]{:S(2)}, u32[]{:S(2)}) collective-permute-start(f32[64,128]{1,0:T(8,128)S(1)} %copy-done.19), channel_id=1, source_target_pairs={{0,8},{4,12},{8,0},{12,4},{16,24},{20,28},{24,16},{28,20},{1,9},{5... | collective-permute-start | bytes 98312 | tf_op jit(solution)/shard_map/ppermute | solution.py:463
  113.6 28.5 %collective-permute-start.10 = (f32[64,1024]{1,0:T(8,128)}, f32[64,1024]{1,0:T(8,128)}, u32[]{:S(2)}, u32[]{:S(2)}) collective-permute-start(f32[64,1024]{1,0:T(8,128)} %add.60), channel_id=1, source_target_pairs={{8,0},{12,4},{16,24},{20,28},{9,1},{13,5},{17,25},{21,29},{10,2},{... | collective-permute-start | bytes 786440 | tf_op jit(solution)/shard_map/ppermute | solution.py:475
  114.9 27.2 %collective-permute-start.7 = (f32[64,1024]{1,0:T(8,128)}, f32[64,1024]{1,0:T(8,128)}, u32[]{:S(2)}, u32[]{:S(2)}) collective-permute-start(f32[64,1024]{1,0:T(8,128)} %add.58), channel_id=1, source_target_pairs={{8,0},{12,4},{16,24},{20,28},{9,1},{13,5},{17,25},{21,29},{10,2},{... | collective-permute-start | bytes 786440 | tf_op jit(solution)/shard_map/ppermute | solution.py:475
  116.2 8.4 %copy-start.20 = (f32[64,128]{1,0:T(8,128)}, f32[64,128]{1,0:T(8,128)S(1)}, u32[]{:S(2)}) copy-start(f32[64,128]{1,0:T(8,128)S(1)} %collective-permute-done.17.refs_1_) | copy-start | bytes 98308
  116.2 6.3 %collective-permute-start.18 = (f32[64,128]{1,0:T(8,128)S(1)}, f32[64,128]{1,0:T(8,128)S(1)}, u32[]{:S(2)}, u32[]{:S(2)}) collective-permute-start(f32[64,128]{1,0:T(8,128)S(1)} %copy-done.19), channel_id=1, source_target_pairs={{0,16},{4,20},{8,24},{12,28},{16,0},{20,4},{24,8},{28,12},{1,17},{... | collective-permute-start | bytes 98312 | tf_op jit(solution)/shard_map/ppermute | solution.py:463
  122.5 2.1 %copy-start.21 = (f32[64,128]{1,0:T(8,128)}, f32[64,128]{1,0:T(8,128)S(1)}, u32[]{:S(2)}) copy-start(f32[64,128]{1,0:T(8,128)S(1)} %collective-permute-done.18.refs_2_) | copy-start | bytes 98308
  122.5 5.9 %collective-permute-start.19 = (f32[64,128]{1,0:T(8,128)S(1)}, f32[64,128]{1,0:T(8,128)}, u32[]{:S(2)}, u32[]{:S(2)}) collective-permute-start(f32[64,128]{1,0:T(8,128)S(1)} %copy-done.19), channel_id=1, source_target_pairs={{0,24},{4,28},{8,16},{12,20},{16,8},{20,12},{24,0},{28,4},{1,25},{... | collective-permute-start | bytes 98312 | tf_op jit(solution)/shard_map/ppermute | solution.py:463
  133.0 7.7 %collective-permute-start.26 = (f32[2,64,128]{2,1,0:T(8,128)}, f32[2,64,128]{2,1,0:T(8,128)S(1)}, u32[]{:S(2)}, u32[]{:S(2)}) collective-permute-start(f32[2,64,128]{2,1,0:T(8,128)} %get-tuple-element.41), channel_id=1, source_target_pairs={{0,8},{4,12},{8,0},{12,4},{16,24},{20,28},{24,16},{28,20},{1,9},{5... | collective-permute-start | bytes 196616 | tf_op jit(solution)/shard_map/ppermute | solution.py:463
  133.9 6.8 %collective-permute-start.27 = (f32[2,64,128]{2,1,0:T(8,128)}, f32[2,64,128]{2,1,0:T(8,128)S(1)}, u32[]{:S(2)}, u32[]{:S(2)}) collective-permute-start(f32[2,64,128]{2,1,0:T(8,128)} %get-tuple-element.42), channel_id=1, source_target_pairs={{0,16},{4,20},{8,24},{12,28},{16,0},{20,4},{24,8},{28,12},{1,17},{... | collective-permute-start | bytes 196616 | tf_op jit(solution)/shard_map/ppermute | solution.py:463
  135.8 1.7 %copy-start.7 = (f32[64,1152]{1,0:T(8,128)}, f32[64,1152]{1,0:T(8,128)S(1)}, u32[]{:S(2)}) copy-start(f32[64,1152]{1,0:T(8,128)S(1)} %collective-permute-done.13.refs_3_) | copy-start | bytes 884740
  135.8 6.3 %collective-permute-start.28 = (f32[2,64,128]{2,1,0:T(8,128)}, f32[2,64,128]{2,1,0:T(8,128)S(1)}, u32[]{:S(2)}, u32[]{:S(2)}) collective-permute-start(f32[2,64,128]{2,1,0:T(8,128)} %get-tuple-element.43), channel_id=1, source_target_pairs={{0,24},{4,28},{8,16},{12,20},{16,8},{20,12},{24,0},{28,4},{1,25},{... | collective-permute-start | bytes 196616 | tf_op jit(solution)/shard_map/ppermute | solution.py:463
  140.7 1.4 copy-start.15
  140.7 1.4 copy-start.16
  142.1 0.6 copy-start.17
  146.0 1.5 collective-permute-start.29
  148.2 11.9 %collective-permute-start.30 = (f32[64,128]{1,0:T(8,128)S(1)}, f32[64,128]{1,0:T(8,128)S(1)}, u32[]{:S(2)}, u32[]{:S(2)}) collective-permute-start(f32[64,128]{1,0:T(8,128)S(1)} %fusion), channel_id=1, source_target_pairs={{0,1},{1,2},{2,3},{3,0},{4,5},{5,6},{6,7},{7,4},{8,9},{9,10},{10,1... | collective-permute-start | bytes 98312 | tf_op jit(solution)/shard_map/ppermute | solution.py:456
  148.7 11.5 %collective-permute-start.31 = (f32[64,128]{1,0:T(8,128)S(1)}, f32[64,128]{1,0:T(8,128)S(1)}, u32[]{:S(2)}, u32[]{:S(2)}) collective-permute-start(f32[64,128]{1,0:T(8,128)S(1)} %fusion), channel_id=1, source_target_pairs={{0,2},{1,3},{2,0},{3,1},{4,6},{5,7},{6,4},{7,5},{8,10},{9,11},{10,... | collective-permute-start | bytes 98312 | tf_op jit(solution)/shard_map/ppermute | solution.py:456
  150.2 10.0 %collective-permute-start.32 = (f32[64,128]{1,0:T(8,128)S(1)}, f32[64,128]{1,0:T(8,128)S(1)}, u32[]{:S(2)}, u32[]{:S(2)}) collective-permute-start(f32[64,128]{1,0:T(8,128)S(1)} %fusion), channel_id=1, source_target_pairs={{0,3},{1,0},{2,1},{3,2},{4,7},{5,4},{6,5},{7,6},{8,11},{9,8},{10,9... | collective-permute-start | bytes 98312 | tf_op jit(solution)/shard_map/ppermute | solution.py:456

commit v3 on v2

--- a/solution.py
+++ b/solution.py
@@ -27,14 +27,67 @@
     return pl.CostEstimate(flops=int(flops), bytes_accessed=int(transferred), transcendentals=0)
 
 
+def within(mebibytes):
+    return pltpu.CompilerParams(vmem_limit_bytes=mebibytes << 20)
+
+
+def in_vmem(array):
+    return pltpu.with_memory_space_constraint(array, pltpu.VMEM)
+
+
 def whole(shape):
     return pl.BlockSpec(shape, lambda *_: (0,) * len(shape))
 
 
-def nmr_body(blocks, swept, core_ref, chip_ref, *refs):
-    spectra_refs, ppm_refs = refs[: 2 * blocks], refs[2 * blocks : 4 * blocks]
-    mz_ref, part_ref, keep_ref, send_ref, *parcels = refs[4 * blocks : -1]
-    total = refs[-1]
+def sort_body(blocks, swept, core_ref, chip_ref, *refs):
+    spectra_refs, (keep_ref, send_ref, *parcels) = refs[: 2 * blocks], refs[2 * blocks :]
+    width = spectra_refs[0].shape[1]
+    for core in (0, 1):
+
+        @pl.when(core_ref[0] == core)
+        def _():
+            for b in range(blocks):
+                keep_ref[0, :, b * width : (b + 1) * width] = spectra_refs[2 * b + core][...]
+                send_ref[0, :, b * width : (b + 1) * width] = spectra_refs[2 * b + 1 - core][...]
+
+    if parcels:
+
+        @pl.when(pl.program_id(0) >= swept)
+        def _():
+            for step, parcel in enumerate(parcels, 1):
+                columns = pl.ds(pl.multiple_of((chip_ref[0] ^ step) * width, width), width)
+                parcel[0, 0] = keep_ref[0, :, columns]
+                parcel[0, 1] = send_ref[0, :, columns]
+
+
+def sort_pass(core, chip, spectra, blocks, pieces, swept):
+    samples, positions = spectra.shape
+    width = positions // (2 * blocks * pieces)
+    columns = [
+        pl.BlockSpec((samples, width), functools.partial(lambda b, k, c, h: (0, b * pieces + k), b))
+        for b in range(2 * blocks)
+    ]
+    sorted_shape = jax.ShapeDtypeStruct((pieces, samples, blocks * width), F32)
+    parcels = blocks - 1 if swept < pieces else 0
+    parcel_shape = jax.ShapeDtypeStruct((pieces - swept, 2, samples, width), F32)
+    return pl.pallas_call(
+        functools.partial(sort_body, blocks, swept),
+        name="sort_pass",
+        compiler_params=within(12),
+        grid_spec=pltpu.PrefetchScalarGridSpec(
+            num_scalar_prefetch=2,
+            grid=(pieces,),
+            in_specs=columns,
+            out_specs=[pl.BlockSpec((1, samples, blocks * width), lambda k, c, h: (k, 0, 0))] * 2
+            + [pl.BlockSpec((1, 2, samples, width), lambda k, c, h: (jnp.maximum(k - swept, 0), 0, 0, 0))] * parcels,
+        ),
+        out_shape=[sorted_shape, sorted_shape] + [parcel_shape] * parcels,
+        cost_estimate=cost(1 << 20, 4 * 2 * 64 * positions),
+    )(core, chip, *([spectra] * (2 * blocks)))
+
+
+def nmr_body(blocks, core_ref, keep_ref, send_ref, *refs):
+    ppm_refs, (mz_ref, part_ref, total) = refs[: 2 * blocks], refs[2 * blocks :]
     piece = pl.program_id(0)
     rank = mz_ref.shape[0]
 
@@ -47,34 +100,14 @@
         part_ref[:, rank:] = jnp.zeros_like(part_ref[:, rank:])
         part_ref[rank:, rank:] = rows[:, :rank] + rows[:, rank:]
 
-    halves = [
-        jnp.concatenate([spectra_refs[2 * b + core][...] for b in range(blocks)], axis=1) for core in (0, 1)
-    ]
-    values = jnp.concatenate(halves, axis=1)
-    positions = stack_split([jnp.concatenate([ref[...] for core in (0, 1) for ref in ppm_refs[core::2]], axis=1)])
+    values = jnp.concatenate([keep_ref[0], send_ref[0]], axis=1)
+    positions = stack_split([jnp.concatenate([ref[...] for ref in ppm_refs], axis=1)])
     left = jnp.concatenate([stack_split([values]), positions[:rank]], axis=0)
     total[...] += lax.dot_general(left, positions, NT, preferred_element_type=F32)
 
-    for core in (0, 1):
-
-        @pl.when(core_ref[0] == core)
-        def _():
-            keep_ref[0] = halves[core]
-            send_ref[0] = halves[1 - core]
-
-    if parcels:
-        width = parcels[0].shape[3]
-
-        @pl.when(piece >= swept)
-        def _():
-            for step, parcel in enumerate(parcels, 1):
-                columns = pl.ds(pl.multiple_of((chip_ref[0] ^ step) * width, width), width)
-                parcel[0, 0] = keep_ref[0, :, columns]
-                parcel[0, 1] = send_ref[0, :, columns]
-
     @pl.when(piece == pl.num_programs(0) - 1)
     def _():
-        samples = spectra_refs[0].shape[0]
+        samples = keep_ref.shape[1]
         products = total[...]
         fit = products[:samples] + products[samples : 2 * samples]
         gram = products[2 * samples :]
@@ -83,36 +116,35 @@
         part_ref[rank:, :rank] = gram[:, :rank] + (mixed + mixed.T)
 
 
-def nmr_pass(core, chip, spectra, ppm_factor, mz_factor, blocks, pieces, swept):
-    samples, positions = spectra.shape
+def nmr_pass(core, keep, send, ppm_factor, mz_factor, blocks):
+    pieces, samples, columns = keep.shape
     rank, channels = mz_factor.shape
-    width = positions // (2 * blocks * pieces)
-
-    def columns(rows):
+    width = columns // blocks
+
+    def positions(side):
         return [
-            pl.BlockSpec((rows, width), functools.partial(lambda b, k, c, h: (0, b * pieces + k), b))
-            for b in range(2 * blocks)
+            pl.BlockSpec(
+                (rank, width),
+                functools.partial(lambda b, k, c: (0, (2 * b + (c[0] ^ side)) * pieces + k), b),
+            )
+            for b in range(blocks)
         ]
 
-    sorted_shape = jax.ShapeDtypeStruct((pieces, samples, blocks * width), F32)
-    parcels = blocks - 1 if swept < pieces else 0
-    parcel_shape = jax.ShapeDtypeStruct((pieces - swept, 2, samples, width), F32)
-    return pl.pallas_call(
-        functools.partial(nmr_body, blocks, swept),
+    piece = pl.BlockSpec((1, samples, columns), lambda k, c: (k, 0, 0))
+    return pl.pallas_call(
+        functools.partial(nmr_body, blocks),
         name="nmr_pass",
+        compiler_params=within(16),
         grid_spec=pltpu.PrefetchScalarGridSpec(
-            num_scalar_prefetch=2,
+            num_scalar_prefetch=1,
             grid=(pieces,),
-            in_specs=columns(samples) + columns(rank) + [whole((rank, channels))],
-            out_specs=[whole((2 * rank, 2 * rank))]
-            + [pl.BlockSpec((1, samples, blocks * width), lambda k, c, h: (k, 0, 0))] * 2
-            + [pl.BlockSpec((1, 2, samples, width), lambda k, c, h: (jnp.maximum(k - swept, 0), 0, 0, 0))] * parcels,
+            in_specs=[piece, piece] + positions(0) + positions(1) + [whole((rank, channels))],
+            out_specs=whole((2 * rank, 2 * rank)),
             scratch_shapes=[pltpu.VMEM((2 * samples + rank, 2 * rank), F32)],
         ),
-        out_shape=[jax.ShapeDtypeStruct((2 * rank, 2 * rank), F32), sorted_shape, sorted_shape]
-        + [parcel_shape] * parcels,
-        cost_estimate=cost(2 * 256 * 256 * positions, 4 * 3 * 64 * positions),
-    )(core, chip, *([spectra] * (2 * blocks)), *([ppm_factor] * (2 * blocks)), mz_factor)
+        out_shape=jax.ShapeDtypeStruct((2 * rank, 2 * rank), F32),
+        cost_estimate=cost(2 * 256 * 256 * pieces * columns, 4 * 3 * 64 * pieces * columns),
+    )(core, keep, send, *([ppm_factor] * (2 * blocks)), mz_factor)
 
 
 def lcms_body(lcms_ref, scan_ref, mz_ref, part_ref, out_ref, weights, scans):
@@ -143,6 +175,7 @@
     return pl.pallas_call(
         lcms_body,
         name="lcms_pass",
+        compiler_params=within(32),
         grid=(samples // count,),
         in_specs=[
             pl.BlockSpec((count, steps, channels), lambda i: (i, 0, 0)),
@@ -193,6 +226,7 @@
     return pl.pallas_call(
         first_body,
         name="first_pass",
+        compiler_params=within(12),
         grid=(1,),
         in_specs=[whole(own_pack.shape)] * 2 + [piece] * 2,
         out_specs=[
@@ -228,6 +262,7 @@
     return pl.pallas_call(
         project_body,
         name="project_pass",
+        compiler_params=within(12),
         grid=(count,),
         in_specs=[whole(left.shape), piece, piece],
         out_specs=[whole((rank, columns))] * count,
@@ -239,11 +274,11 @@
 def fit_body(count, earlier, *refs):
     sweeps, refs = refs[: 4 * count], refs[4 * count :]
     own_ref, other_ref, sums_ref = refs[0], refs[1], refs[2 + earlier]
-    _, samples, _ = own_ref.shape
+    _, samples, columns = own_ref.shape
     rank = sums_ref.shape[2] // 2
     sums = None
     for k in range(count):
-        part, inward, across, outward = (ref[...] for ref in sweeps[4 * k : 4 * k + 4])
+        part, inward, across, outward = (ref[:, :columns] for ref in sweeps[4 * k : 4 * k + 4])
         total = part + inward + across + outward
         refs[3 + earlier + k][...] = total
         right = stack_split([total])
@@ -265,12 +300,13 @@
     count, rank = len(sweeps), sweeps[0][0].shape[0]
     pieces = pl.BlockSpec((count, samples, columns), lambda i: (first // count, 0, 0))
     assert first % count == 0
-    arrays = [array for sweep in sweeps for array in sweep]
+    arrays = [in_vmem(array) for sweep in sweeps for array in sweep]
     sums_shape = (2, samples, 2 * rank)
     sums, *totals = pl.pallas_call(
         functools.partial(fit_body, count, len(earlier)),
+        compiler_params=within(16),
         grid=(1,),
-        in_specs=[whole((rank, columns))] * len(arrays)
+        in_specs=[pl.BlockSpec(memory_space=pltpu.VMEM)] * len(arrays)
         + [pieces, pieces]
         + [whole(sums_shape)] * len(earlier),
         out_specs=[whole(sums_shape)] + [whole((rank, columns))] * count,
@@ -282,7 +318,7 @@
 
 
 def eliminate(matrix, right):
-    size, ahead = matrix.shape[0], 4
+    size, ahead = matrix.shape[0], 8
     whole_rows = jnp.concatenate([matrix, right], axis=1)
     groups = [whole_rows[i : i + 8] for i in range(0, size, 8)]
     lanes = whole_rows.shape[1]
@@ -328,6 +364,7 @@
     return pl.pallas_call(
         mix_body,
         name="mix_pass",
+        compiler_params=within(6),
         grid=(1,),
         in_specs=[pl.BlockSpec((rank, 2 * rank), lambda i: (0, columns // (2 * rank)))] * len(sweep)
         + [whole(pack.shape), whole(scan_factor.shape)],
@@ -337,22 +374,25 @@
     )(*sweep, pack, scan_factor)
 
 
-def sample_body(fit_ref, mix_ref, lcms_gram_ref, pack_ref, out_ref):
+def sample_body(*refs):
+    parts, (mix_ref, lcms_gram_ref, pack_ref, out_ref) = refs[:-4], refs[-4:]
     rank = mix_ref.shape[0]
     mix = mix_ref[...]
-    fit = dot32(fit_ref[:, :rank], mix)
-    new_gram = dot32(mix, dot32(fit_ref[:, rank:], mix), (((0,), (0,)), ((), ())))
+    both = sum(part[...] for part in parts)
+    fit = dot32(both[:, :rank], mix)
+    new_gram = dot32(mix, dot32(both[:, rank:], mix), (((0,), (0,)), ((), ())))
     right = pack_ref[: fit.shape[0], rank:] + fit
     out_ref[...] = eliminate(lcms_gram_ref[...] + new_gram, right.T).T
 
 
-def sample_pass(fit, mix, lcms_gram, pack):
+def sample_pass(parts, mix, lcms_gram, pack):
     return pl.pallas_call(
         sample_body,
         name="sample_pass",
-        out_shape=jax.ShapeDtypeStruct((fit.shape[0], mix.shape[0]), F32),
+        compiler_params=within(6),
+        out_shape=jax.ShapeDtypeStruct((parts[0].shape[0], mix.shape[0]), F32),
         cost_estimate=cost(1 << 22, 65536),
-    )(fit, mix, lcms_gram, pack)
+    )(*parts, mix, lcms_gram, pack)
 
 
 def ppm_body(chip_ref, mix_ref, *refs):
@@ -376,6 +416,7 @@
     return pl.pallas_call(
         ppm_body,
         name="ppm_pass",
+        compiler_params=within(12),
         grid_spec=pltpu.PrefetchScalarGridSpec(
             num_scalar_prefetch=1,
             grid=(1,),
@@ -433,6 +474,7 @@
     return pl.pallas_call(
         functools.partial(direct_body, chips, count),
         name="direct_pass",
+        compiler_params=within(16),
         grid_spec=pltpu.PrefetchScalarGridSpec(
             num_scalar_prefetch=1,
             grid=(1,),
@@ -449,11 +491,11 @@
     )(chip, *rows, *([own] * count), *([other] * count), *came, *swapped)
 
 
-def sum_over_mz(values, count):
-    result = values
+def from_mz(values, count):
+    result = [values]
     for step in range(1, count):
         hops = [(i, (i + step) % count) for i in range(count)]
-        result = result + lax.ppermute(values, "mz", hops)
+        result.append(lax.ppermute(values, "mz", hops))
     return result
 
 
@@ -499,11 +541,13 @@
     core, chip = (run % 2).reshape(1), (run // 2).reshape(1)
     swap = [(i, i ^ 1) for i in range(runs)]
 
-    part, own, leaving, *parcels = nmr_pass(core, chip, spectra, ppm_factor, mz_factor, chips, pieces, swept)
+    spectra = pltpu.with_memory_space_constraint(spectra, pltpu.HBM)
+    own, leaving, *parcels = sort_pass(core, chip, spectra, chips, pieces, swept)
     came = from_chips(parcels, runs) if parcels else []
     other = lax.ppermute(leaving, "run", swap)
+    part = nmr_pass(core, own, leaving, ppm_factor, mz_factor, chips)
     pack = lcms_pass(lcms, scan_factor, mz_factor, part)
-    pack = sum_over_mz(pack, mzs)
+    pack = sum(from_mz(pack, mzs))
     left, rows, first = first_pass(pack, lax.ppermute(pack, "run", swap), own, other)
     sweeps = sum_over_chips([first, *project_pass(left, own, other, 1, swept - 1)], runs)
     projected, direct = None, []
@@ -519,8 +563,8 @@
         totals, sums = totals + done, [sums]
     mix, lcms_gram = mix_pass(sweeps[0], pack, scan_factor, own.shape[2])
     ppm_new = ppm_pass(chip, mix, totals, projected, width)
-    fit = sum_over_mz(sums[0][0] + lax.ppermute(sums[0], "run", swap)[1], mzs)
-    sample_factor = sample_pass(fit, mix, lcms_gram, pack)
+    fits = from_mz(sums[0][0] + lax.ppermute(sums[0], "run", swap)[1], mzs)
+    sample_factor = sample_pass(fits, mix, lcms_gram, pack)
     return (sample_factor, ppm_new)
 
 

time: 167 us -> 150 us (0.90)
  Pallas kernels: 55.4 us -> 37.8 us
  waiting for transfers between devices: 37.9 us -> 44.9 us
  other arithmetic: 4.62 us -> 0.28 us
  local copies, waits for them, and re-layouts: 2.07 us -> 0.01 us
    pallas_call x9 -> x10, Pallas kernels: 50.9 us -> 35.7 us  [the longest x1 16.4 us: lcms_pass(): pl.pallas_call(lcms_body, name='lcms_pass', compiler_params=within(32), g...]
    ppermute x9, waiting for transfers between devices: 27.8 us -> 34.9 us  [from_chips(): lax.ppermute(values[step - 1], 'run', [(i, i ^ 2 * step) for i in range(r...]
    pallas_call x1, Pallas kernels: 4.53 us -> 2.12 us  [direct_pass(): pl.pallas_call(functools.partial(direct_body, chips, count), name='direct...]
    add x3 -> x2, other arithmetic: 2.25 us -> 0.02 us  [the longest x1 0.02 us: per_device(): pack = sum(from_mz(pack, mzs))]
    add x4, other arithmetic: 2.24 us -> 0.14 us  [sum_over_chips(): outward = send(part + across, [(1, 0), (2, 3)])]
    unnamed x46 -> x6, local copies, waits for them, and re-layouts: 2.07 us -> 0.01 us
  transfers between devices with their start and end apart: 33 -> 33, of which waited for: 9 -> 10; matrix products, arithmetic and copies ran while one was open for 2% -> 0% of each run, Pallas kernels for 22% -> 19%
where the time goes in v3:
time: 150 us; the launch traced here: 149 us
  starting transfers between devices  64.8 us (43%)
  waiting for transfers between devices  44.9 us (30%)
  Pallas kernels  37.8 us (25%)
    ppermute x9, starting transfers between devices, from_chips(): lax.ppermute(values[step - 1], 'run', [(i, i ^ 2 * step) for i in range(r...  38.8 us
    ppermute x9, waiting for transfers between devices, from_chips(): lax.ppermute(values[step - 1], 'run', [(i, i ^ 2 * step) for i in range(r...  34.9 us
    pallas_call x1, Pallas kernels, lcms_pass(): pl.pallas_call(lcms_body, name='lcms_pass', compiler_params=within(32), g...  16.4 us
    ppermute x12, starting transfers between devices, send(): return lax.ppermute(values, 'run', hops)  15.4 us
    ppermute x6, starting transfers between devices, from_mz(): result.append(lax.ppermute(values, 'mz', hops))  8.89 us
    ppermute x12, waiting for transfers between devices, send(): return lax.ppermute(values, 'run', hops)  6.65 us
    pallas_call x1, Pallas kernels, sort_pass(): pl.pallas_call(functools.partial(sort_body, blocks, swept), name='sort_pa...  5.39 us
    pallas_call x1, Pallas kernels, nmr_pass(): pl.pallas_call(functools.partial(nmr_body, blocks), name='nmr_pass', comp...  4.77 us
  transfers between devices with their start and end apart: 33, of which 10 were waited for; matrix products, arithmetic and copies ran while one was open for 0% of the time, Pallas kernels for 19%

profile of v3, /device:TPU:0, one launch (start us, length us, event | category | flops | bytes accessed | tf_op | source)
XLA Modules:
  0.0 148.9 jit_solution(17564273952058731719)
XLA Ops:
  0.7 5.4 %sort_pass.1 = (f32[8,64,1024]{2,1,0:T(8,128)S(1)}, f32[8,64,1024]{2,1,0:T(8,128)S(1)}, f32[4,2,64,256]{3,2,1,0:T(8,128)S(1)}, f32[4,2,64,256]{3,2,1,0:T(8,128)S(1)}, f32[4,2,64,256]{3,2,1,0:T(8,128)S(1)}) custom-call(s32[1]{0:T(128)} %bitcast.core_ref, s32[1]{0:T(128)} %bitcast.1.chip_ref, f32[64,16384]{1,0:T(8,128)} %refs_7_.2, f32[64,16384]{1,0:T(8,128)} %refs_7_.2, ...), custom_call_target="tpu_custom_call" | custom-call | flops 1048576 | bytes 8388608 | tf_op jit(solution)/shard_map/sort_pass/pallas_call | solution.py:73
  6.1 0.5 collective-permute-start.4
  6.6 2.7 %collective-permute-start.20 = (f32[4,2,64,256]{3,2,1,0:T(8,128)S(1)}, f32[4,2,64,256]{3,2,1,0:T(8,128)S(1)}, u32[]{:S(2)}, u32[]{:S(2)}) collective-permute-start(f32[4,2,64,256]{3,2,1,0:T(8,128)S(1)} %get-tuple-element.35), channel_id=1, source_target_pairs={{0,8},{4,12},{8,0},{12,4},{16,24},{20,28},{24,16},{28,20},{1,9},{5... | collective-permute-start | bytes 1572872 | tf_op jit(solution)/shard_map/ppermute | solution.py:505
  9.3 4.8 %nmr_pass.1.part_ref = f32[128,128]{1,0:T(8,128)S(1)} custom-call(s32[1]{0:T(128)} %bitcast.core_ref, f32[8,64,1024]{2,1,0:T(8,128)S(1)} %get-tuple-element.26.keep_ref.own_ref.refs_8_.refs_4_.refs_5_.refs_6_.refs_7_, f32[8,64,1024]{2,1,0:T(8,128)S(1)} %get-tuple-element.27.send_ref, f32[64,16384]{1,0:T(8,128)S(1)} %copy-done, f32[64,16384]{1,0:T(8,128)S(1)} %copy-done, ...), custom_call_target="tpu_custom_call" | custom-call | flops 1073741824 | bytes 6291456 | tf_op jit(solution)/shard_map/nmr_pass/pallas_call | solution.py:134
  14.1 16.4 %lcms_pass.1 = f32[128,128]{1,0:T(8,128)S(1)} custom-call(bf16[64,256,1024]{2,1,0:T(8,128)(2,1)} %lcms_ref.1, f32[64,256]{1,0:T(8,128)S(1)} %copy-done.2, f32[64,1024]{1,0:T(8,128)S(1)} %copy-done.1, f32[128,128]{1,0:T(8,128)S(1)} %nmr_pass.1.part_ref), custom_call_target="tpu_custom_call" | custom-call | flops 8589934592 | bytes 33554432 | tf_op jit(solution)/shard_map/lcms_pass/pallas_call | solution.py:175
  30.4 1.5 %collective-permute-start = (f32[128,128]{1,0:T(8,128)S(1)}, f32[128,128]{1,0:T(8,128)S(1)}, u32[]{:S(2)}, u32[]{:S(2)}) collective-permute-start(f32[128,128]{1,0:T(8,128)S(1)} %lcms_pass.1), channel_id=1, source_target_pairs={{0,1},{1,2},{2,3},{3,0},{4,5},{5,6},{6,7},{7,4},{8,9},{9,10},{10,1... | collective-permute-start | bytes 196616 | tf_op jit(solution)/shard_map/ppermute | solution.py:498
  31.9 1.5 %collective-permute-start.1 = (f32[128,128]{1,0:T(8,128)S(1)}, f32[128,128]{1,0:T(8,128)S(1)}, u32[]{:S(2)}, u32[]{:S(2)}) collective-permute-start(f32[128,128]{1,0:T(8,128)S(1)} %lcms_pass.1), channel_id=1, source_target_pairs={{0,2},{1,3},{2,0},{3,1},{4,6},{5,7},{6,4},{7,5},{8,10},{9,11},{10,... | collective-permute-start | bytes 196616 | tf_op jit(solution)/shard_map/ppermute | solution.py:498
  33.4 1.4 collective-permute-start.2
  34.9 0.7 collective-permute-done
  35.6 2.6 %collective-permute-start.21 = (f32[4,2,64,256]{3,2,1,0:T(8,128)S(1)}, f32[4,2,64,256]{3,2,1,0:T(8,128)S(1)}, u32[]{:S(2)}, u32[]{:S(2)}) collective-permute-start(f32[4,2,64,256]{3,2,1,0:T(8,128)S(1)} %get-tuple-element.36), channel_id=1, source_target_pairs={{0,16},{4,20},{8,24},{12,28},{16,0},{20,4},{24,8},{28,12},{1,17},{... | collective-permute-start | bytes 1572872 | tf_op jit(solution)/shard_map/ppermute | solution.py:505
  38.2 0.0 collective-permute-done.1
  38.2 1.1 collective-permute-start.22
  39.4 0.0 collective-permute-done.2
  39.4 0.6 collective-permute-start.3
  40.0 1.4 collective-permute-done.3.other_pack
  41.4 0.4 first_pass.1
  41.8 2.6 %collective-permute-start.11 = (f32[64,1152]{1,0:T(8,128)S(1)}, f32[64,1152]{1,0:T(8,128)S(1)}, u32[]{:S(2)}, u32[]{:S(2)}) collective-permute-start(f32[64,1152]{1,0:T(8,128)S(1)} %get-tuple-element.31.refs_0_), channel_id=1, source_target_pairs={{0,8},{4,12},{24,16},{28,20},{1,9},{5,13},{25,17},{29,21},{2,10},{... | collective-permute-start | bytes 884744 | tf_op jit(solution)/shard_map/ppermute | solution.py:517
  44.4 0.8 project_pass.1
  45.2 1.3 collective-permute-start.14
  46.6 25.6 %collective-permute-done.21.refs_13_ = f32[4,2,64,256]{3,2,1,0:T(8,128)S(1)} collective-permute-done((f32[4,2,64,256]{3,2,1,0:T(8,128)S(1)}, f32[4,2,64,256]{3,2,1,0:T(8,128)S(1)}, u32[]{:S(2)}, u32[]{:S(2)}) %collective-permute-start.21) | collective-permute-done | bytes 524320 | tf_op jit(solution)/shard_map/ppermute | solution.py:505
  72.1 2.4 %collective-permute-start.8 = (f32[64,1024]{1,0:T(8,128)S(1)}, f32[64,1024]{1,0:T(8,128)S(1)}, u32[]{:S(2)}, u32[]{:S(2)}) collective-permute-start(f32[64,1024]{1,0:T(8,128)S(1)} %get-tuple-element.30.refs_4_), channel_id=1, source_target_pairs={{0,8},{4,12},{24,16},{28,20},{1,9},{5,13},{25,17},{29,21},{2,10},{... | collective-permute-start | bytes 786440 | tf_op jit(solution)/shard_map/ppermute | solution.py:517
  74.5 1.3 collective-permute-start.5
  75.9 0.0 collective-permute-done.22.refs_14_
  75.9 0.7 collective-permute-start.12
  76.6 0.1 collective-permute-start.24
  76.7 0.0 collective-permute-done.14.refs_5_
  76.7 0.5 collective-permute-start.25
  77.2 4.0 %collective-permute-done.8.refs_5_ = f32[64,1024]{1,0:T(8,128)S(1)} collective-permute-done((f32[64,1024]{1,0:T(8,128)S(1)}, f32[64,1024]{1,0:T(8,128)S(1)}, u32[]{:S(2)}, u32[]{:S(2)}) %collective-permute-start.8) | collective-permute-done | bytes 262176 | tf_op jit(solution)/shard_map/ppermute | solution.py:517
  81.2 0.7 collective-permute-start.15
  81.9 2.6 %collective-permute-done.5.refs_1_ = f32[64,1024]{1,0:T(8,128)S(1)} collective-permute-done((f32[64,1024]{1,0:T(8,128)S(1)}, f32[64,1024]{1,0:T(8,128)S(1)}, u32[]{:S(2)}, u32[]{:S(2)}) %collective-permute-start.5) | collective-permute-done | bytes 262176 | tf_op jit(solution)/shard_map/ppermute | solution.py:517
  84.6 0.7 collective-permute-start.9
  85.3 0.7 collective-permute-start.6
  86.0 0.0 collective-permute-done.15.refs_6_
  86.0 1.3 collective-permute-start.13
  87.4 1.3 collective-permute-start.16
  88.7 0.0 collective-permute-done.6.refs_2_
  88.7 22.4 %collective-permute-start.17 = (f32[64,128]{1,0:T(8,128)S(1)}, f32[64,128]{1,0:T(8,128)S(1)}, u32[]{:S(2)}, u32[]{:S(2)}) collective-permute-start(f32[64,128]{1,0:T(8,128)S(1)} %get-tuple-element.34.refs_0_), channel_id=1, source_target_pairs={{0,8},{4,12},{8,0},{12,4},{16,24},{20,28},{24,16},{28,20},{1,9},{5... | collective-permute-start | bytes 98312 | tf_op jit(solution)/shard_map/ppermute | solution.py:505
  111.2 0.0 collective-permute-done.24.refs_16_
  111.2 1.3 collective-permute-start.10
  112.5 0.0 collective-permute-done.25.refs_17_
  112.5 1.3 collective-permute-start.7
  113.8 3.0 %collective-permute-start.18 = (f32[64,128]{1,0:T(8,128)S(1)}, f32[64,128]{1,0:T(8,128)S(1)}, u32[]{:S(2)}, u32[]{:S(2)}) collective-permute-start(f32[64,128]{1,0:T(8,128)S(1)} %get-tuple-element.34.refs_0_), channel_id=1, source_target_pairs={{0,16},{4,20},{8,24},{12,28},{16,0},{20,4},{24,8},{28,12},{1,17},{... | collective-permute-start | bytes 98312 | tf_op jit(solution)/shard_map/ppermute | solution.py:505
  116.8 2.0 %collective-permute-done.18.refs_2_ = f32[64,128]{1,0:T(8,128)S(1)} collective-permute-done((f32[64,128]{1,0:T(8,128)S(1)}, f32[64,128]{1,0:T(8,128)S(1)}, u32[]{:S(2)}, u32[]{:S(2)}) %collective-permute-start.18) | collective-permute-done | bytes 32800 | tf_op jit(solution)/shard_map/ppermute | solution.py:505
  118.8 2.5 %collective-permute-start.19 = (f32[64,128]{1,0:T(8,128)S(1)}, f32[64,128]{1,0:T(8,128)S(1)}, u32[]{:S(2)}, u32[]{:S(2)}) collective-permute-start(f32[64,128]{1,0:T(8,128)S(1)} %get-tuple-element.34.refs_0_), channel_id=1, source_target_pairs={{0,24},{4,28},{8,16},{12,20},{16,8},{20,12},{24,0},{28,4},{1,25},{... | collective-permute-start | bytes 98312 | tf_op jit(solution)/shard_map/ppermute | solution.py:505
  121.3 3.3 %collective-permute-done.19.refs_3_ = f32[64,128]{1,0:T(8,128)S(1)} collective-permute-done((f32[64,128]{1,0:T(8,128)S(1)}, f32[64,128]{1,0:T(8,128)S(1)}, u32[]{:S(2)}, u32[]{:S(2)}) %collective-permute-start.19) | collective-permute-done | bytes 32800 | tf_op jit(solution)/shard_map/ppermute | solution.py:505
  124.6 2.1 %direct_pass.1 = (f32[64,1024]{1,0:T(8,128)S(1)}, f32[2,64,128]{2,1,0:T(8,128)S(1)}, f32[2,64,128]{2,1,0:T(8,128)S(1)}, f32[2,64,128]{2,1,0:T(8,128)S(1)}, f32[2,64,128]{2,1,0:T(8,128)S(1)}) custom-call(s32[1]{0:T(128)} %bitcast.1.chip_ref, f32[64,128]{1,0:T(8,128)S(1)} %get-tuple-element.34.refs_0_, f32[64,128]{1,0:T(8,128)S(1)} %collective-permute-done.17.refs_1_, ...), custom_call_target="tpu_custom_call" | custom-call | flops 1073741824 | bytes 2097152 | tf_op jit(solution)/shard_map/direct_pass/pallas_call | solution.py:474
  126.7 0.9 collective-permute-start.26
  127.6 2.2 %collective-permute-start.27 = (f32[2,64,128]{2,1,0:T(8,128)S(1)}, f32[2,64,128]{2,1,0:T(8,128)S(1)}, u32[]{:S(2)}, u32[]{:S(2)}) collective-permute-start(f32[2,64,128]{2,1,0:T(8,128)S(1)} %get-tuple-element.40), channel_id=1, source_target_pairs={{0,16},{4,20},{8,24},{12,28},{16,0},{20,4},{24,8},{28,12},{1,17},{... | collective-permute-start | bytes 196616 | tf_op jit(solution)/shard_map/ppermute | solution.py:505
  129.8 1.3 collective-permute-start.28
  131.2 0.7 shard_map.68
  131.9 0.0 collective-permute-done.26.refs_12_
  132.0 0.8 collective-permute-done.27.refs_13_
  132.8 3.1 %collective-permute-done.28.refs_14_ = f32[2,64,128]{2,1,0:T(8,128)S(1)} collective-permute-done((f32[2,64,128]{2,1,0:T(8,128)S(1)}, f32[2,64,128]{2,1,0:T(8,128)S(1)}, u32[]{:S(2)}, u32[]{:S(2)}) %collective-permute-start.28) | collective-permute-done | bytes 65568 | tf_op jit(solution)/shard_map/ppermute | solution.py:505
  135.9 0.0 collective-permute-done.10.refs_7_
  135.9 0.0 collective-permute-done.7.refs_3_
  135.9 0.8 shard_map.69
  136.7 0.1 collective-permute-start.29
  136.8 1.2 collective-permute-done.29
  138.0 0.5 collective-permute-start.30
  138.5 1.5 %collective-permute-start.31 = (f32[64,128]{1,0:T(8,128)S(1)}, f32[64,128]{1,0:T(8,128)S(1)}, u32[]{:S(2)}, u32[]{:S(2)}) collective-permute-start(f32[64,128]{1,0:T(8,128)S(1)} %fusion.refs_0_), channel_id=1, source_target_pairs={{0,2},{1,3},{2,0},{3,1},{4,6},{5,7},{6,4},{7,5},{8,10},{9,11},{10,... | collective-permute-start | bytes 98312 | tf_op jit(solution)/shard_map/ppermute | solution.py:498
  140.1 2.4 %collective-permute-start.32 = (f32[64,128]{1,0:T(8,128)S(1)}, f32[64,128]{1,0:T(8,128)S(1)}, u32[]{:S(2)}, u32[]{:S(2)}) collective-permute-start(f32[64,128]{1,0:T(8,128)S(1)} %fusion.refs_0_), channel_id=1, source_target_pairs={{0,3},{1,0},{2,1},{3,2},{4,7},{5,4},{6,5},{7,6},{8,11},{9,8},{10,9... | collective-permute-start | bytes 98312 | tf_op jit(solution)/shard_map/ppermute | solution.py:498
  142.4 2.2 %mix_pass.1 = (f32[64,64]{1,0:T(8,128)S(1)}, f32[64,64]{1,0:T(8,128)S(1)}) custom-call(f32[64,1152]{1,0:T(8,128)S(1)} %get-tuple-element.31.refs_0_, f32[64,1152]{1,0:T(8,128)S(1)} %collective-permute-done.11.refs_1_, f32[64,1152]{1,0:T(8,128)S(1)} %collective-permute-done.12.refs_2_, f32[64,1152]{1,0:T(8,128)S(1)} %collective-permute-done.13.refs_3_, ...), custom_call_target="tpu_custom_call" | custom-call | flops 4194304 | bytes 65536 | tf_op jit(solution)/shard_map/mix_pass/pallas_call | solution.py:364
  144.7 1.2 ppm_pass.1
  145.9 3.0 %sample_pass.1 = f32[64,64]{1,0:T(8,128)} custom-call(f32[64,128]{1,0:T(8,128)S(1)} %fusion.refs_0_, f32[64,128]{1,0:T(8,128)S(1)} %collective-permute-done.30.refs_1_, f32[64,128]{1,0:T(8,128)S(1)} %collective-permute-done.31.refs_2_, f32[64,128]{1,0:T(8,128)S(1)} %collective-permute-done.32.refs_3_, f32[64,64]{1,0:T(8,128)S(1)} %get-tuple-element.43.refs_4_.mix_ref, ...), custom_call_target="tpu_custom_call" | custom-call | flops 4194304 | bytes 65536 | tf_op jit(solution)/shard_map/sample_pass/pallas_call | solution.py:389
  (29 shorter events, 0.3 us)
Async XLA Ops:
  0.6 8.6 %copy-start = (f32[64,16384]{1,0:T(8,128)S(1)}, f32[64,16384]{1,0:T(8,128)}, u32[]{:S(2)}) copy-start(f32[64,16384]{1,0:T(8,128)} %refs_7_.3) | copy-start | bytes 12582916
  0.7 8.6 %copy-start.1 = (f32[64,1024]{1,0:T(8,128)S(1)}, f32[64,1024]{1,0:T(8,128)}, u32[]{:S(2)}) copy-start(f32[64,1024]{1,0:T(8,128)} %mz_ref.1) | copy-start | bytes 786436
  6.1 35.3 %collective-permute-start.4 = (f32[8,64,1024]{2,1,0:T(8,128)S(1)}, f32[8,64,1024]{2,1,0:T(8,128)S(1)}, u32[]{:S(2)}, u32[]{:S(2)}) collective-permute-start(f32[8,64,1024]{2,1,0:T(8,128)S(1)} %get-tuple-element.27.send_ref), channel_id=1, source_target_pairs={{0,4},{4,0},{8,12},{12,8},{16,20},{20,16},{24,28},{28,24},{1,5},{5... | collective-permute-start | bytes 6291464 | tf_op jit(solution)/shard_map/ppermute | solution.py:547
  6.6 32.8 %collective-permute-start.20 = (f32[4,2,64,256]{3,2,1,0:T(8,128)S(1)}, f32[4,2,64,256]{3,2,1,0:T(8,128)S(1)}, u32[]{:S(2)}, u32[]{:S(2)}) collective-permute-start(f32[4,2,64,256]{3,2,1,0:T(8,128)S(1)} %get-tuple-element.35), channel_id=1, source_target_pairs={{0,8},{4,12},{8,0},{12,4},{16,24},{20,28},{24,16},{28,20},{1,9},{5... | collective-permute-start | bytes 1572872 | tf_op jit(solution)/shard_map/ppermute | solution.py:505
  9.3 4.8 %copy-start.2 = (f32[64,256]{1,0:T(8,128)S(1)}, f32[64,256]{1,0:T(8,128)}, u32[]{:S(2)}) copy-start(f32[64,256]{1,0:T(8,128)} %refs_5_.5) | copy-start | bytes 196612
  30.4 5.2 %collective-permute-start = (f32[128,128]{1,0:T(8,128)S(1)}, f32[128,128]{1,0:T(8,128)S(1)}, u32[]{:S(2)}, u32[]{:S(2)}) collective-permute-start(f32[128,128]{1,0:T(8,128)S(1)} %lcms_pass.1), channel_id=1, source_target_pairs={{0,1},{1,2},{2,3},{3,0},{4,5},{5,6},{6,7},{7,4},{8,9},{9,10},{10,1... | collective-permute-start | bytes 196616 | tf_op jit(solution)/shard_map/ppermute | solution.py:498
  31.9 6.3 %collective-permute-start.1 = (f32[128,128]{1,0:T(8,128)S(1)}, f32[128,128]{1,0:T(8,128)S(1)}, u32[]{:S(2)}, u32[]{:S(2)}) collective-permute-start(f32[128,128]{1,0:T(8,128)S(1)} %lcms_pass.1), channel_id=1, source_target_pairs={{0,2},{1,3},{2,0},{3,1},{4,6},{5,7},{6,4},{7,5},{8,10},{9,11},{10,... | collective-permute-start | bytes 196616 | tf_op jit(solution)/shard_map/ppermute | solution.py:498
  33.4 6.0 %collective-permute-start.2 = (f32[128,128]{1,0:T(8,128)S(1)}, f32[128,128]{1,0:T(8,128)S(1)}, u32[]{:S(2)}, u32[]{:S(2)}) collective-permute-start(f32[128,128]{1,0:T(8,128)S(1)} %lcms_pass.1), channel_id=1, source_target_pairs={{0,3},{1,0},{2,1},{3,2},{4,7},{5,4},{6,5},{7,6},{8,11},{9,8},{10,9... | collective-permute-start | bytes 196616 | tf_op jit(solution)/shard_map/ppermute | solution.py:498
  35.6 36.5 %collective-permute-start.21 = (f32[4,2,64,256]{3,2,1,0:T(8,128)S(1)}, f32[4,2,64,256]{3,2,1,0:T(8,128)S(1)}, u32[]{:S(2)}, u32[]{:S(2)}) collective-permute-start(f32[4,2,64,256]{3,2,1,0:T(8,128)S(1)} %get-tuple-element.36), channel_id=1, source_target_pairs={{0,16},{4,20},{8,24},{12,28},{16,0},{20,4},{24,8},{28,12},{1,17},{... | collective-permute-start | bytes 1572872 | tf_op jit(solution)/shard_map/ppermute | solution.py:505
  38.2 37.7 %collective-permute-start.22 = (f32[4,2,64,256]{3,2,1,0:T(8,128)S(1)}, f32[4,2,64,256]{3,2,1,0:T(8,128)S(1)}, u32[]{:S(2)}, u32[]{:S(2)}) collective-permute-start(f32[4,2,64,256]{3,2,1,0:T(8,128)S(1)} %get-tuple-element.37), channel_id=1, source_target_pairs={{0,24},{4,28},{8,16},{12,20},{16,8},{20,12},{24,0},{28,4},{1,25},{... | collective-permute-start | bytes 1572872 | tf_op jit(solution)/shard_map/ppermute | solution.py:505
  39.4 37.2 %collective-permute-start.23 = (f32[4,2,64,256]{3,2,1,0:T(8,128)S(1)}, f32[4,2,64,256]{3,2,1,0:T(8,128)S(1)}, u32[]{:S(2)}, u32[]{:S(2)}) collective-permute-start(f32[4,2,64,256]{3,2,1,0:T(8,128)S(1)} %collective-permute-done.20.refs_12_), channel_id=1, source_target_pairs={{0,4},{4,0},{8,12},{12,8},{16,20},{20,16},{24,28},{28,24},{1,5},{5... | collective-permute-start | bytes 1572872 | tf_op jit(solution)/shard_map/ppermute | solution.py:556
  39.4 2.0 %collective-permute-start.3 = (f32[128,128]{1,0:T(8,128)S(1)}, f32[128,128]{1,0:T(8,128)S(1)}, u32[]{:S(2)}, u32[]{:S(2)}) collective-permute-start(f32[128,128]{1,0:T(8,128)S(1)} %add_add_fusion.own_pack.refs_4_.refs_6_), channel_id=1, source_target_pairs={{0,4},{4,0},{8,12},{12,8},{16,20},{20,16},{24,28},{28,24},{1,5},{5... | collective-permute-start | bytes 196616 | tf_op jit(solution)/shard_map/ppermute | solution.py:551
  41.8 32.7 %collective-permute-start.11 = (f32[64,1152]{1,0:T(8,128)S(1)}, f32[64,1152]{1,0:T(8,128)S(1)}, u32[]{:S(2)}, u32[]{:S(2)}) collective-permute-start(f32[64,1152]{1,0:T(8,128)S(1)} %get-tuple-element.31.refs_0_), channel_id=1, source_target_pairs={{0,8},{4,12},{24,16},{28,20},{1,9},{5,13},{25,17},{29,21},{2,10},{... | collective-permute-start | bytes 884744 | tf_op jit(solution)/shard_map/ppermute | solution.py:517
  45.2 31.4 %collective-permute-start.14 = (f32[64,1024]{1,0:T(8,128)S(1)}, f32[64,1024]{1,0:T(8,128)S(1)}, u32[]{:S(2)}, u32[]{:S(2)}) collective-permute-start(f32[64,1024]{1,0:T(8,128)S(1)} %get-tuple-element.32.refs_4_), channel_id=1, source_target_pairs={{0,8},{4,12},{24,16},{28,20},{1,9},{5,13},{25,17},{29,21},{2,10},{... | collective-permute-start | bytes 786440 | tf_op jit(solution)/shard_map/ppermute | solution.py:517
  72.1 9.1 %collective-permute-start.8 = (f32[64,1024]{1,0:T(8,128)S(1)}, f32[64,1024]{1,0:T(8,128)S(1)}, u32[]{:S(2)}, u32[]{:S(2)}) collective-permute-start(f32[64,1024]{1,0:T(8,128)S(1)} %get-tuple-element.30.refs_4_), channel_id=1, source_target_pairs={{0,8},{4,12},{24,16},{28,20},{1,9},{5,13},{25,17},{29,21},{2,10},{... | collective-permute-start | bytes 786440 | tf_op jit(solution)/shard_map/ppermute | solution.py:517
  74.5 10.0 %collective-permute-start.5 = (f32[64,1024]{1,0:T(8,128)S(1)}, f32[64,1024]{1,0:T(8,128)S(1)}, u32[]{:S(2)}, u32[]{:S(2)}) collective-permute-start(f32[64,1024]{1,0:T(8,128)S(1)} %get-tuple-element.29.refs_0_), channel_id=1, source_target_pairs={{0,8},{4,12},{24,16},{28,20},{1,9},{5,13},{25,17},{29,21},{2,10},{... | collective-permute-start | bytes 786440 | tf_op jit(solution)/shard_map/ppermute | solution.py:517
  75.9 9.4 %collective-permute-start.12 = (f32[64,1152]{1,0:T(8,128)S(1)}, f32[64,1152]{1,0:T(8,128)S(1)}, u32[]{:S(2)}, u32[]{:S(2)}) collective-permute-start(f32[64,1152]{1,0:T(8,128)S(1)} %add.51), channel_id=1, source_target_pairs={{8,16},{12,20},{16,8},{20,12},{9,17},{13,21},{17,9},{21,13},{10,18... | collective-permute-start | bytes 884744 | tf_op jit(solution)/shard_map/ppermute | solution.py:517
  76.6 34.6 %collective-permute-start.24 = (f32[4,2,64,256]{3,2,1,0:T(8,128)S(1)}, f32[4,2,64,256]{3,2,1,0:T(8,128)S(1)}, u32[]{:S(2)}, u32[]{:S(2)}) collective-permute-start(f32[4,2,64,256]{3,2,1,0:T(8,128)S(1)} %collective-permute-done.21.refs_13_), channel_id=1, source_target_pairs={{0,4},{4,0},{8,12},{12,8},{16,20},{20,16},{24,28},{28,24},{1,5},{5... | collective-permute-start | bytes 1572872 | tf_op jit(solution)/shard_map/ppermute | solution.py:556
  76.7 35.8 %collective-permute-start.25 = (f32[4,2,64,256]{3,2,1,0:T(8,128)S(1)}, f32[4,2,64,256]{3,2,1,0:T(8,128)S(1)}, u32[]{:S(2)}, u32[]{:S(2)}) collective-permute-start(f32[4,2,64,256]{3,2,1,0:T(8,128)S(1)} %collective-permute-done.22.refs_14_), channel_id=1, source_target_pairs={{0,4},{4,0},{8,12},{12,8},{16,20},{20,16},{24,28},{28,24},{1,5},{5... | collective-permute-start | bytes 1572872 | tf_op jit(solution)/shard_map/ppermute | solution.py:556
  81.2 4.8 %collective-permute-start.15 = (f32[64,1024]{1,0:T(8,128)S(1)}, f32[64,1024]{1,0:T(8,128)S(1)}, u32[]{:S(2)}, u32[]{:S(2)}) collective-permute-start(f32[64,1024]{1,0:T(8,128)S(1)} %add.53), channel_id=1, source_target_pairs={{8,16},{12,20},{16,8},{20,12},{9,17},{13,21},{17,9},{21,13},{10,18... | collective-permute-start | bytes 786440 | tf_op jit(solution)/shard_map/ppermute | solution.py:517
  84.6 2.8 %collective-permute-start.9 = (f32[64,1024]{1,0:T(8,128)S(1)}, f32[64,1024]{1,0:T(8,128)S(1)}, u32[]{:S(2)}, u32[]{:S(2)}) collective-permute-start(f32[64,1024]{1,0:T(8,128)S(1)} %add.49), channel_id=1, source_target_pairs={{8,16},{12,20},{16,8},{20,12},{9,17},{13,21},{17,9},{21,13},{10,18... | collective-permute-start | bytes 786440 | tf_op jit(solution)/shard_map/ppermute | solution.py:517
  85.3 3.4 %collective-permute-start.6 = (f32[64,1024]{1,0:T(8,128)S(1)}, f32[64,1024]{1,0:T(8,128)S(1)}, u32[]{:S(2)}, u32[]{:S(2)}) collective-permute-start(f32[64,1024]{1,0:T(8,128)S(1)} %add.47), channel_id=1, source_target_pairs={{8,16},{12,20},{16,8},{20,12},{9,17},{13,21},{17,9},{21,13},{10,18... | collective-permute-start | bytes 786440 | tf_op jit(solution)/shard_map/ppermute | solution.py:517
  86.0 43.8 %collective-permute-start.13 = (f32[64,1152]{1,0:T(8,128)S(1)}, f32[64,1152]{1,0:T(8,128)S(1)}, u32[]{:S(2)}, u32[]{:S(2)}) collective-permute-start(f32[64,1152]{1,0:T(8,128)S(1)} %add.52), channel_id=1, source_target_pairs={{8,0},{12,4},{16,24},{20,28},{9,1},{13,5},{17,25},{21,29},{10,2},{... | collective-permute-start | bytes 884744 | tf_op jit(solution)/shard_map/ppermute | solution.py:517
  87.4 40.3 %collective-permute-start.16 = (f32[64,1024]{1,0:T(8,128)S(1)}, f32[64,1024]{1,0:T(8,128)S(1)}, u32[]{:S(2)}, u32[]{:S(2)}) collective-permute-start(f32[64,1024]{1,0:T(8,128)S(1)} %add.54), channel_id=1, source_target_pairs={{8,0},{12,4},{16,24},{20,28},{9,1},{13,5},{17,25},{21,29},{10,2},{... | collective-permute-start | bytes 786440 | tf_op jit(solution)/shard_map/ppermute | solution.py:517
  88.7 25.1 %collective-permute-start.17 = (f32[64,128]{1,0:T(8,128)S(1)}, f32[64,128]{1,0:T(8,128)S(1)}, u32[]{:S(2)}, u32[]{:S(2)}) collective-permute-start(f32[64,128]{1,0:T(8,128)S(1)} %get-tuple-element.34.refs_0_), channel_id=1, source_target_pairs={{0,8},{4,12},{8,0},{12,4},{16,24},{20,28},{24,16},{28,20},{1,9},{5... | collective-permute-start | bytes 98312 | tf_op jit(solution)/shard_map/ppermute | solution.py:505
  111.2 24.7 %collective-permute-start.10 = (f32[64,1024]{1,0:T(8,128)S(1)}, f32[64,1024]{1,0:T(8,128)S(1)}, u32[]{:S(2)}, u32[]{:S(2)}) collective-permute-start(f32[64,1024]{1,0:T(8,128)S(1)} %add.50), channel_id=1, source_target_pairs={{8,0},{12,4},{16,24},{20,28},{9,1},{13,5},{17,25},{21,29},{10,2},{... | collective-permute-start | bytes 786440 | tf_op jit(solution)/shard_map/ppermute | solution.py:517
  112.5 23.4 %collective-permute-start.7 = (f32[64,1024]{1,0:T(8,128)S(1)}, f32[64,1024]{1,0:T(8,128)S(1)}, u32[]{:S(2)}, u32[]{:S(2)}) collective-permute-start(f32[64,1024]{1,0:T(8,128)S(1)} %add.48), channel_id=1, source_target_pairs={{8,0},{12,4},{16,24},{20,28},{9,1},{13,5},{17,25},{21,29},{10,2},{... | collective-permute-start | bytes 786440 | tf_op jit(solution)/shard_map/ppermute | solution.py:517
  113.8 5.0 %collective-permute-start.18 = (f32[64,128]{1,0:T(8,128)S(1)}, f32[64,128]{1,0:T(8,128)S(1)}, u32[]{:S(2)}, u32[]{:S(2)}) collective-permute-start(f32[64,128]{1,0:T(8,128)S(1)} %get-tuple-element.34.refs_0_), channel_id=1, source_target_pairs={{0,16},{4,20},{8,24},{12,28},{16,0},{20,4},{24,8},{28,12},{1,17},{... | collective-permute-start | bytes 98312 | tf_op jit(solution)/shard_map/ppermute | solution.py:505
  118.8 5.8 %collective-permute-start.19 = (f32[64,128]{1,0:T(8,128)S(1)}, f32[64,128]{1,0:T(8,128)S(1)}, u32[]{:S(2)}, u32[]{:S(2)}) collective-permute-start(f32[64,128]{1,0:T(8,128)S(1)} %get-tuple-element.34.refs_0_), channel_id=1, source_target_pairs={{0,24},{4,28},{8,16},{12,20},{16,8},{20,12},{24,0},{28,4},{1,25},{... | collective-permute-start | bytes 98312 | tf_op jit(solution)/shard_map/ppermute | solution.py:505
  126.7 5.2 %collective-permute-start.26 = (f32[2,64,128]{2,1,0:T(8,128)S(1)}, f32[2,64,128]{2,1,0:T(8,128)S(1)}, u32[]{:S(2)}, u32[]{:S(2)}) collective-permute-start(f32[2,64,128]{2,1,0:T(8,128)S(1)} %get-tuple-element.39), channel_id=1, source_target_pairs={{0,8},{4,12},{8,0},{12,4},{16,24},{20,28},{24,16},{28,20},{1,9},{5... | collective-permute-start | bytes 196616 | tf_op jit(solution)/shard_map/ppermute | solution.py:505
  127.6 5.2 %collective-permute-start.27 = (f32[2,64,128]{2,1,0:T(8,128)S(1)}, f32[2,64,128]{2,1,0:T(8,128)S(1)}, u32[]{:S(2)}, u32[]{:S(2)}) collective-permute-start(f32[2,64,128]{2,1,0:T(8,128)S(1)} %get-tuple-element.40), channel_id=1, source_target_pairs={{0,16},{4,20},{8,24},{12,28},{16,0},{20,4},{24,8},{28,12},{1,17},{... | collective-permute-start | bytes 196616 | tf_op jit(solution)/shard_map/ppermute | solution.py:505
  129.8 6.1 %collective-permute-start.28 = (f32[2,64,128]{2,1,0:T(8,128)S(1)}, f32[2,64,128]{2,1,0:T(8,128)S(1)}, u32[]{:S(2)}, u32[]{:S(2)}) collective-permute-start(f32[2,64,128]{2,1,0:T(8,128)S(1)} %get-tuple-element.41), channel_id=1, source_target_pairs={{0,24},{4,28},{8,16},{12,20},{16,8},{20,12},{24,0},{28,4},{1,25},{... | collective-permute-start | bytes 196616 | tf_op jit(solution)/shard_map/ppermute | solution.py:505
  136.7 1.3 collective-permute-start.29
  138.0 7.9 %collective-permute-start.30 = (f32[64,128]{1,0:T(8,128)S(1)}, f32[64,128]{1,0:T(8,128)S(1)}, u32[]{:S(2)}, u32[]{:S(2)}) collective-permute-start(f32[64,128]{1,0:T(8,128)S(1)} %fusion.refs_0_), channel_id=1, source_target_pairs={{0,1},{1,2},{2,3},{3,0},{4,5},{5,6},{6,7},{7,4},{8,9},{9,10},{10,1... | collective-permute-start | bytes 98312 | tf_op jit(solution)/shard_map/ppermute | solution.py:498
  138.5 7.3 %collective-permute-start.31 = (f32[64,128]{1,0:T(8,128)S(1)}, f32[64,128]{1,0:T(8,128)S(1)}, u32[]{:S(2)}, u32[]{:S(2)}) collective-permute-start(f32[64,128]{1,0:T(8,128)S(1)} %fusion.refs_0_), channel_id=1, source_target_pairs={{0,2},{1,3},{2,0},{3,1},{4,6},{5,7},{6,4},{7,5},{8,10},{9,11},{10,... | collective-permute-start | bytes 98312 | tf_op jit(solution)/shard_map/ppermute | solution.py:498
  140.1 5.8 %collective-permute-start.32 = (f32[64,128]{1,0:T(8,128)S(1)}, f32[64,128]{1,0:T(8,128)S(1)}, u32[]{:S(2)}, u32[]{:S(2)}) collective-permute-start(f32[64,128]{1,0:T(8,128)S(1)} %fusion.refs_0_), channel_id=1, source_target_pairs={{0,3},{1,0},{2,1},{3,2},{4,7},{5,4},{6,5},{7,6},{8,11},{9,8},{10,9... | collective-permute-start | bytes 98312 | tf_op jit(solution)/shard_map/ppermute | solution.py:498

commit v4 on v3

--- a/solution.py
+++ b/solution.py
@@ -39,47 +39,53 @@
     return pl.BlockSpec(shape, lambda *_: (0,) * len(shape))
 
 
-def sort_body(blocks, swept, core_ref, chip_ref, *refs):
+def sort_body(blocks, first, core_ref, chip_ref, *refs):
     spectra_refs, (keep_ref, send_ref, *parcels) = refs[: 2 * blocks], refs[2 * blocks :]
-    width = spectra_refs[0].shape[1]
+    count, width = keep_ref.shape[0], keep_ref.shape[2] // blocks
     for core in (0, 1):
 
         @pl.when(core_ref[0] == core)
         def _():
             for b in range(blocks):
-                keep_ref[0, :, b * width : (b + 1) * width] = spectra_refs[2 * b + core][...]
-                send_ref[0, :, b * width : (b + 1) * width] = spectra_refs[2 * b + 1 - core][...]
+                for j in range(count):
+                    taken = slice(j * width, (j + 1) * width)
+                    keep_ref[j, :, b * width : (b + 1) * width] = spectra_refs[2 * b + core][:, taken]
+                    send_ref[j, :, b * width : (b + 1) * width] = spectra_refs[2 * b + 1 - core][:, taken]
 
     if parcels:
 
-        @pl.when(pl.program_id(0) >= swept)
+        @pl.when(pl.program_id(0) >= first)
         def _():
             for step, parcel in enumerate(parcels, 1):
                 columns = pl.ds(pl.multiple_of((chip_ref[0] ^ step) * width, width), width)
-                parcel[0, 0] = keep_ref[0, :, columns]
-                parcel[0, 1] = send_ref[0, :, columns]
+                for j in range(count):
+                    parcel[j, 0] = keep_ref[j, :, columns]
+                    parcel[j, 1] = send_ref[j, :, columns]
 
 
 def sort_pass(core, chip, spectra, blocks, pieces, swept):
     samples, positions = spectra.shape
     width = positions // (2 * blocks * pieces)
+    count = 2 if pieces % 2 == 0 and swept % 2 == 0 else 1
+    steps, first = pieces // count, swept // count
     columns = [
-        pl.BlockSpec((samples, width), functools.partial(lambda b, k, c, h: (0, b * pieces + k), b))
+        pl.BlockSpec((samples, count * width), functools.partial(lambda b, k, c, h: (0, b * steps + k), b))
         for b in range(2 * blocks)
     ]
     sorted_shape = jax.ShapeDtypeStruct((pieces, samples, blocks * width), F32)
     parcels = blocks - 1 if swept < pieces else 0
     parcel_shape = jax.ShapeDtypeStruct((pieces - swept, 2, samples, width), F32)
-    return pl.pallas_call(
-        functools.partial(sort_body, blocks, swept),
+    parcel_spec = pl.BlockSpec((count, 2, samples, width), lambda k, c, h: (jnp.maximum(k - first, 0), 0, 0, 0))
+    return pl.pallas_call(
+        functools.partial(sort_body, blocks, first),
         name="sort_pass",
-        compiler_params=within(12),
+        compiler_params=within(16),
         grid_spec=pltpu.PrefetchScalarGridSpec(
             num_scalar_prefetch=2,
-            grid=(pieces,),
+            grid=(steps,),
             in_specs=columns,
-            out_specs=[pl.BlockSpec((1, samples, blocks * width), lambda k, c, h: (k, 0, 0))] * 2
-            + [pl.BlockSpec((1, 2, samples, width), lambda k, c, h: (jnp.maximum(k - swept, 0), 0, 0, 0))] * parcels,
+            out_specs=[pl.BlockSpec((count, samples, blocks * width), lambda k, c, h: (k, 0, 0))] * 2
+            + [parcel_spec] * parcels,
         ),
         out_shape=[sorted_shape, sorted_shape] + [parcel_shape] * parcels,
         cost_estimate=cost(1 << 20, 4 * 2 * 64 * positions),
@@ -171,7 +177,7 @@
 def lcms_pass(lcms, scan_factor, mz_factor, part):
     samples, steps, channels = lcms.shape
     rank = mz_factor.shape[0]
-    count = 8
+    count = 16
     return pl.pallas_call(
         lcms_body,
         name="lcms_pass",
@@ -287,11 +293,20 @@
         sums = products if sums is None else sums + products
     sums = sums[:, :rank] + sums[:, rank:]
     gram = sums[4 * samples : 4 * samples + rank] + sums[4 * samples + rank :]
+    fits = [
+        sums[side * samples : (side + 1) * samples] + sums[(side + 2) * samples : (side + 3) * samples]
+        for side in (0, 1)
+    ]
+    for ref in refs[2 : 2 + earlier]:
+        if len(ref.shape) == 3:
+            continue
+        fits = [fits[side] + ref[:samples, side * rank : (side + 1) * rank] for side in (0, 1)]
+        gram = gram + jnp.concatenate([ref[samples:, :rank], ref[samples:, rank:]], axis=0)
     for side in (0, 1):
-        fit = sums[side * samples : (side + 1) * samples] + sums[(side + 2) * samples : (side + 3) * samples]
-        total = jnp.concatenate([fit, gram], axis=1)
+        total = jnp.concatenate([fits[side], gram], axis=1)
         for ref in refs[2 : 2 + earlier]:
-            total = total + ref[side]
+            if len(ref.shape) == 3:
+                total = total + ref[side]
         sums_ref[side] = total
 
 
@@ -308,7 +323,7 @@
         grid=(1,),
         in_specs=[pl.BlockSpec(memory_space=pltpu.VMEM)] * len(arrays)
         + [pieces, pieces]
-        + [whole(sums_shape)] * len(earlier),
+        + [whole(array.shape) for array in earlier],
         out_specs=[whole(sums_shape)] + [whole((rank, columns))] * count,
         out_shape=[jax.ShapeDtypeStruct(sums_shape, F32)]
         + [jax.ShapeDtypeStruct((rank, columns), F32)] * count,
@@ -459,8 +474,8 @@
     for x in range(chips):
         fit = sums[x][: 2 * samples] + sums[x][2 * samples :]
         fit = fit[:, :rank] + fit[:, rank:]
-        for side in (0, 1):
-            sums_refs[x][side] = jnp.concatenate([fit[side * samples : (side + 1) * samples], gram], axis=1)
+        sums_refs[x][:samples] = jnp.concatenate([fit[:samples], fit[samples:]], axis=1)
+        sums_refs[x][samples:] = jnp.concatenate([gram[: rank // 2], gram[rank // 2 :]], axis=1)
 
 
 def direct_pass(chip, rows, own, other, came, swapped, first):
@@ -483,10 +498,10 @@
             + pieces
             + [pl.BlockSpec((count, 1, samples, width), lambda i, c: (0, 0, 0, 0))] * (chips - 1)
             + [pl.BlockSpec((count, 1, samples, width), lambda i, c: (0, 1, 0, 0))] * (chips - 1),
-            out_specs=[whole((rank, count * width))] + [whole((2, samples, 2 * rank))] * chips,
+            out_specs=[whole((rank, count * width))] + [whole((samples + rank // 2, 2 * rank))] * chips,
         ),
         out_shape=[jax.ShapeDtypeStruct((rank, count * width), F32)]
-        + [jax.ShapeDtypeStruct((2, samples, 2 * rank), F32)] * chips,
+        + [jax.ShapeDtypeStruct((samples + rank // 2, 2 * rank), F32)] * chips,
         cost_estimate=cost(2 * 512 * 512 * count * width * 2, 4 * 512 * count * width),
     )(chip, *rows, *([own] * count), *([other] * count), *came, *swapped)
 

time: 150 us -> 164 us (1.093)
  waiting for transfers between devices: 44.9 us -> 69.3 us
  starting transfers between devices: 64.8 us -> 58.7 us
  Pallas kernels: 37.8 us -> 34.5 us
    ppermute x12, waiting for transfers between devices: 6.65 us -> 28.9 us  [send(): return lax.ppermute(values, 'run', hops)]
    ppermute x9, starting transfers between devices: 38.8 us -> 29 us  [from_chips(): lax.ppermute(values[step - 1], 'run', [(i, i ^ 2 * step) for i in range(r...]
    ppermute x12, starting transfers between devices: 15.4 us -> 18.5 us  [send(): return lax.ppermute(values, 'run', hops)]
    ppermute x9, waiting for transfers between devices: 34.9 us -> 37.9 us  [from_chips(): lax.ppermute(values[step - 1], 'run', [(i, i ^ 2 * step) for i in range(r...]
    pallas_call x1, Pallas kernels: 16.4 us -> 14.7 us  [lcms_pass(): pl.pallas_call(lcms_body, name='lcms_pass', compiler_params=within(32), g...]
  transfers between devices with their start and end apart: 33 -> 33, of which waited for: 10 -> 12; matrix products, arithmetic and copies ran while one was open for 0% -> 0% of each run, Pallas kernels for 19% -> 16%
where the time goes in v4:
time: 164 us
  waiting for transfers between devices  69.3 us (42%)
  starting transfers between devices  58.7 us (36%)
  Pallas kernels  34.5 us (21%)
    ppermute x9, waiting for transfers between devices, from_chips(): lax.ppermute(values[step - 1], 'run', [(i, i ^ 2 * step) for i in range(r...  37.9 us
    ppermute x9, starting transfers between devices, from_chips(): lax.ppermute(values[step - 1], 'run', [(i, i ^ 2 * step) for i in range(r...  29 us
    ppermute x12, waiting for transfers between devices, send(): return lax.ppermute(values, 'run', hops)  28.9 us
    ppermute x12, starting transfers between devices, send(): return lax.ppermute(values, 'run', hops)  18.5 us
    pallas_call x1, Pallas kernels, lcms_pass(): pl.pallas_call(lcms_body, name='lcms_pass', compiler_params=within(32), g...  14.7 us
    ppermute x6, starting transfers between devices, from_mz(): result.append(lax.ppermute(values, 'mz', hops))  10.4 us
    pallas_call x1, Pallas kernels, nmr_pass(): pl.pallas_call(functools.partial(nmr_body, blocks), name='nmr_pass', comp...  4.76 us
    pallas_call x1, Pallas kernels, sort_pass(): pl.pallas_call(functools.partial(sort_body, blocks, first), name='sort_pa...  3.76 us
  transfers between devices with their start and end apart: 33, of which 12 were waited for; matrix products, arithmetic and copies ran while one was open for 0% of the time, Pallas kernels for 16%

profile of v4, /device:TPU:0, one launch (start us, length us, event | category | flops | bytes accessed | tf_op | source)
XLA Modules:
  0.0 163.8 jit_solution(1760845527859670145)
XLA Ops:
  0.7 3.8 %sort_pass.1 = (f32[8,64,1024]{2,1,0:T(8,128)S(1)}, f32[8,64,1024]{2,1,0:T(8,128)S(1)}, f32[4,2,64,256]{3,2,1,0:T(8,128)S(1)}, f32[4,2,64,256]{3,2,1,0:T(8,128)S(1)}, f32[4,2,64,256]{3,2,1,0:T(8,128)S(1)}) custom-call(s32[1]{0:T(128)} %bitcast.core_ref, s32[1]{0:T(128)} %bitcast.1.chip_ref, f32[64,16384]{1,0:T(8,128)} %refs_7_.2, f32[64,16384]{1,0:T(8,128)} %refs_7_.2, ...), custom_call_target="tpu_custom_call" | custom-call | flops 1048576 | bytes 8388608 | tf_op jit(solution)/shard_map/sort_pass/pallas_call | solution.py:79
  4.4 0.6 collective-permute-start.4
  5.0 4.8 %nmr_pass.1.part_ref = f32[128,128]{1,0:T(8,128)S(1)} custom-call(s32[1]{0:T(128)} %bitcast.core_ref, f32[8,64,1024]{2,1,0:T(8,128)S(1)} %get-tuple-element.26.keep_ref.own_ref.refs_8_.refs_4_.refs_5_.refs_6_.refs_7_, f32[8,64,1024]{2,1,0:T(8,128)S(1)} %get-tuple-element.27.send_ref, f32[64,16384]{1,0:T(8,128)S(1)} %copy-done, f32[64,16384]{1,0:T(8,128)S(1)} %copy-done, ...), custom_call_target="tpu_custom_call" | custom-call | flops 1073741824 | bytes 6291456 | tf_op jit(solution)/shard_map/nmr_pass/pallas_call | solution.py:140
  9.8 14.7 %lcms_pass.1 = f32[128,128]{1,0:T(8,128)S(1)} custom-call(bf16[64,256,1024]{2,1,0:T(8,128)(2,1)} %lcms_ref.1, f32[64,256]{1,0:T(8,128)S(1)} %copy-done.2, f32[64,1024]{1,0:T(8,128)S(1)} %copy-done.1, f32[128,128]{1,0:T(8,128)S(1)} %nmr_pass.1.part_ref), custom_call_target="tpu_custom_call" | custom-call | flops 8589934592 | bytes 33554432 | tf_op jit(solution)/shard_map/lcms_pass/pallas_call | solution.py:181
  24.5 2.6 %collective-permute-start = (f32[128,128]{1,0:T(8,128)S(1)}, f32[128,128]{1,0:T(8,128)S(1)}, u32[]{:S(2)}, u32[]{:S(2)}) collective-permute-start(f32[128,128]{1,0:T(8,128)S(1)} %lcms_pass.1), channel_id=1, source_target_pairs={{0,1},{1,2},{2,3},{3,0},{4,5},{5,6},{6,7},{7,4},{8,9},{9,10},{10,1... | collective-permute-start | bytes 196616 | tf_op jit(solution)/shard_map/ppermute | solution.py:513
  27.1 1.5 collective-permute-start.1
  28.6 1.4 collective-permute-start.2
  30.0 1.6 collective-permute-start.20
  31.6 0.0 collective-permute-done
  31.6 0.5 collective-permute-done.1
  32.1 0.8 collective-permute-done.2
  32.9 0.1 collective-permute-start.3
  33.0 2.6 %collective-permute-start.21 = (f32[4,2,64,256]{3,2,1,0:T(8,128)S(1)}, f32[4,2,64,256]{3,2,1,0:T(8,128)S(1)}, u32[]{:S(2)}, u32[]{:S(2)}) collective-permute-start(f32[4,2,64,256]{3,2,1,0:T(8,128)S(1)} %get-tuple-element.36), channel_id=1, source_target_pairs={{0,16},{4,20},{8,24},{12,28},{16,0},{20,4},{24,8},{28,12},{1,17},{... | collective-permute-start | bytes 1572872 | tf_op jit(solution)/shard_map/ppermute | solution.py:520
  35.6 0.4 first_pass.1
  36.1 3.5 %collective-permute-start.11 = (f32[64,1152]{1,0:T(8,128)S(1)}, f32[64,1152]{1,0:T(8,128)S(1)}, u32[]{:S(2)}, u32[]{:S(2)}) collective-permute-start(f32[64,1152]{1,0:T(8,128)S(1)} %get-tuple-element.31.refs_0_), channel_id=1, source_target_pairs={{0,8},{4,12},{24,16},{28,20},{1,9},{5,13},{25,17},{29,21},{2,10},{... | collective-permute-start | bytes 884744 | tf_op jit(solution)/shard_map/ppermute | solution.py:532
  39.6 1.1 collective-permute-start.22
  40.7 0.8 project_pass.1
  41.5 1.3 collective-permute-start.14
  42.8 9.2 %collective-permute-done.20.refs_12_ = f32[4,2,64,256]{3,2,1,0:T(8,128)S(1)} collective-permute-done((f32[4,2,64,256]{3,2,1,0:T(8,128)S(1)}, f32[4,2,64,256]{3,2,1,0:T(8,128)S(1)}, u32[]{:S(2)}, u32[]{:S(2)}) %collective-permute-start.20) | collective-permute-done | bytes 524320 | tf_op jit(solution)/shard_map/ppermute | solution.py:520
  52.0 1.5 collective-permute-start.8
  53.4 8.1 %collective-permute-done.11.refs_1_ = f32[64,1152]{1,0:T(8,128)S(1)} collective-permute-done((f32[64,1152]{1,0:T(8,128)S(1)}, f32[64,1152]{1,0:T(8,128)S(1)}, u32[]{:S(2)}, u32[]{:S(2)}) %collective-permute-start.11) | collective-permute-done | bytes 294944 | tf_op jit(solution)/shard_map/ppermute | solution.py:532
  61.5 4.4 %collective-permute-start.5 = (f32[64,1024]{1,0:T(8,128)S(1)}, f32[64,1024]{1,0:T(8,128)S(1)}, u32[]{:S(2)}, u32[]{:S(2)}) collective-permute-start(f32[64,1024]{1,0:T(8,128)S(1)} %get-tuple-element.29.refs_0_), channel_id=1, source_target_pairs={{0,8},{4,12},{24,16},{28,20},{1,9},{5,13},{25,17},{29,21},{2,10},{... | collective-permute-start | bytes 786440 | tf_op jit(solution)/shard_map/ppermute | solution.py:532
  65.9 12.5 %collective-permute-done.14.refs_5_ = f32[64,1024]{1,0:T(8,128)S(1)} collective-permute-done((f32[64,1024]{1,0:T(8,128)S(1)}, f32[64,1024]{1,0:T(8,128)S(1)}, u32[]{:S(2)}, u32[]{:S(2)}) %collective-permute-start.14) | collective-permute-done | bytes 262176 | tf_op jit(solution)/shard_map/ppermute | solution.py:532
  78.4 0.7 collective-permute-start.12
  79.1 0.0 collective-permute-done.21.refs_13_
  79.1 0.7 collective-permute-start.15
  79.8 0.1 collective-permute-start.23
  79.9 4.1 %collective-permute-done.8.refs_5_ = f32[64,1024]{1,0:T(8,128)S(1)} collective-permute-done((f32[64,1024]{1,0:T(8,128)S(1)}, f32[64,1024]{1,0:T(8,128)S(1)}, u32[]{:S(2)}, u32[]{:S(2)}) %collective-permute-start.8) | collective-permute-done | bytes 262176 | tf_op jit(solution)/shard_map/ppermute | solution.py:532
  84.0 4.2 %collective-permute-done.5.refs_1_ = f32[64,1024]{1,0:T(8,128)S(1)} collective-permute-done((f32[64,1024]{1,0:T(8,128)S(1)}, f32[64,1024]{1,0:T(8,128)S(1)}, u32[]{:S(2)}, u32[]{:S(2)}) %collective-permute-start.5) | collective-permute-done | bytes 262176 | tf_op jit(solution)/shard_map/ppermute | solution.py:532
  88.3 0.0 collective-permute-start.25
  88.3 0.0 collective-permute-done.15.refs_6_
  88.3 0.7 collective-permute-start.9
  89.0 0.7 collective-permute-start.6
  89.8 0.0 collective-permute-done.9.refs_6_
  89.8 1.3 collective-permute-start.13
  91.1 1.3 collective-permute-start.16
  92.5 0.0 collective-permute-done.23.refs_15_
  92.5 1.3 collective-permute-start.10
  93.8 0.0 collective-permute-done.24.refs_16_
  93.8 1.3 collective-permute-start.7
  95.1 18.0 %collective-permute-start.17 = (f32[64,128]{1,0:T(8,128)S(1)}, f32[64,128]{1,0:T(8,128)S(1)}, u32[]{:S(2)}, u32[]{:S(2)}) collective-permute-start(f32[64,128]{1,0:T(8,128)S(1)} %get-tuple-element.34.refs_0_), channel_id=1, source_target_pairs={{0,8},{4,12},{8,0},{12,4},{16,24},{20,28},{24,16},{28,20},{1,9},{5... | collective-permute-start | bytes 98312 | tf_op jit(solution)/shard_map/ppermute | solution.py:520
  113.1 16.1 %collective-permute-done.17.refs_1_ = f32[64,128]{1,0:T(8,128)S(1)} collective-permute-done((f32[64,128]{1,0:T(8,128)S(1)}, f32[64,128]{1,0:T(8,128)S(1)}, u32[]{:S(2)}, u32[]{:S(2)}) %collective-permute-start.17) | collective-permute-done | bytes 32800 | tf_op jit(solution)/shard_map/ppermute | solution.py:520
  129.2 0.0 collective-permute-start.18
  129.2 5.2 %collective-permute-done.18.refs_2_ = f32[64,128]{1,0:T(8,128)S(1)} collective-permute-done((f32[64,128]{1,0:T(8,128)S(1)}, f32[64,128]{1,0:T(8,128)S(1)}, u32[]{:S(2)}, u32[]{:S(2)}) %collective-permute-start.18) | collective-permute-done | bytes 32800 | tf_op jit(solution)/shard_map/ppermute | solution.py:520
  134.4 1.3 collective-permute-start.19
  135.7 4.5 %collective-permute-done.19.refs_3_ = f32[64,128]{1,0:T(8,128)S(1)} collective-permute-done((f32[64,128]{1,0:T(8,128)S(1)}, f32[64,128]{1,0:T(8,128)S(1)}, u32[]{:S(2)}, u32[]{:S(2)}) %collective-permute-start.19) | collective-permute-done | bytes 32800 | tf_op jit(solution)/shard_map/ppermute | solution.py:520
  140.1 2.1 %direct_pass.1 = (f32[64,1024]{1,0:T(8,128)S(1)}, f32[96,128]{1,0:T(8,128)S(1)}, f32[96,128]{1,0:T(8,128)S(1)}, f32[96,128]{1,0:T(8,128)S(1)}, f32[96,128]{1,0:T(8,128)S(1)}) custom-call(s32[1]{0:T(128)} %bitcast.1.chip_ref, f32[64,128]{1,0:T(8,128)S(1)} %get-tuple-element.34.refs_0_, f32[64,128]{1,0:T(8,128)S(1)} %collective-permute-done.17.refs_1_, ...), custom_call_target="tpu_custom_call" | custom-call | flops 1073741824 | bytes 2097152 | tf_op jit(solution)/shard_map/direct_pass/pallas_call | solution.py:489
  142.3 0.1 collective-permute-start.26
  142.3 0.0 collective-permute-done.16.refs_7_
  142.3 2.1 %collective-permute-start.27 = (f32[96,128]{1,0:T(8,128)S(1)}, f32[96,128]{1,0:T(8,128)S(1)}, u32[]{:S(2)}, u32[]{:S(2)}) collective-permute-start(f32[96,128]{1,0:T(8,128)S(1)} %get-tuple-element.40), channel_id=1, source_target_pairs={{0,16},{4,20},{8,24},{12,28},{16,0},{20,4},{24,8},{28,12},{1,17},{... | collective-permute-start | bytes 147464 | tf_op jit(solution)/shard_map/ppermute | solution.py:520
  144.4 0.0 collective-permute-done.13.refs_3_
  144.4 2.3 %collective-permute-start.28 = (f32[96,128]{1,0:T(8,128)S(1)}, f32[96,128]{1,0:T(8,128)S(1)}, u32[]{:S(2)}, u32[]{:S(2)}) collective-permute-start(f32[96,128]{1,0:T(8,128)S(1)} %get-tuple-element.41), channel_id=1, source_target_pairs={{0,24},{4,28},{8,16},{12,20},{16,8},{20,12},{24,0},{28,4},{1,25},{... | collective-permute-start | bytes 147464 | tf_op jit(solution)/shard_map/ppermute | solution.py:520
  146.7 0.7 shard_map.68
  147.5 0.0 collective-permute-done.27.refs_13_
  147.5 2.9 %collective-permute-done.28.refs_14_ = f32[96,128]{1,0:T(8,128)S(1)} collective-permute-done((f32[96,128]{1,0:T(8,128)S(1)}, f32[96,128]{1,0:T(8,128)S(1)}, u32[]{:S(2)}, u32[]{:S(2)}) %collective-permute-start.28) | collective-permute-done | bytes 49184 | tf_op jit(solution)/shard_map/ppermute | solution.py:520
  150.3 0.8 shard_map.69
  151.1 0.1 collective-permute-start.29
  151.2 1.2 collective-permute-done.29
  152.4 2.7 %collective-permute-start.30 = (f32[64,128]{1,0:T(8,128)S(1)}, f32[64,128]{1,0:T(8,128)S(1)}, u32[]{:S(2)}, u32[]{:S(2)}) collective-permute-start(f32[64,128]{1,0:T(8,128)S(1)} %fusion.refs_0_), channel_id=1, source_target_pairs={{0,1},{1,2},{2,3},{3,0},{4,5},{5,6},{6,7},{7,4},{8,9},{9,10},{10,1... | collective-permute-start | bytes 98312 | tf_op jit(solution)/shard_map/ppermute | solution.py:513
  155.1 1.7 %collective-permute-start.31 = (f32[64,128]{1,0:T(8,128)S(1)}, f32[64,128]{1,0:T(8,128)S(1)}, u32[]{:S(2)}, u32[]{:S(2)}) collective-permute-start(f32[64,128]{1,0:T(8,128)S(1)} %fusion.refs_0_), channel_id=1, source_target_pairs={{0,2},{1,3},{2,0},{3,1},{4,6},{5,7},{6,4},{7,5},{8,10},{9,11},{10,... | collective-permute-start | bytes 98312 | tf_op jit(solution)/shard_map/ppermute | solution.py:513
  156.8 0.6 collective-permute-start.32
  157.3 2.2 %mix_pass.1 = (f32[64,64]{1,0:T(8,128)S(1)}, f32[64,64]{1,0:T(8,128)S(1)}) custom-call(f32[64,1152]{1,0:T(8,128)S(1)} %get-tuple-element.31.refs_0_, f32[64,1152]{1,0:T(8,128)S(1)} %collective-permute-done.11.refs_1_, f32[64,1152]{1,0:T(8,128)S(1)} %collective-permute-done.12.refs_2_, f32[64,1152]{1,0:T(8,128)S(1)} %collective-permute-done.13.refs_3_, ...), custom_call_target="tpu_custom_call" | custom-call | flops 4194304 | bytes 65536 | tf_op jit(solution)/shard_map/mix_pass/pallas_call | solution.py:379
  159.6 1.2 ppm_pass.1
  160.8 3.0 %sample_pass.1 = f32[64,64]{1,0:T(8,128)} custom-call(f32[64,128]{1,0:T(8,128)S(1)} %fusion.refs_0_, f32[64,128]{1,0:T(8,128)S(1)} %collective-permute-done.30.refs_1_, f32[64,128]{1,0:T(8,128)S(1)} %collective-permute-done.31.refs_2_, f32[64,128]{1,0:T(8,128)S(1)} %collective-permute-done.32.refs_3_, f32[64,64]{1,0:T(8,128)S(1)} %get-tuple-element.43.refs_4_.mix_ref, ...), custom_call_target="tpu_custom_call" | custom-call | flops 4194304 | bytes 65536 | tf_op jit(solution)/shard_map/sample_pass/pallas_call | solution.py:404
  (29 shorter events, 0.3 us)
Async XLA Ops:
  0.6 4.3 %copy-start = (f32[64,16384]{1,0:T(8,128)S(1)}, f32[64,16384]{1,0:T(8,128)}, u32[]{:S(2)}) copy-start(f32[64,16384]{1,0:T(8,128)} %refs_7_.3) | copy-start | bytes 12582916
  0.7 4.3 %copy-start.1 = (f32[64,1024]{1,0:T(8,128)S(1)}, f32[64,1024]{1,0:T(8,128)}, u32[]{:S(2)}) copy-start(f32[64,1024]{1,0:T(8,128)} %mz_ref.1) | copy-start | bytes 786436
  4.4 31.2 %collective-permute-start.4 = (f32[8,64,1024]{2,1,0:T(8,128)S(1)}, f32[8,64,1024]{2,1,0:T(8,128)S(1)}, u32[]{:S(2)}, u32[]{:S(2)}) collective-permute-start(f32[8,64,1024]{2,1,0:T(8,128)S(1)} %get-tuple-element.27.send_ref), channel_id=1, source_target_pairs={{0,4},{4,0},{8,12},{12,8},{16,20},{20,16},{24,28},{28,24},{1,5},{5... | collective-permute-start | bytes 6291464 | tf_op jit(solution)/shard_map/ppermute | solution.py:562
  5.0 4.8 %copy-start.2 = (f32[64,256]{1,0:T(8,128)S(1)}, f32[64,256]{1,0:T(8,128)}, u32[]{:S(2)}) copy-start(f32[64,256]{1,0:T(8,128)} %refs_5_.5) | copy-start | bytes 196612
  24.5 7.1 %collective-permute-start = (f32[128,128]{1,0:T(8,128)S(1)}, f32[128,128]{1,0:T(8,128)S(1)}, u32[]{:S(2)}, u32[]{:S(2)}) collective-permute-start(f32[128,128]{1,0:T(8,128)S(1)} %lcms_pass.1), channel_id=1, source_target_pairs={{0,1},{1,2},{2,3},{3,0},{4,5},{5,6},{6,7},{7,4},{8,9},{9,10},{10,1... | collective-permute-start | bytes 196616 | tf_op jit(solution)/shard_map/ppermute | solution.py:513
  27.1 5.0 %collective-permute-start.1 = (f32[128,128]{1,0:T(8,128)S(1)}, f32[128,128]{1,0:T(8,128)S(1)}, u32[]{:S(2)}, u32[]{:S(2)}) collective-permute-start(f32[128,128]{1,0:T(8,128)S(1)} %lcms_pass.1), channel_id=1, source_target_pairs={{0,2},{1,3},{2,0},{3,1},{4,6},{5,7},{6,4},{7,5},{8,10},{9,11},{10,... | collective-permute-start | bytes 196616 | tf_op jit(solution)/shard_map/ppermute | solution.py:513
  28.6 4.3 %collective-permute-start.2 = (f32[128,128]{1,0:T(8,128)S(1)}, f32[128,128]{1,0:T(8,128)S(1)}, u32[]{:S(2)}, u32[]{:S(2)}) collective-permute-start(f32[128,128]{1,0:T(8,128)S(1)} %lcms_pass.1), channel_id=1, source_target_pairs={{0,3},{1,0},{2,1},{3,2},{4,7},{5,4},{6,5},{7,6},{8,11},{9,8},{10,9... | collective-permute-start | bytes 196616 | tf_op jit(solution)/shard_map/ppermute | solution.py:513
  30.0 22.0 %collective-permute-start.20 = (f32[4,2,64,256]{3,2,1,0:T(8,128)S(1)}, f32[4,2,64,256]{3,2,1,0:T(8,128)S(1)}, u32[]{:S(2)}, u32[]{:S(2)}) collective-permute-start(f32[4,2,64,256]{3,2,1,0:T(8,128)S(1)} %get-tuple-element.35), channel_id=1, source_target_pairs={{0,8},{4,12},{8,0},{12,4},{16,24},{20,28},{24,16},{28,20},{1,9},{5... | collective-permute-start | bytes 1572872 | tf_op jit(solution)/shard_map/ppermute | solution.py:520
  32.9 2.7 %collective-permute-start.3 = (f32[128,128]{1,0:T(8,128)S(1)}, f32[128,128]{1,0:T(8,128)S(1)}, u32[]{:S(2)}, u32[]{:S(2)}) collective-permute-start(f32[128,128]{1,0:T(8,128)S(1)} %add_add_fusion.own_pack.refs_4_.refs_6_), channel_id=1, source_target_pairs={{0,4},{4,0},{8,12},{12,8},{16,20},{20,16},{24,28},{28,24},{1,5},{5... | collective-permute-start | bytes 196616 | tf_op jit(solution)/shard_map/ppermute | solution.py:566
  33.0 46.2 %collective-permute-start.21 = (f32[4,2,64,256]{3,2,1,0:T(8,128)S(1)}, f32[4,2,64,256]{3,2,1,0:T(8,128)S(1)}, u32[]{:S(2)}, u32[]{:S(2)}) collective-permute-start(f32[4,2,64,256]{3,2,1,0:T(8,128)S(1)} %get-tuple-element.36), channel_id=1, source_target_pairs={{0,16},{4,20},{8,24},{12,28},{16,0},{20,4},{24,8},{28,12},{1,17},{... | collective-permute-start | bytes 1572872 | tf_op jit(solution)/shard_map/ppermute | solution.py:520
  36.1 25.5 %collective-permute-start.11 = (f32[64,1152]{1,0:T(8,128)S(1)}, f32[64,1152]{1,0:T(8,128)S(1)}, u32[]{:S(2)}, u32[]{:S(2)}) collective-permute-start(f32[64,1152]{1,0:T(8,128)S(1)} %get-tuple-element.31.refs_0_), channel_id=1, source_target_pairs={{0,8},{4,12},{24,16},{28,20},{1,9},{5,13},{25,17},{29,21},{2,10},{... | collective-permute-start | bytes 884744 | tf_op jit(solution)/shard_map/ppermute | solution.py:532
  39.6 40.3 %collective-permute-start.22 = (f32[4,2,64,256]{3,2,1,0:T(8,128)S(1)}, f32[4,2,64,256]{3,2,1,0:T(8,128)S(1)}, u32[]{:S(2)}, u32[]{:S(2)}) collective-permute-start(f32[4,2,64,256]{3,2,1,0:T(8,128)S(1)} %get-tuple-element.37), channel_id=1, source_target_pairs={{0,24},{4,28},{8,16},{12,20},{16,8},{20,12},{24,0},{28,4},{1,25},{... | collective-permute-start | bytes 1572872 | tf_op jit(solution)/shard_map/ppermute | solution.py:520
  41.5 36.9 %collective-permute-start.14 = (f32[64,1024]{1,0:T(8,128)S(1)}, f32[64,1024]{1,0:T(8,128)S(1)}, u32[]{:S(2)}, u32[]{:S(2)}) collective-permute-start(f32[64,1024]{1,0:T(8,128)S(1)} %get-tuple-element.32.refs_4_), channel_id=1, source_target_pairs={{0,8},{4,12},{24,16},{28,20},{1,9},{5,13},{25,17},{29,21},{2,10},{... | collective-permute-start | bytes 786440 | tf_op jit(solution)/shard_map/ppermute | solution.py:532
  52.0 32.0 %collective-permute-start.8 = (f32[64,1024]{1,0:T(8,128)S(1)}, f32[64,1024]{1,0:T(8,128)S(1)}, u32[]{:S(2)}, u32[]{:S(2)}) collective-permute-start(f32[64,1024]{1,0:T(8,128)S(1)} %get-tuple-element.30.refs_4_), channel_id=1, source_target_pairs={{0,8},{4,12},{24,16},{28,20},{1,9},{5,13},{25,17},{29,21},{2,10},{... | collective-permute-start | bytes 786440 | tf_op jit(solution)/shard_map/ppermute | solution.py:532
  61.5 26.7 %collective-permute-start.5 = (f32[64,1024]{1,0:T(8,128)S(1)}, f32[64,1024]{1,0:T(8,128)S(1)}, u32[]{:S(2)}, u32[]{:S(2)}) collective-permute-start(f32[64,1024]{1,0:T(8,128)S(1)} %get-tuple-element.29.refs_0_), channel_id=1, source_target_pairs={{0,8},{4,12},{24,16},{28,20},{1,9},{5,13},{25,17},{29,21},{2,10},{... | collective-permute-start | bytes 786440 | tf_op jit(solution)/shard_map/ppermute | solution.py:532
  78.4 10.6 %collective-permute-start.12 = (f32[64,1152]{1,0:T(8,128)S(1)}, f32[64,1152]{1,0:T(8,128)S(1)}, u32[]{:S(2)}, u32[]{:S(2)}) collective-permute-start(f32[64,1152]{1,0:T(8,128)S(1)} %add.51), channel_id=1, source_target_pairs={{8,16},{12,20},{16,8},{20,12},{9,17},{13,21},{17,9},{21,13},{10,18... | collective-permute-start | bytes 884744 | tf_op jit(solution)/shard_map/ppermute | solution.py:532
  79.1 9.2 %collective-permute-start.15 = (f32[64,1024]{1,0:T(8,128)S(1)}, f32[64,1024]{1,0:T(8,128)S(1)}, u32[]{:S(2)}, u32[]{:S(2)}) collective-permute-start(f32[64,1024]{1,0:T(8,128)S(1)} %add.53), channel_id=1, source_target_pairs={{8,16},{12,20},{16,8},{20,12},{9,17},{13,21},{17,9},{21,13},{10,18... | collective-permute-start | bytes 786440 | tf_op jit(solution)/shard_map/ppermute | solution.py:532
  79.8 12.7 %collective-permute-start.23 = (f32[4,2,64,256]{3,2,1,0:T(8,128)S(1)}, f32[4,2,64,256]{3,2,1,0:T(8,128)S(1)}, u32[]{:S(2)}, u32[]{:S(2)}) collective-permute-start(f32[4,2,64,256]{3,2,1,0:T(8,128)S(1)} %collective-permute-done.20.refs_12_), channel_id=1, source_target_pairs={{0,4},{4,0},{8,12},{12,8},{16,20},{20,16},{24,28},{28,24},{1,5},{5... | collective-permute-start | bytes 1572872 | tf_op jit(solution)/shard_map/ppermute | solution.py:571
  84.0 9.8 %collective-permute-start.24 = (f32[4,2,64,256]{3,2,1,0:T(8,128)S(1)}, f32[4,2,64,256]{3,2,1,0:T(8,128)S(1)}, u32[]{:S(2)}, u32[]{:S(2)}) collective-permute-start(f32[4,2,64,256]{3,2,1,0:T(8,128)S(1)} %collective-permute-done.21.refs_13_), channel_id=1, source_target_pairs={{0,4},{4,0},{8,12},{12,8},{16,20},{20,16},{24,28},{28,24},{1,5},{5... | collective-permute-start | bytes 1572872 | tf_op jit(solution)/shard_map/ppermute | solution.py:571
  88.3 6.9 %collective-permute-start.25 = (f32[4,2,64,256]{3,2,1,0:T(8,128)S(1)}, f32[4,2,64,256]{3,2,1,0:T(8,128)S(1)}, u32[]{:S(2)}, u32[]{:S(2)}) collective-permute-start(f32[4,2,64,256]{3,2,1,0:T(8,128)S(1)} %collective-permute-done.22.refs_14_), channel_id=1, source_target_pairs={{0,4},{4,0},{8,12},{12,8},{16,20},{20,16},{24,28},{28,24},{1,5},{5... | collective-permute-start | bytes 1572872 | tf_op jit(solution)/shard_map/ppermute | solution.py:571
  88.3 1.5 collective-permute-start.9
  89.0 2.1 %collective-permute-start.6 = (f32[64,1024]{1,0:T(8,128)S(1)}, f32[64,1024]{1,0:T(8,128)S(1)}, u32[]{:S(2)}, u32[]{:S(2)}) collective-permute-start(f32[64,1024]{1,0:T(8,128)S(1)} %add.47), channel_id=1, source_target_pairs={{8,16},{12,20},{16,8},{20,12},{9,17},{13,21},{17,9},{21,13},{10,18... | collective-permute-start | bytes 786440 | tf_op jit(solution)/shard_map/ppermute | solution.py:532
  89.8 54.7 %collective-permute-start.13 = (f32[64,1152]{1,0:T(8,128)S(1)}, f32[64,1152]{1,0:T(8,128)S(1)}, u32[]{:S(2)}, u32[]{:S(2)}) collective-permute-start(f32[64,1152]{1,0:T(8,128)S(1)} %add.52), channel_id=1, source_target_pairs={{8,0},{12,4},{16,24},{20,28},{9,1},{13,5},{17,25},{21,29},{10,2},{... | collective-permute-start | bytes 884744 | tf_op jit(solution)/shard_map/ppermute | solution.py:532
  91.1 51.2 %collective-permute-start.16 = (f32[64,1024]{1,0:T(8,128)S(1)}, f32[64,1024]{1,0:T(8,128)S(1)}, u32[]{:S(2)}, u32[]{:S(2)}) collective-permute-start(f32[64,1024]{1,0:T(8,128)S(1)} %add.54), channel_id=1, source_target_pairs={{8,0},{12,4},{16,24},{20,28},{9,1},{13,5},{17,25},{21,29},{10,2},{... | collective-permute-start | bytes 786440 | tf_op jit(solution)/shard_map/ppermute | solution.py:532
  92.5 57.8 %collective-permute-start.10 = (f32[64,1024]{1,0:T(8,128)S(1)}, f32[64,1024]{1,0:T(8,128)S(1)}, u32[]{:S(2)}, u32[]{:S(2)}) collective-permute-start(f32[64,1024]{1,0:T(8,128)S(1)} %add.50), channel_id=1, source_target_pairs={{8,0},{12,4},{16,24},{20,28},{9,1},{13,5},{17,25},{21,29},{10,2},{... | collective-permute-start | bytes 786440 | tf_op jit(solution)/shard_map/ppermute | solution.py:532
  93.8 56.5 %collective-permute-start.7 = (f32[64,1024]{1,0:T(8,128)S(1)}, f32[64,1024]{1,0:T(8,128)S(1)}, u32[]{:S(2)}, u32[]{:S(2)}) collective-permute-start(f32[64,1024]{1,0:T(8,128)S(1)} %add.48), channel_id=1, source_target_pairs={{8,0},{12,4},{16,24},{20,28},{9,1},{13,5},{17,25},{21,29},{10,2},{... | collective-permute-start | bytes 786440 | tf_op jit(solution)/shard_map/ppermute | solution.py:532
  95.1 34.1 %collective-permute-start.17 = (f32[64,128]{1,0:T(8,128)S(1)}, f32[64,128]{1,0:T(8,128)S(1)}, u32[]{:S(2)}, u32[]{:S(2)}) collective-permute-start(f32[64,128]{1,0:T(8,128)S(1)} %get-tuple-element.34.refs_0_), channel_id=1, source_target_pairs={{0,8},{4,12},{8,0},{12,4},{16,24},{20,28},{24,16},{28,20},{1,9},{5... | collective-permute-start | bytes 98312 | tf_op jit(solution)/shard_map/ppermute | solution.py:520
  129.2 5.2 %collective-permute-start.18 = (f32[64,128]{1,0:T(8,128)S(1)}, f32[64,128]{1,0:T(8,128)S(1)}, u32[]{:S(2)}, u32[]{:S(2)}) collective-permute-start(f32[64,128]{1,0:T(8,128)S(1)} %get-tuple-element.34.refs_0_), channel_id=1, source_target_pairs={{0,16},{4,20},{8,24},{12,28},{16,0},{20,4},{24,8},{28,12},{1,17},{... | collective-permute-start | bytes 98312 | tf_op jit(solution)/shard_map/ppermute | solution.py:520
  134.4 5.7 %collective-permute-start.19 = (f32[64,128]{1,0:T(8,128)S(1)}, f32[64,128]{1,0:T(8,128)S(1)}, u32[]{:S(2)}, u32[]{:S(2)}) collective-permute-start(f32[64,128]{1,0:T(8,128)S(1)} %get-tuple-element.34.refs_0_), channel_id=1, source_target_pairs={{0,24},{4,28},{8,16},{12,20},{16,8},{20,12},{24,0},{28,4},{1,25},{... | collective-permute-start | bytes 98312 | tf_op jit(solution)/shard_map/ppermute | solution.py:520
  142.3 5.2 %collective-permute-start.26 = (f32[96,128]{1,0:T(8,128)S(1)}, f32[96,128]{1,0:T(8,128)S(1)}, u32[]{:S(2)}, u32[]{:S(2)}) collective-permute-start(f32[96,128]{1,0:T(8,128)S(1)} %get-tuple-element.39), channel_id=1, source_target_pairs={{0,8},{4,12},{8,0},{12,4},{16,24},{20,28},{24,16},{28,20},{1,9},{5... | collective-permute-start | bytes 147464 | tf_op jit(solution)/shard_map/ppermute | solution.py:520
  142.3 5.1 %collective-permute-start.27 = (f32[96,128]{1,0:T(8,128)S(1)}, f32[96,128]{1,0:T(8,128)S(1)}, u32[]{:S(2)}, u32[]{:S(2)}) collective-permute-start(f32[96,128]{1,0:T(8,128)S(1)} %get-tuple-element.40), channel_id=1, source_target_pairs={{0,16},{4,20},{8,24},{12,28},{16,0},{20,4},{24,8},{28,12},{1,17},{... | collective-permute-start | bytes 147464 | tf_op jit(solution)/shard_map/ppermute | solution.py:520
  144.4 5.9 %collective-permute-start.28 = (f32[96,128]{1,0:T(8,128)S(1)}, f32[96,128]{1,0:T(8,128)S(1)}, u32[]{:S(2)}, u32[]{:S(2)}) collective-permute-start(f32[96,128]{1,0:T(8,128)S(1)} %get-tuple-element.41), channel_id=1, source_target_pairs={{0,24},{4,28},{8,16},{12,20},{16,8},{20,12},{24,0},{28,4},{1,25},{... | collective-permute-start | bytes 147464 | tf_op jit(solution)/shard_map/ppermute | solution.py:520
  151.1 1.3 collective-permute-start.29
  152.4 8.3 %collective-permute-start.30 = (f32[64,128]{1,0:T(8,128)S(1)}, f32[64,128]{1,0:T(8,128)S(1)}, u32[]{:S(2)}, u32[]{:S(2)}) collective-permute-start(f32[64,128]{1,0:T(8,128)S(1)} %fusion.refs_0_), channel_id=1, source_target_pairs={{0,1},{1,2},{2,3},{3,0},{4,5},{5,6},{6,7},{7,4},{8,9},{9,10},{10,1... | collective-permute-start | bytes 98312 | tf_op jit(solution)/shard_map/ppermute | solution.py:513
  155.1 5.7 %collective-permute-start.31 = (f32[64,128]{1,0:T(8,128)S(1)}, f32[64,128]{1,0:T(8,128)S(1)}, u32[]{:S(2)}, u32[]{:S(2)}) collective-permute-start(f32[64,128]{1,0:T(8,128)S(1)} %fusion.refs_0_), channel_id=1, source_target_pairs={{0,2},{1,3},{2,0},{3,1},{4,6},{5,7},{6,4},{7,5},{8,10},{9,11},{10,... | collective-permute-start | bytes 98312 | tf_op jit(solution)/shard_map/ppermute | solution.py:513
  156.8 4.0 %collective-permute-start.32 = (f32[64,128]{1,0:T(8,128)S(1)}, f32[64,128]{1,0:T(8,128)S(1)}, u32[]{:S(2)}, u32[]{:S(2)}) collective-permute-start(f32[64,128]{1,0:T(8,128)S(1)} %fusion.refs_0_), channel_id=1, source_target_pairs={{0,3},{1,0},{2,1},{3,2},{4,7},{5,4},{6,5},{7,6},{8,11},{9,8},{10,9... | collective-permute-start | bytes 98312 | tf_op jit(solution)/shard_map/ppermute | solution.py:513
